TPU v7x, 128 devices: a whole 4x4x4 slice. The times are simulated.
128 devices in a mesh: dp: 8 (over z, core), mp: 16 (over x, y).
Axes of the slice: x: 4, y: 4, z: 4, core: 2. Of those that a mesh axis runs over, the one named last changes fastest.
Arguments:
- node_feats: bfloat16 [262144, 128], P(('dp', 'mp')), may hold values from -6 to 6
- batch_deg: int32 [262144], P(('dp', 'mp')), may hold values from 1 to 8
- batch_nbrs: int32 [262144, 8], P(('dp', 'mp')), may hold values from 0 to 2047
- halo_nbrs: int32 [262144, 8], P(('dp', 'mp')), may hold values from 0 to 511
- halo_len: int32 [262144], P(('dp', 'mp')), may hold values from 1 to 8
- halo_rows: int32 [65536], P(('dp', 'mp')), may hold values from 0 to 262143, as said below
- halo_deg: int32 [65536], P(('dp', 'mp')), may hold values from 1 to 8
- feat_table: bfloat16 [262144, 128], P(('dp', 'mp')), may hold values from -6 to 6
- emb_table: bfloat16 [262144, 512], P(('dp', 'mp')), may hold values from -4 to 4
- grad_table: bfloat16 [262144, 512], P(('dp', 'mp')), may hold values from -6 to 6
- weight_one: bfloat16 [128, 512], replicated, may hold values from -0.5 to 0.5
- weight_two: bfloat16 [512, 512], replicated, may hold values from -0.25 to 0.25
- grad_out: bfloat16 [262144, 512], P(('dp', 'mp')), may hold values from -6 to 6
Outputs:
- out_embed: bfloat16 [262144, 512], P(('dp', 'mp'))
- halo_grad: bfloat16 [262144, 512], P(('dp', 'mp'))
- grad_one: float32 [128, 512], replicated
- grad_two: float32 [512, 512], replicated
Inputs may be any that keep to these rules, and one draw needn't show every extreme that they name: `halo_rows`: slot s of each device's 512 halo slots names a row of the block of 2048 rows held by device s // 4 of dp+mp (device index dp * 16 + mp), so that every device asks every owner for exactly 4 rows; rows may repeat.
All inputs are finite; a program needn't handle non-finite values.
Results may differ from a plain program's by a relative error of at most 0.006.
Values may be sent and summed in bfloat16 or wider, within the bound.
No kernel may reach another device: no remote copies, remote signals or barrier semaphores. Data moves between devices by JAX's collectives and lax.ppermute only.
A program may use at most 128 MiB of HBM per device.

v0:
```python
import jax
import jax.numpy as jnp
from jax import lax
from jax.experimental import pallas as pl
from jax.experimental.pallas import tpu as pltpu
from jax.sharding import PartitionSpec as P

BF = jnp.bfloat16
F32 = jnp.float32
AXES = ("dp", "mp")
NB = 2048
NH = 512
HID = 512
FEAT = 128
STEP = 512
VMEM_LIMIT = 56 * 1024 * 1024


def dot(left, right):
    return jnp.dot(left, right, preferred_element_type=F32)


def dot_t(left, right):
    return lax.dot_general(left, right, (((1,), (1,)), ((), ())), preferred_element_type=F32)


def dot_tl(left, right):
    return lax.dot_general(left, right, (((0,), (0,)), ((), ())), preferred_element_type=F32)


def columns(row):
    n = row.shape[1]
    return jnp.concatenate(
        [jnp.broadcast_to(row[:, s : s + 128], (128, 128)).T for s in range(0, n, 128)], axis=0
    )


def scale_rows(x, col):
    reps = x.shape[1] // 128
    return x * (jnp.tile(col, (1, reps)) if reps > 1 else col)


def add_counts(dst_ref, row0, nbrs, width):
    rows = 16
    lane = lax.broadcasted_iota(jnp.int32, (rows, 128), 1)
    one = jnp.ones((rows, 128), BF)
    zero = jnp.zeros((rows, 128), BF)
    for r in range(0, nbrs.shape[0], rows):
        idx = [
            jnp.broadcast_to(nbrs[r : r + rows, k : k + 1], (rows, 128)).astype(jnp.int16)
            for k in range(8)
        ]
        for c in range(0, width, 128):
            here = (lane + c).astype(jnp.int16)
            acc = jnp.where(idx[0] == here, one, zero)
            for k in range(1, 8):
                acc = acc + jnp.where(idx[k] == here, one, zero)
            dst_ref[pl.ds(row0 + r, rows), c : c + 128] = acc


def halo_kernel(hn_ref, hl_ref, bdeg_ref, hdeg_ref, g_ref, h_ref, gt_ref, p_ref, lenb_ref):
    inv = lax.rsqrt(bdeg_ref[...].astype(F32))
    inv_h = lax.rsqrt(hdeg_ref[...].astype(F32))
    lenb_ref[...] = columns(hl_ref[...].astype(F32))

    def build(i, _):
        r = pl.multiple_of(i * 128, 128)
        nbrs = hn_ref[pl.ds(r, 128), :]
        slot = lax.broadcasted_iota(jnp.int32, nbrs.shape, 1).astype(F32)
        nbrs = jnp.where(slot < lenb_ref[pl.ds(r, 128), 0:8], nbrs, -1)
        add_counts(h_ref, r, nbrs, NH)
        return 0

    lax.fori_loop(0, NB // 128, build, 0)
    for s in range(0, NB, 512):
        gt = g_ref[s : s + 512, :].astype(F32).T * inv[:, s : s + 512]
        gt_ref[:, s : s + 512] = gt.astype(BF)
    pt = dot(gt_ref[...], h_ref[...]) * inv_h
    p_ref[...] = pt.T.astype(BF)


def halo_call(hn, hl, bdeg, hdeg, g):
    return pl.pallas_call(
        halo_kernel,
        out_shape=(
            jax.ShapeDtypeStruct((NB, NH), BF),
            jax.ShapeDtypeStruct((HID, NB), BF),
            jax.ShapeDtypeStruct((NH, HID), BF),
        ),
        scratch_shapes=[pltpu.VMEM((NB, 128), F32)],
        compiler_params=pltpu.CompilerParams(vmem_limit_bytes=VMEM_LIMIT),
        name="halo_part",
    )(hn, hl, bdeg, hdeg, g)


def pair_up(top, bottom):
    w = top.shape[1]
    t = top.reshape(64, 8, w)
    b = bottom.reshape(64, 8, w)
    low = lax.broadcasted_iota(jnp.int32, (64, 8, w), 1) < 4
    even = jnp.where(low, t, pltpu.roll(b, 4, 1))
    odd = jnp.where(low, pltpu.roll(t, 4, 1), b)
    return jnp.concatenate([even, odd], axis=1).astype(BF).reshape(1024, w)


def part_up(both):
    w = both.shape[1]
    x = both.reshape(64, 16, w).astype(F32)
    even, odd = x[:, 0:8], x[:, 8:16]
    low = lax.broadcasted_iota(jnp.int32, (64, 8, w), 1) < 4
    top = jnp.where(low, even, pltpu.roll(odd, 4, 1))
    bottom = jnp.where(low, pltpu.roll(even, 4, 1), odd)
    return top.reshape(512, w), bottom.reshape(512, w)


def pick_kernel(ask_ref, x_ref, e_ref, v_ref, p_ref, out_ref, s_ref):
    a = ask_ref[...]
    lane = lax.broadcasted_iota(jnp.int32, (64, 8, 8), 2)
    sub = lax.broadcasted_iota(jnp.int32, (64, 8, 8), 1)
    mine = jnp.where(lane == sub, jnp.broadcast_to(a[:, None, :], (64, 8, 8)), 0)
    col = jnp.sum(mine.astype(F32), axis=2, keepdims=True).reshape(512, 1).astype(jnp.int32)
    colb = jnp.broadcast_to(col, (512, 128))
    lanes = lax.broadcasted_iota(jnp.int32, (512, 128), 1)
    for c in range(0, 2048, 128):
        s_ref[:, c : c + 128] = jnp.where(colb == lanes + c, 1.0, 0.0).astype(BF)
    s = s_ref[...]
    out_ref[:, 0:512] = pair_up(dot(s, e_ref[...]), dot(s, v_ref[...]))
    p = p_ref[...].astype(F32)
    out_ref[:, 512:640] = pair_up(dot(s, x_ref[...]), p[:, 0:128])
    out_ref[:, 640:768] = pair_up(p[:, 128:256], p[:, 256:384])
    out_ref[:, 768:896] = pair_up(p[:, 384:512], p[:, 384:512])


def pick_call(asked, x, e, v, p):
    return pl.pallas_call(
        pick_kernel,
        out_shape=(
            jax.ShapeDtypeStruct((1024, 896), BF),
            jax.ShapeDtypeStruct((NH, NB), BF),
        ),
        compiler_params=pltpu.CompilerParams(vmem_limit_bytes=VMEM_LIMIT),
        name="pick_rows",
    )(asked, x, e, v, p)


def batch_kernel(nb_ref, bdeg_ref, f_ref, gt_ref, c_ref, cf_ref, st_ref, fs_ref):
    i = pl.program_id(0)

    @pl.when(i == 0)
    def _():
        col = columns(lax.rsqrt(bdeg_ref[...].astype(F32)))
        fs_ref[...] = (f_ref[...].astype(F32) * col).astype(BF)

    def build(t, _):
        r = pl.multiple_of(t * 64, 64)
        add_counts(c_ref, r, nb_ref[pl.ds(r, 64), :], NB)
        return 0

    lax.fori_loop(0, STEP // 64, build, 0)
    diag0 = pl.multiple_of(i * STEP, STEP)
    eye = (
        lax.broadcasted_iota(jnp.int32, (STEP, STEP), 0)
        == lax.broadcasted_iota(jnp.int32, (STEP, STEP), 1)
    ).astype(F32).astype(BF)
    c_ref[:, pl.ds(diag0, STEP)] = c_ref[:, pl.ds(diag0, STEP)] + eye
    c = c_ref[...]
    cf_ref[...] = dot(c, fs_ref[...])
    part = dot(gt_ref[...], c)

    @pl.when(i == 0)
    def _():
        st_ref[...] = part

    @pl.when(i > 0)
    def _():
        st_ref[...] = st_ref[...] + part


def batch_call(nb, bdeg, f, gt):
    return pl.pallas_call(
        batch_kernel,
        grid=(NB // STEP,),
        in_specs=[
            pl.BlockSpec((STEP, 8), lambda i: (i, 0)),
            pl.BlockSpec((1, NB), lambda i: (0, 0)),
            pl.BlockSpec((NB, FEAT), lambda i: (0, 0)),
            pl.BlockSpec((HID, STEP), lambda i: (0, i)),
        ],
        out_specs=[
            pl.BlockSpec((STEP, NB), lambda i: (i, 0)),
            pl.BlockSpec((STEP, FEAT), lambda i: (i, 0)),
            pl.BlockSpec((HID, NB), lambda i: (0, 0)),
        ],
        out_shape=(
            jax.ShapeDtypeStruct((NB, NB), BF),
            jax.ShapeDtypeStruct((NB, FEAT), F32),
            jax.ShapeDtypeStruct((HID, NB), F32),
        ),
        scratch_shapes=[pltpu.VMEM((NB, FEAT), BF)],
        compiler_params=pltpu.CompilerParams(vmem_limit_bytes=VMEM_LIMIT),
        name="batch_part",
    )(nb, bdeg, f, gt)


def main_kernel(
    r_ref, c_ref, h_ref, cf_ref, st_ref, gt_ref, w1_ref, w2_ref, bdeg_ref, hdeg_ref,
    u_ref, pa_ref, grads_ref,
    hid_ref, u1_ref, he_ref, hvt_ref, g1_ref, g2_ref, inv_ref,
):
    i = pl.program_id(0)
    inv = lax.rsqrt(bdeg_ref[...].astype(F32))

    @pl.when(i == 0)
    def _():
        col_h = columns(lax.rsqrt(hdeg_ref[...].astype(F32)))
        he, hv = part_up(r_ref[:, 0:512])
        he_ref[...] = scale_rows(he, col_h).astype(BF)
        hvt_ref[...] = scale_rows(hv, col_h).T.astype(BF)
        hx, p0 = part_up(r_ref[:, 512:640])
        hx = (hx * col_h).astype(BF)
        p1, p2 = part_up(r_ref[:, 640:768])
        p3, _ = part_up(r_ref[:, 768:896])
        pa_ref[:, 0:128] = p0.astype(BF)
        pa_ref[:, 128:256] = p1.astype(BF)
        pa_ref[:, 256:384] = p2.astype(BF)
        pa_ref[:, 384:512] = p3.astype(BF)
        inv_ref[...] = columns(inv)
        for s in range(0, NB, 512):
            col = inv_ref[s : s + 512, :]
            u1 = (cf_ref[s : s + 512, :] + dot(h_ref[s : s + 512, :], hx)).astype(BF)
            u1_ref[s : s + 512, :] = u1
            pre = scale_rows(dot(u1, w1_ref[...]), col)
            hid_ref[s : s + 512, :] = scale_rows(jax.nn.silu(pre), col).astype(BF)

    r = pl.multiple_of(i * STEP, STEP)
    h = h_ref[pl.ds(r, STEP), :]
    u = (dot(c_ref[...], hid_ref[...]) + dot(h, he_ref[...])).astype(BF)
    u_ref[...] = u
    g2 = dot(gt_ref[...], u)
    row = lax.rsqrt(bdeg_ref[:, pl.ds(r, STEP)].astype(F32))
    spread = ((st_ref[...] + dot_t(hvt_ref[...], h)) * row).astype(BF)
    back = dot(w2_ref[...], spread)
    u1 = u1_ref[pl.ds(r, STEP), :]
    w1t = w1_ref[...].astype(F32).T.astype(BF)
    pre = dot_t(w1t, u1) * row
    sig = jax.nn.sigmoid(pre)
    d_pre = (back * (sig * (1.0 + pre * (1.0 - sig))) * row).astype(BF)
    g1 = dot(d_pre, u1)

    @pl.when(i == 0)
    def _():
        g1_ref[...] = g1
        g2_ref[...] = g2

    @pl.when(i > 0)
    def _():
        g1_ref[...] += g1
        g2_ref[...] += g2

    @pl.when(i == pl.num_programs(0) - 1)
    def _():
        t1 = g1_ref[...].T.astype(BF)
        t2 = g2_ref[...].T.astype(BF)
        grads_ref[0:512, 0:256] = t2[:, 0:256]
        grads_ref[512:1024, 0:256] = t2[:, 256:512]
        for q in range(4):
            grads_ref[128 * q : 128 * q + 128, 256:384] = t1[:, 128 * q : 128 * q + 128]
        grads_ref[512:1024, 256:384] = jnp.zeros((512, 128), BF)


def main_call(recv, c, h, cf, st, gt, w1, w2, bdeg, hdeg):
    whole = lambda *shape: pl.BlockSpec(shape, lambda i: (0, 0))
    return pl.pallas_call(
        main_kernel,
        grid=(NB // STEP,),
        in_specs=[
            whole(1024, 896),
            pl.BlockSpec((STEP, NB), lambda i: (i, 0)),
            whole(NB, NH),
            whole(NB, FEAT),
            pl.BlockSpec((HID, STEP), lambda i: (0, i)),
            pl.BlockSpec((HID, STEP), lambda i: (0, i)),
            whole(FEAT, HID),
            whole(HID, HID),
            whole(1, NB),
            whole(1, NH),
        ],
        out_specs=[
            pl.BlockSpec((STEP, HID), lambda i: (i, 0)),
            whole(NH, HID),
            whole(1024, 384),
        ],
        out_shape=(
            jax.ShapeDtypeStruct((NB, HID), BF),
            jax.ShapeDtypeStruct((NH, HID), BF),
            jax.ShapeDtypeStruct((1024, 384), BF),
        ),
        scratch_shapes=[
            pltpu.VMEM((NB, HID), BF),
            pltpu.VMEM((NB, FEAT), BF),
            pltpu.VMEM((NH, HID), BF),
            pltpu.VMEM((HID, NH), BF),
            pltpu.VMEM((HID, FEAT), F32),
            pltpu.VMEM((HID, HID), F32),
            pltpu.VMEM((NB, 128), F32),
        ],
        compiler_params=pltpu.CompilerParams(vmem_limit_bytes=VMEM_LIMIT),
        name="main_part",
    )(recv, c, h, cf, st, gt, w1, w2, bdeg, hdeg)


def tail_kernel(u_ref, w2_ref, bdeg_ref, s_ref, pa_ref, out_ref, hg_ref):
    i = pl.program_id(0)
    r = pl.multiple_of(i * STEP, STEP)
    col = columns(lax.rsqrt(bdeg_ref[:, pl.ds(r, STEP)].astype(F32)))
    out_ref[...] = scale_rows(dot(u_ref[...], w2_ref[...]), col).astype(BF)
    hg_ref[...] = dot_tl(s_ref[...], pa_ref[...]).astype(BF)


def tail_call(u, w2, bdeg, s, pa):
    whole = lambda *shape: pl.BlockSpec(shape, lambda i: (0, 0))
    return pl.pallas_call(
        tail_kernel,
        grid=(NB // STEP,),
        in_specs=[
            pl.BlockSpec((STEP, HID), lambda i: (i, 0)),
            whole(HID, HID),
            whole(1, NB),
            pl.BlockSpec((NH, STEP), lambda i: (0, i)),
            whole(NH, HID),
        ],
        out_specs=[
            pl.BlockSpec((STEP, HID), lambda i: (i, 0)),
            pl.BlockSpec((STEP, HID), lambda i: (i, 0)),
        ],
        out_shape=(
            jax.ShapeDtypeStruct((NB, HID), BF),
            jax.ShapeDtypeStruct((NB, HID), BF),
        ),
        compiler_params=pltpu.CompilerParams(vmem_limit_bytes=VMEM_LIMIT),
        name="tail_part",
    )(u, w2, bdeg, s, pa)


def sum_kernel(x_ref, o_ref):
    total = jnp.sum(x_ref[...].astype(F32), axis=0)
    o_ref[...] = jnp.broadcast_to(total.astype(BF)[None], (128, 8, 384))


def sum_call(x):
    return pl.pallas_call(
        sum_kernel,
        out_shape=jax.ShapeDtypeStruct((128, 8, 384), BF),
        name="sum_part",
    )(x)


def final_kernel(x_ref, g1_ref, g2_ref):
    factor = 1.0 / 512.0
    g2_ref[:, 0:256] = x_ref[0:512, 0:256].astype(F32) * factor
    g2_ref[:, 256:512] = x_ref[512:1024, 0:256].astype(F32) * factor
    for q in range(4):
        part = x_ref[128 * q : 128 * q + 128, 256:384].astype(F32)
        g1_ref[:, 128 * q : 128 * q + 128] = part * factor


def final_call(x):
    return pl.pallas_call(
        final_kernel,
        out_shape=(
            jax.ShapeDtypeStruct((FEAT, HID), F32),
            jax.ShapeDtypeStruct((HID, HID), F32),
        ),
        name="final_part",
    )(x)


def exchange(x):
    return lax.all_to_all(x, AXES, split_axis=0, concat_axis=0, tiled=True)


def local(
    node_feats, batch_deg, batch_nbrs, halo_nbrs, halo_len, halo_rows, halo_deg,
    feat_table, emb_table, grad_table, weight_one, weight_two, grad_out,
):
    bdeg = batch_deg.reshape(1, NB)
    hdeg = halo_deg.reshape(1, NH)
    offsets = (halo_rows % NB).reshape(128, 1, 4)
    asked = exchange(offsets)
    h, gt, p = halo_call(halo_nbrs, halo_len.reshape(1, NB), bdeg, hdeg, grad_out)
    send, s = pick_call(asked.reshape(64, 8), feat_table, emb_table, grad_table, p)
    recv = exchange(send.reshape(128, 8, 896)).reshape(1024, 896)
    c, cf, st = batch_call(batch_nbrs, bdeg, node_feats, gt)
    u, pa, grads = main_call(recv, c, h, cf, st, gt, weight_one, weight_two, bdeg, hdeg)
    shares = exchange(grads.reshape(128, 8, 384))
    out_embed, halo_grad = tail_call(u, weight_two, bdeg, s, pa)
    sums = exchange(sum_call(shares)).reshape(1024, 384)
    grad_one, grad_two = final_call(sums)
    return out_embed, halo_grad, grad_one, grad_two


def solution(mesh):
    rows = P(AXES, None)
    flat = P(AXES)
    return jax.shard_map(
        local,
        mesh=mesh,
        in_specs=(
            rows, flat, rows, rows, flat, flat, flat, rows, rows, rows, P(), P(), rows,
        ),
        out_specs=(rows, rows, P(), P()),
        check_vma=False,
    )
```

profile of v0, /device:TPU:1, one launch (start us, length us, event | category | flops | bytes accessed | tf_op | source)
XLA Modules:
  0.0 141.3 jit_solution(12288889589525847642)
XLA Ops:
  0.6 0.7 add_select_fusion
  1.3 0.7 reshape.35
  2.1 11.5 %all-to-all-start = ((s32[128,1,4]{2,1,0:T(1,128)}), s32[128,1,4]{2,1,0:T(1,128)S(1)}, u32[]{:S(2)}, u32[]{:S(2)}) async-start(s32[128,1,4]{2,1,0:T(1,128)} %bitcast), calls=%async_computation | async-start | bytes 131072 | tf_op jit(solution)/shard_map/all_to_all | solution.py:379
  13.6 2.2 %copy.22.hn_ref = s32[2048,8]{1,0:T(8,128)} copy(s32[2048,8]{0,1:T(8,128)} %param.16) | data formatting | bytes 131072 | tf_op args[3]
  15.7 9.5 %halo_part.1 = (bf16[2048,512]{1,0:T(8,128)(2,1)}, bf16[512,2048]{1,0:T(8,128)(2,1)}, bf16[512,512]{1,0:T(8,128)(2,1)}) custom-call(s32[2048,8]{1,0:T(8,128)} %copy.22.hn_ref, s32[1,2048]{1,0:T(1,128)} %bitcast.16, s32[1,2048]{1,0:T(1,128)} %bitcast.12, s32[1,512]{1,0:T(1,128)} %bitcast.17, bf16[2048,512]{1,0:T(8,128)(2,1)} %g_ref.1), custom_call_target="tpu_custom_call" | custom-call | tf_op jit(solution)/shard_map/halo_part/pallas_call | solution.py:83
  25.2 0.0 all-to-all-done
  25.2 0.5 broadcast.11
  25.7 0.8 reduce.3
  26.5 0.7 reshape.36.ask_ref
  27.2 7.0 %pick_rows.1 = (bf16[1024,896]{1,0:T(8,128)(2,1)}, bf16[512,2048]{1,0:T(8,128)(2,1)}) custom-call(s32[64,8]{1,0:T(8,128)} %reshape.36.ask_ref, bf16[2048,128]{1,0:T(8,128)(2,1)} %x_ref.1, bf16[2048,512]{1,0:T(8,128)(2,1)} %e_ref.1, bf16[2048,512]{1,0:T(8,128)(2,1)} %v_ref.1, bf16[512,512]{1,0:T(8,128)(2,1)} %get-tuple-element.19.p_ref), custom_call_target="tpu_custom_call" | custom-call | tf_op jit(solution)/shard_map/pick_rows/pallas_call | solution.py:135
  34.1 0.0 copy-start.2
  34.1 9.8 %all-to-all-start.1 = ((bf16[128,8,896]{2,1,0:T(8,128)(2,1)}), bf16[128,8,896]{2,1,0:T(8,128)(2,1)S(1)}, u32[]{:S(2)}, u32[]{:S(2)}) async-start(bf16[128,8,896]{2,1,0:T(8,128)(2,1)} %bitcast.10), calls=%async_computation.1 | async-start | bytes 3670016 | tf_op jit(solution)/shard_map/all_to_all | solution.py:379
  43.9 0.0 copy-done.2
  43.9 1.3 copy.23.nb_ref
  45.2 23.1 %batch_part.1 = (bf16[2048,2048]{1,0:T(8,128)(2,1)}, f32[2048,128]{1,0:T(8,128)}, f32[512,2048]{1,0:T(8,128)}) custom-call(s32[2048,8]{1,0:T(8,128)} %copy.23.nb_ref, s32[1,2048]{1,0:T(1,128)} %bitcast.13, bf16[2048,128]{1,0:T(8,128)(2,1)} %f_ref.1, bf16[512,2048]{1,0:T(8,128)(2,1)} %get-tuple-element.21.gt_ref), custom_call_target="tpu_custom_call" | custom-call | tf_op jit(solution)/shard_map/batch_part/pallas_call | solution.py:180
  68.3 2.5 %all-to-all-done.1 = bf16[128,8,896]{2,1,0:T(8,128)(2,1)S(1)} async-done(((bf16[128,8,896]{2,1,0:T(8,128)(2,1)}), bf16[128,8,896]{2,1,0:T(8,128)(2,1)S(1)}, u32[]{:S(2)}, u32[]{:S(2)}) %all-to-all-start.1) | async-done | bytes 1835040 | tf_op jit(solution)/shard_map/all_to_all | solution.py:379
  70.8 0.0 copy-start
  70.8 1.2 copy-done
  72.1 19.5 %main_part.1 = (bf16[2048,512]{1,0:T(8,128)(2,1)}, bf16[512,512]{1,0:T(8,128)(2,1)}, bf16[1024,384]{1,0:T(8,128)(2,1)}) custom-call(bf16[1024,896]{1,0:T(8,128)(2,1)} %bitcast.8, bf16[2048,2048]{1,0:T(8,128)(2,1)} %get-tuple-element.22.c_ref, bf16[2048,512]{1,0:T(8,128)(2,1)} %get-tuple-element.23.h_ref, f32[2048,128]{1,0:T(8,128)} %get-tuple-element.24.cf_ref, ...), custom_call_target="tpu_custom_call" | custom-call | tf_op jit(solution)/shard_map/main_part/pallas_call | solution.py:273
  91.6 23.4 %all_to_all.20.x_ref = bf16[128,8,384]{2,1,0:T(8,128)(2,1)} all-to-all(bf16[128,8,384]{2,1,0:T(8,128)(2,1)} %bitcast.11), channel_id=1, replica_groups=mesh['dp'=8,'mp'=16] {'dp','mp'}, dimensions={0} | all-to-all | bytes 1572864 | tf_op jit(solution)/shard_map/all_to_all | solution.py:379
  115.0 2.2 %sum_part.1 = bf16[128,8,384]{2,1,0:T(8,128)(2,1)} custom-call(bf16[128,8,384]{2,1,0:T(8,128)(2,1)} %all_to_all.20.x_ref), custom_call_target="tpu_custom_call" | custom-call | tf_op jit(solution)/shard_map/sum_part/pallas_call | solution.py:351
  117.2 4.8 %all-to-all-start.3 = ((bf16[128,8,384]{2,1,0:T(8,128)(2,1)}), bf16[128,8,384]{2,1,0:T(8,128)(2,1)S(1)}, u32[]{:S(2)}, u32[]{:S(2)}) async-start(bf16[128,8,384]{2,1,0:T(8,128)(2,1)} %sum_part.1), calls=%async_computation.3 | async-start | bytes 1572864 | tf_op jit(solution)/shard_map/all_to_all | solution.py:379
  122.0 6.0 %tail_part.1 = (bf16[2048,512]{1,0:T(8,128)(2,1)}, bf16[2048,512]{1,0:T(8,128)(2,1)}) custom-call(bf16[2048,512]{1,0:T(8,128)(2,1)} %get-tuple-element.26.u_ref, bf16[512,512]{1,0:T(8,128)(2,1)} %w2_ref.3, s32[1,2048]{1,0:T(1,128)} %bitcast.15, bf16[512,2048]{1,0:T(8,128)(2,1)} %get-tuple-element.27.s_ref, bf16[512,512]{1,0:T(8,128)(2,1)} %get-tuple-element.28.pa_ref), custom_call_target="tpu_custom_call" | custom-call | tf_op jit(solution)/shard_map/tail_part/pallas_call | solution.py:322
  128.0 10.1 %all-to-all-done.3 = bf16[128,8,384]{2,1,0:T(8,128)(2,1)S(1)} async-done(((bf16[128,8,384]{2,1,0:T(8,128)(2,1)}), bf16[128,8,384]{2,1,0:T(8,128)(2,1)S(1)}, u32[]{:S(2)}, u32[]{:S(2)}) %all-to-all-start.3) | async-done | bytes 786464 | tf_op jit(solution)/shard_map/all_to_all | solution.py:379
  138.1 0.0 copy-start.1
  138.1 0.9 copy-done.1
  139.0 2.3 %final_part.1 = (f32[128,512]{1,0:T(8,128)}, f32[512,512]{1,0:T(8,128)}) custom-call(bf16[1024,384]{1,0:T(8,128)(2,1)} %bitcast.9), custom_call_target="tpu_custom_call" | custom-call | tf_op jit(solution)/shard_map/final_part/pallas_call | solution.py:368
Async XLA Ops:
  2.1 23.1 %all-to-all-start = ((s32[128,1,4]{2,1,0:T(1,128)}), s32[128,1,4]{2,1,0:T(1,128)S(1)}, u32[]{:S(2)}, u32[]{:S(2)}) async-start(s32[128,1,4]{2,1,0:T(1,128)} %bitcast), calls=%async_computation | async-start | bytes 131072 | tf_op jit(solution)/shard_map/all_to_all | solution.py:379
  34.1 9.8 %copy-start.2 = (s32[2048,8]{0,1:T(8,128)S(1)}, s32[2048,8]{0,1:T(8,128)}, u32[]{:S(2)}) copy-start(s32[2048,8]{0,1:T(8,128)} %param.15) | copy-start | bytes 196612
  34.1 36.7 %all-to-all-start.1 = ((bf16[128,8,896]{2,1,0:T(8,128)(2,1)}), bf16[128,8,896]{2,1,0:T(8,128)(2,1)S(1)}, u32[]{:S(2)}, u32[]{:S(2)}) async-start(bf16[128,8,896]{2,1,0:T(8,128)(2,1)} %bitcast.10), calls=%async_computation.1 | async-start | bytes 3670016 | tf_op jit(solution)/shard_map/all_to_all | solution.py:379
  70.8 1.3 copy-start
  117.2 20.9 %all-to-all-start.3 = ((bf16[128,8,384]{2,1,0:T(8,128)(2,1)}), bf16[128,8,384]{2,1,0:T(8,128)(2,1)S(1)}, u32[]{:S(2)}, u32[]{:S(2)}) async-start(bf16[128,8,384]{2,1,0:T(8,128)(2,1)} %sum_part.1), calls=%async_computation.3 | async-start | bytes 1572864 | tf_op jit(solution)/shard_map/all_to_all | solution.py:379
  138.1 0.9 copy-start.1
where the time goes:
time: 142 us; the launch traced here: 141 us
  Pallas kernels  69.5 us (49%)
  starting transfers between devices  26 us (18%)
  blocking collectives  23.4 us (16%)
  waiting for transfers between devices  12.6 us (9%)
  local copies, waits for them, and re-layouts  7.54 us (5%)
  other arithmetic  1.5 us (1%)
    all_to_all x3, starting transfers between devices, exchange(): return lax.all_to_all(x, AXES, split_axis=0, concat_axis=0, tiled=True)  26 us
    all_to_all x1, blocking collectives, exchange(): return lax.all_to_all(x, AXES, split_axis=0, concat_axis=0, tiled=True)  23.4 us
    pallas_call x1, Pallas kernels, batch_call(): pl.pallas_call(batch_kernel, grid=(NB // STEP,), in_specs=[pl.BlockSpec((...  23.1 us
    pallas_call x1, Pallas kernels, main_call(): pl.pallas_call(main_kernel, grid=(NB // STEP,), in_specs=[whole(1024, 896...  19.5 us
    all_to_all x3, waiting for transfers between devices, exchange(): return lax.all_to_all(x, AXES, split_axis=0, concat_axis=0, tiled=True)  12.6 us
    pallas_call x1, Pallas kernels, halo_call(): pl.pallas_call(halo_kernel, out_shape=(jax.ShapeDtypeStruct((NB, NH), BF)...  9.45 us
    pallas_call x1, Pallas kernels, pick_call(): pl.pallas_call(pick_kernel, out_shape=(jax.ShapeDtypeStruct((1024, 896),...  6.96 us
    pallas_call x1, Pallas kernels, tail_call(): pl.pallas_call(tail_kernel, grid=(NB // STEP,), in_specs=[pl.BlockSpec((S...  6.03 us
  transfers between devices with their start and end apart: 3, of which 2 were waited for; matrix products, arithmetic and copies ran while one was open for 2% of the time, Pallas kernels for 27%

commit v1 on v0

v1 whole, which is shorter than its diff:
```python
import jax
import jax.numpy as jnp
from jax import lax
from jax.experimental import pallas as pl
from jax.experimental.pallas import tpu as pltpu
from jax.sharding import PartitionSpec as P

BF = jnp.bfloat16
F32 = jnp.float32
AXES = ("dp", "mp")
NB = 2048
NH = 512
HID = 512
FEAT = 128
STEP = 512
VMEM_LIMIT = 56 * 1024 * 1024


def dot(left, right):
    return jnp.dot(left, right, preferred_element_type=F32)


def dot_t(left, right):
    return lax.dot_general(left, right, (((1,), (1,)), ((), ())), preferred_element_type=F32)


def dot_tl(left, right):
    return lax.dot_general(left, right, (((0,), (0,)), ((), ())), preferred_element_type=F32)


def columns(row):
    n = row.shape[1]
    return jnp.concatenate(
        [jnp.broadcast_to(row[:, s : s + 128], (128, 128)).T for s in range(0, n, 128)], axis=0
    )


def scale_rows(x, col):
    reps = x.shape[1] // 128
    return x * (jnp.tile(col, (1, reps)) if reps > 1 else col)


def count_tiles(dst_ref, nbrs, rows0, n_rows):
    times = jnp.ones(nbrs.shape, jnp.int32)
    for k in range(1, 8):
        times = times + (nbrs == pltpu.roll(nbrs, k, 0)).astype(jnp.int32)
    times = times.astype(F32)
    zero = jnp.zeros((16, 128), BF)
    sub = lax.broadcasted_iota(jnp.int32, (16, 128), 0)
    for c in range(0, nbrs.shape[1], 128):
        idx = [
            jnp.broadcast_to(nbrs[k : k + 1, c : c + 128], (16, 128)).astype(jnp.int16)
            for k in range(8)
        ]
        val = [jnp.broadcast_to(times[k : k + 1, c : c + 128], (16, 128)).astype(BF) for k in range(8)]

        def group(t, _):
            base = pl.multiple_of(t * 128, 128)
            first = (sub + (base + rows0)).astype(jnp.int16)
            for r in range(0, 128, 16):
                here = first + jnp.int16(r)
                acc = zero
                for k in range(8):
                    acc = jnp.where(idx[k] == here, val[k], acc)
                dst_ref[pl.ds(base + r, 16), c : c + 128] = acc
            return 0

        lax.fori_loop(0, n_rows // 128, group, 0)


def halo_kernel(hn_ref, hl_ref, bdeg_ref, hdeg_ref, g_hbm, h_ref, gs_ref, p_ref, g_ref, sem):
    copy = pltpu.make_async_copy(g_hbm, g_ref, sem)
    copy.start()
    nbrs = hn_ref[...]
    slot = lax.broadcasted_iota(jnp.int32, nbrs.shape, 0)
    nbrs = jnp.where(slot < hl_ref[...], nbrs, -1)
    count_tiles(h_ref, nbrs, 0, NH)
    inv = columns(lax.rsqrt(bdeg_ref[...].astype(F32)))
    inv_h = columns(lax.rsqrt(hdeg_ref[...].astype(F32)))
    copy.wait()
    for s in range(0, NB, 512):
        gs_ref[s : s + 512, :] = scale_rows(g_ref[s : s + 512, :].astype(F32), inv[s : s + 512]).astype(BF)
    p_ref[...] = scale_rows(dot(h_ref[...], gs_ref[...]), inv_h).astype(BF)


def any_spec():
    return pl.BlockSpec(memory_space=pl.ANY)


def vmem_spec():
    return pl.BlockSpec(memory_space=pltpu.VMEM)


def halo_call(hn, hl, bdeg, hdeg, g):
    return pl.pallas_call(
        halo_kernel,
        in_specs=[vmem_spec()] * 4 + [any_spec()],
        out_specs=[vmem_spec()] * 3,
        out_shape=(
            jax.ShapeDtypeStruct((NH, NB), BF),
            jax.ShapeDtypeStruct((NB, HID), BF),
            jax.ShapeDtypeStruct((NH, HID), BF),
        ),
        scratch_shapes=[pltpu.VMEM((NB, HID), BF), pltpu.SemaphoreType.DMA(())],
        compiler_params=pltpu.CompilerParams(vmem_limit_bytes=VMEM_LIMIT),
        name="halo_part",
    )(hn, hl, bdeg, hdeg, g)


def pair_up(top, bottom):
    w = top.shape[1]
    t = top.reshape(64, 8, w)
    b = bottom.reshape(64, 8, w)
    low = lax.broadcasted_iota(jnp.int32, (64, 8, w), 1) < 4
    even = jnp.where(low, t, pltpu.roll(b, 4, 1))
    odd = jnp.where(low, pltpu.roll(t, 4, 1), b)
    return jnp.concatenate([even, odd], axis=1).astype(BF).reshape(1024, w)


def part_up(both):
    w = both.shape[1]
    x = both.reshape(64, 16, w).astype(F32)
    even, odd = x[:, 0:8], x[:, 8:16]
    low = lax.broadcasted_iota(jnp.int32, (64, 8, w), 1) < 4
    top = jnp.where(low, even, pltpu.roll(odd, 4, 1))
    bottom = jnp.where(low, pltpu.roll(even, 4, 1), odd)
    return top.reshape(512, w), bottom.reshape(512, w)


def pick_kernel(ask_ref, x_hbm, e_hbm, v_hbm, p_ref, out_ref, s_ref, x_ref, e_ref, v_ref, sems):
    copies = [
        pltpu.make_async_copy(src, dst, sems.at[n])
        for n, (src, dst) in enumerate(((e_hbm, e_ref), (v_hbm, v_ref), (x_hbm, x_ref)))
    ]
    for copy in copies:
        copy.start()
    a = ask_ref[...].reshape(64, 2, 1, 4)
    sub = lax.broadcasted_iota(jnp.int32, (64, 8, 4), 1)
    lane = lax.broadcasted_iota(jnp.int32, (64, 8, 4), 2)
    mine = jnp.where(
        sub < 4, jnp.broadcast_to(a[:, 0], (64, 8, 4)), jnp.broadcast_to(a[:, 1], (64, 8, 4))
    )
    mine = jnp.where(lane == (sub & 3), mine & (NB - 1), 0)
    col = jnp.sum(mine.astype(F32), axis=2, keepdims=True).reshape(512, 1).astype(jnp.int32)
    colb = jnp.broadcast_to(col, (512, 128)).astype(jnp.int16)
    lanes = lax.broadcasted_iota(jnp.int32, (512, 128), 1)
    one = jnp.ones((512, 128), BF)
    for c in range(0, NB, 128):
        s_ref[:, c : c + 128] = jnp.where(colb == (lanes + c).astype(jnp.int16), one, one - one)
    p = p_ref[...].astype(F32)
    out_ref[:, 640:768] = pair_up(p[:, 128:256], p[:, 256:384])
    out_ref[:, 768:896] = pair_up(p[:, 384:512], p[:, 384:512])
    s = s_ref[...]
    copies[0].wait()
    picked = dot(s, e_ref[...])
    copies[1].wait()
    out_ref[:, 0:512] = pair_up(picked, dot(s, v_ref[...]))
    copies[2].wait()
    out_ref[:, 512:640] = pair_up(dot(s, x_ref[...]), p[:, 0:128])


def pick_call(asked, x, e, v, p):
    return pl.pallas_call(
        pick_kernel,
        in_specs=[vmem_spec(), any_spec(), any_spec(), any_spec(), vmem_spec()],
        out_specs=[vmem_spec()] * 2,
        out_shape=(
            jax.ShapeDtypeStruct((1024, 896), BF),
            jax.ShapeDtypeStruct((NH, NB), BF),
        ),
        scratch_shapes=[
            pltpu.VMEM((NB, FEAT), BF),
            pltpu.VMEM((NB, HID), BF),
            pltpu.VMEM((NB, HID), BF),
            pltpu.SemaphoreType.DMA((3,)),
        ],
        compiler_params=pltpu.CompilerParams(vmem_limit_bytes=VMEM_LIMIT),
        name="pick_rows",
    )(asked, x, e, v, p)


def batch_kernel(nb_ref, bdeg_ref, f_ref, gs_ref, c_ref, cf_ref, sp_ref, fs_ref):
    i = pl.program_id(0)

    @pl.when(i == 0)
    def _():
        col = columns(lax.rsqrt(bdeg_ref[...].astype(F32)))
        fs_ref[...] = (f_ref[...].astype(F32) * col).astype(BF)

    r0 = pl.multiple_of(i * STEP, STEP)
    count_tiles(c_ref, nb_ref[...], r0, STEP)
    eye = (
        lax.broadcasted_iota(jnp.int32, (128, 128), 0)
        == lax.broadcasted_iota(jnp.int32, (128, 128), 1)
    ).astype(F32).astype(BF)
    for r in range(0, STEP, 128):
        at = pl.ds(pl.multiple_of(r0 + r, 128), 128)
        c_ref[r : r + 128, at] = c_ref[r : r + 128, at] + eye
    c = c_ref[...]
    sp_ref[...] = dot(c, gs_ref[...])
    part = dot_tl(c, fs_ref[pl.ds(r0, STEP), :])

    @pl.when(i == 0)
    def _():
        cf_ref[...] = part

    @pl.when(i > 0)
    def _():
        cf_ref[...] += part


def batch_call(nb, bdeg, f, gs):
    whole = lambda *shape: pl.BlockSpec(shape, lambda i: (0, 0))
    return pl.pallas_call(
        batch_kernel,
        grid=(NB // STEP,),
        in_specs=[whole(8, NB), whole(1, NB), whole(NB, FEAT), whole(NB, HID)],
        out_specs=[
            pl.BlockSpec((STEP, NB), lambda i: (i, 0)),
            whole(NB, FEAT),
            pl.BlockSpec((STEP, HID), lambda i: (i, 0)),
        ],
        out_shape=(
            jax.ShapeDtypeStruct((NB, NB), BF),
            jax.ShapeDtypeStruct((NB, FEAT), F32),
            jax.ShapeDtypeStruct((NB, HID), F32),
        ),
        scratch_shapes=[pltpu.VMEM((NB, FEAT), BF)],
        compiler_params=pltpu.CompilerParams(vmem_limit_bytes=VMEM_LIMIT),
        name="batch_part",
    )(nb, bdeg, f, gs)


def main_kernel(
    r_hbm, h_hbm, cf_hbm, c_hbm, sp_hbm, gs_hbm, w1_ref, w2_ref, bdeg_ref, hdeg_ref,
    u_ref, pa_ref, grads_ref,
    r_ref, h_ref, cf_ref, c_ref, sp_ref, gs_ref,
    hid_ref, der_ref, u1_ref, he_ref, hv_ref, g1_ref, g2_ref, sems,
):
    pairs = (
        (r_hbm, r_ref), (h_hbm, h_ref), (cf_hbm, cf_ref), (c_hbm, c_ref), (gs_hbm, gs_ref), (sp_hbm, sp_ref),
    )
    copies = [pltpu.make_async_copy(src, dst, sems.at[n]) for n, (src, dst) in enumerate(pairs)]
    for copy in copies:
        copy.start()
    inv = columns(lax.rsqrt(bdeg_ref[...].astype(F32)))
    col_h = columns(lax.rsqrt(hdeg_ref[...].astype(F32)))
    copies[0].wait()
    hx, p0 = part_up(r_ref[:, 512:640])
    hx = (hx * col_h).astype(BF)
    copies[1].wait()
    copies[2].wait()
    for s in range(0, NB, STEP):
        col = inv[s : s + STEP]
        u1 = (cf_ref[s : s + STEP, :] + dot_tl(h_ref[:, s : s + STEP], hx)).astype(BF)
        u1_ref[s : s + STEP, :] = u1
        pre = scale_rows(dot(u1, w1_ref[...]), col)
        sig = 0.5 + 0.5 * jnp.tanh(0.5 * pre)
        hid_ref[s : s + STEP, :] = scale_rows(pre * sig, col).astype(BF)
        der_ref[s : s + STEP, :] = scale_rows(sig * (1.0 + pre * (1.0 - sig)), col * col)
    he, hv = part_up(r_ref[:, 0:512])
    he_ref[...] = scale_rows(he, col_h).astype(BF)
    hv_ref[...] = scale_rows(hv, col_h).astype(BF)
    p1, p2 = part_up(r_ref[:, 640:768])
    p3, _ = part_up(r_ref[:, 768:896])
    pa_ref[:, 0:128] = p0.astype(BF)
    pa_ref[:, 128:256] = p1.astype(BF)
    pa_ref[:, 256:384] = p2.astype(BF)
    pa_ref[:, 384:512] = p3.astype(BF)
    for copy in copies[3:]:
        copy.wait()
    for s in range(0, NB, STEP):
        h = h_ref[:, s : s + STEP]
        u = (dot_tl(c_ref[:, s : s + STEP], hid_ref[...]) + dot_tl(h, he_ref[...])).astype(BF)
        u_ref[s : s + STEP, :] = u
        spread = (sp_ref[s : s + STEP, :] + dot_tl(h, hv_ref[...])).astype(BF)
        d_pre = (dot_t(spread, w2_ref[...]) * der_ref[s : s + STEP, :]).astype(BF)
        g2 = dot_tl(u, gs_ref[s : s + STEP, :])
        g1 = dot_tl(u1_ref[s : s + STEP, :], d_pre)
        if s == 0:
            g1_ref[...] = g1
            g2_ref[...] = g2
        else:
            g1_ref[...] += g1
            g2_ref[...] += g2
    grads_ref[0:512, 0:256] = g2_ref[:, 0:256].astype(BF)
    grads_ref[512:1024, 0:256] = g2_ref[:, 256:512].astype(BF)
    for q in range(4):
        grads_ref[128 * q : 128 * q + 128, 256:384] = g1_ref[:, 128 * q : 128 * q + 128].astype(BF)
    grads_ref[512:1024, 256:384] = jnp.zeros((512, 128), BF)


def main_call(recv, c, h, cf, sp, gs, w1, w2, bdeg, hdeg):
    return pl.pallas_call(
        main_kernel,
        in_specs=[any_spec()] * 6 + [vmem_spec()] * 4,
        out_specs=[vmem_spec()] * 3,
        out_shape=(
            jax.ShapeDtypeStruct((NB, HID), BF),
            jax.ShapeDtypeStruct((NH, HID), BF),
            jax.ShapeDtypeStruct((1024, 384), BF),
        ),
        scratch_shapes=[
            pltpu.VMEM((1024, 896), BF),
            pltpu.VMEM((NH, NB), BF),
            pltpu.VMEM((NB, FEAT), F32),
            pltpu.VMEM((NB, NB), BF),
            pltpu.VMEM((NB, HID), F32),
            pltpu.VMEM((NB, HID), BF),
            pltpu.VMEM((NB, HID), BF),
            pltpu.VMEM((NB, HID), F32),
            pltpu.VMEM((NB, FEAT), BF),
            pltpu.VMEM((NH, HID), BF),
            pltpu.VMEM((NH, HID), BF),
            pltpu.VMEM((FEAT, HID), F32),
            pltpu.VMEM((HID, HID), F32),
            pltpu.SemaphoreType.DMA((6,)),
        ],
        compiler_params=pltpu.CompilerParams(vmem_limit_bytes=VMEM_LIMIT),
        name="main_part",
    )(recv, h, cf, c, sp, gs, w1, w2, bdeg, hdeg)


def tail_kernel(u_ref, w2_ref, bdeg_ref, s_ref, pa_ref, out_ref, hg_ref):
    i = pl.program_id(0)
    r = pl.multiple_of(i * STEP, STEP)
    col = columns(lax.rsqrt(bdeg_ref[:, pl.ds(r, STEP)].astype(F32)))
    out_ref[...] = scale_rows(dot(u_ref[...], w2_ref[...]), col).astype(BF)
    hg_ref[...] = dot_tl(s_ref[...], pa_ref[...]).astype(BF)


def tail_call(u, w2, bdeg, s, pa):
    whole = lambda *shape: pl.BlockSpec(shape, lambda i: (0, 0))
    return pl.pallas_call(
        tail_kernel,
        grid=(NB // STEP,),
        in_specs=[
            pl.BlockSpec((STEP, HID), lambda i: (i, 0)),
            whole(HID, HID),
            whole(1, NB),
            pl.BlockSpec((NH, STEP), lambda i: (0, i)),
            whole(NH, HID),
        ],
        out_specs=[
            pl.BlockSpec((STEP, HID), lambda i: (i, 0)),
            pl.BlockSpec((STEP, HID), lambda i: (i, 0)),
        ],
        out_shape=(
            jax.ShapeDtypeStruct((NB, HID), BF),
            jax.ShapeDtypeStruct((NB, HID), BF),
        ),
        compiler_params=pltpu.CompilerParams(vmem_limit_bytes=VMEM_LIMIT),
        name="tail_part",
    )(u, w2, bdeg, s, pa)


def sum_kernel(x_ref, o_ref):
    total = jnp.sum(x_ref[...].astype(F32), axis=0)
    o_ref[...] = jnp.broadcast_to(total.astype(BF)[None], (128, 8, 384))


def sum_call(x):
    return pl.pallas_call(
        sum_kernel,
        out_shape=jax.ShapeDtypeStruct((128, 8, 384), BF),
        name="sum_part",
    )(x)


def final_kernel(x_ref, g1_ref, g2_ref):
    factor = 1.0 / 512.0
    g2_ref[:, 0:256] = x_ref[0:512, 0:256].astype(F32) * factor
    g2_ref[:, 256:512] = x_ref[512:1024, 0:256].astype(F32) * factor
    for q in range(4):
        part = x_ref[128 * q : 128 * q + 128, 256:384].astype(F32)
        g1_ref[:, 128 * q : 128 * q + 128] = part * factor


def final_call(x):
    return pl.pallas_call(
        final_kernel,
        out_shape=(
            jax.ShapeDtypeStruct((FEAT, HID), F32),
            jax.ShapeDtypeStruct((HID, HID), F32),
        ),
        name="final_part",
    )(x)


def exchange(x):
    return lax.all_to_all(x, AXES, split_axis=0, concat_axis=0, tiled=True)


def local(
    node_feats, batch_deg, batch_nbrs, halo_nbrs, halo_len, halo_rows, halo_deg,
    feat_table, emb_table, grad_table, weight_one, weight_two, grad_out,
):
    bdeg = batch_deg.reshape(1, NB)
    hdeg = halo_deg.reshape(1, NH)
    asked = exchange(halo_rows.reshape(128, 1, 4))
    h, gs, p = halo_call(halo_nbrs.T, halo_len.reshape(1, NB), bdeg, hdeg, grad_out)
    send, s = pick_call(asked, feat_table, emb_table, grad_table, p)
    recv = exchange(send.reshape(128, 8, 896)).reshape(1024, 896)
    c, cf, sp = batch_call(batch_nbrs.T, bdeg, node_feats, gs)
    u, pa, grads = main_call(recv, c, h, cf, sp, gs, weight_one, weight_two, bdeg, hdeg)
    shares = exchange(grads.reshape(128, 8, 384))
    out_embed, halo_grad = tail_call(u, weight_two, bdeg, s, pa)
    sums = exchange(sum_call(shares)).reshape(1024, 384)
    grad_one, grad_two = final_call(sums)
    return out_embed, halo_grad, grad_one, grad_two


def solution(mesh):
    rows = P(AXES, None)
    flat = P(AXES)
    return jax.shard_map(
        local,
        mesh=mesh,
        in_specs=(
            rows, flat, rows, rows, flat, flat, flat, rows, rows, rows, P(), P(), rows,
        ),
        out_specs=(rows, rows, P(), P()),
        check_vma=False,
    )
```

time: 142 us -> 133 us (0.937)
  waiting for transfers between devices: 12.6 us -> 21.8 us
  Pallas kernels: 69.5 us -> 61.4 us
  starting transfers between devices: 26 us -> 22 us
  local copies, waits for them, and re-layouts: 7.54 us -> 4.23 us
  blocking collectives: 23.4 us -> 21.8 us
  other arithmetic: 1.5 us -> 0 us
    all_to_all x3, waiting for transfers between devices: 12.6 us -> 21.8 us  [exchange(): return lax.all_to_all(x, AXES, split_axis=0, concat_axis=0, tiled=True)]
    pallas_call x4, Pallas kernels: 59 us -> 50.9 us  [the longest x1 19.2 us: batch_call(): pl.pallas_call(batch_kernel, grid=(NB // STEP,), in_specs=[whole(8, NB),...]
    all_to_all x3, starting transfers between devices: 26 us -> 22 us  [exchange(): return lax.all_to_all(x, AXES, split_axis=0, concat_axis=0, tiled=True)]
    unnamed x8 -> x6, local copies, waits for them, and re-layouts: 5.6 us -> 2.82 us
    all_to_all x1, blocking collectives: 23.4 us -> 21.8 us  [exchange(): return lax.all_to_all(x, AXES, split_axis=0, concat_axis=0, tiled=True)]
  transfers between devices with their start and end apart: 3 -> 3, of which waited for: 2 -> 3; matrix products, arithmetic and copies ran while one was open for 2% -> 0% of each run, Pallas kernels for 27% -> 23%
where the time goes in v1:
time: 133 us; the launch traced here: 132 us
  Pallas kernels  61.4 us (46%)
  starting transfers between devices  22 us (17%)
  waiting for transfers between devices  21.8 us (16%)
  blocking collectives  21.8 us (16%)
  local copies, waits for them, and re-layouts  4.23 us (3%)
    all_to_all x3, starting transfers between devices, exchange(): return lax.all_to_all(x, AXES, split_axis=0, concat_axis=0, tiled=True)  22 us
    all_to_all x3, waiting for transfers between devices, exchange(): return lax.all_to_all(x, AXES, split_axis=0, concat_axis=0, tiled=True)  21.8 us
    all_to_all x1, blocking collectives, exchange(): return lax.all_to_all(x, AXES, split_axis=0, concat_axis=0, tiled=True)  21.8 us
    pallas_call x1, Pallas kernels, batch_call(): pl.pallas_call(batch_kernel, grid=(NB // STEP,), in_specs=[whole(8, NB),...  19.2 us
    pallas_call x1, Pallas kernels, main_call(): pl.pallas_call(main_kernel, in_specs=[any_spec()] * 6 + [vmem_spec()] * 4...  17.9 us
    pallas_call x1, Pallas kernels, pick_call(): pl.pallas_call(pick_kernel, in_specs=[vmem_spec(), any_spec(), any_spec()...  8.27 us
    pallas_call x1, Pallas kernels, tail_call(): pl.pallas_call(tail_kernel, grid=(NB // STEP,), in_specs=[pl.BlockSpec((S...  6.04 us
    pallas_call x1, Pallas kernels, halo_call(): pl.pallas_call(halo_kernel, in_specs=[vmem_spec()] * 4 + [any_spec()], ou...  5.5 us
  transfers between devices with their start and end apart: 3, of which 3 were waited for; matrix products, arithmetic and copies ran while one was open for 0% of the time, Pallas kernels for 23%

profile of v1, /device:TPU:1, one launch (start us, length us, event | category | flops | bytes accessed | tf_op | source)
XLA Modules:
  0.0 131.9 jit_solution(2136057941536753470)
XLA Ops:
  0.6 1.4 %reshape.32 = s32[128,1,4]{2,0,1:T(8,128)} reshape(s32[512]{0:T(512)} %param.18) | data formatting | bytes 4096 | tf_op jit(solution)/shard_map/reshape | solution.py:400
  2.0 11.5 %all-to-all-start = ((s32[128,1,4]{2,1,0:T(1,128)}), s32[128,1,4]{2,1,0:T(1,128)S(1)}, u32[]{:S(2)}, u32[]{:S(2)}) async-start(s32[128,1,4]{2,1,0:T(1,128)} %bitcast), calls=%async_computation | async-start | bytes 131072 | tf_op jit(solution)/shard_map/all_to_all | solution.py:391
  13.5 5.5 %halo_part.1 = (bf16[512,2048]{1,0:T(8,128)(2,1)}, bf16[2048,512]{1,0:T(8,128)(2,1)}, bf16[512,512]{1,0:T(8,128)(2,1)}) custom-call(s32[8,2048]{1,0:T(8,128)} %bitcast.18, s32[1,2048]{1,0:T(1,128)} %bitcast.20, s32[1,2048]{1,0:T(1,128)} %bitcast.14, s32[1,512]{1,0:T(1,128)} %bitcast.21, bf16[2048,512]{1,0:T(8,128)(2,1)} %g_hbm.1), custom_call_target="tpu_custom_call" | custom-call | tf_op jit(solution)/shard_map/halo_part/pallas_call | solution.py:95
  19.0 4.0 %all-to-all-done.ask_ref = s32[128,1,4]{2,1,0:T(1,128)S(1)} async-done(((s32[128,1,4]{2,1,0:T(1,128)}), s32[128,1,4]{2,1,0:T(1,128)S(1)}, u32[]{:S(2)}, u32[]{:S(2)}) %all-to-all-start) | async-done | bytes 2080 | tf_op jit(solution)/shard_map/all_to_all | solution.py:391
  23.1 0.0 copy-start.2
  23.1 0.6 copy-done.2
  23.7 8.3 %pick_rows.1 = (bf16[1024,896]{1,0:T(8,128)(2,1)}, bf16[512,2048]{1,0:T(8,128)(2,1)}) custom-call(s32[128,1,4]{2,1,0:T(1,128)} %copy-done.2, bf16[2048,128]{1,0:T(8,128)(2,1)} %x_hbm.1, bf16[2048,512]{1,0:T(8,128)(2,1)} %e_hbm.1, bf16[2048,512]{1,0:T(8,128)(2,1)} %v_hbm.1, bf16[512,512]{1,0:T(8,128)(2,1)} %get-tuple-element.19.p_ref), custom_call_target="tpu_custom_call" | custom-call | tf_op jit(solution)/shard_map/pick_rows/pallas_call | solution.py:163
  32.0 5.8 %all-to-all-start.1 = ((bf16[128,8,896]{2,1,0:T(8,128)(2,1)}), bf16[128,8,896]{2,1,0:T(8,128)(2,1)S(1)}, u32[]{:S(2)}, u32[]{:S(2)}) async-start(bf16[128,8,896]{2,1,0:T(8,128)(2,1)} %bitcast.12), calls=%async_computation.1 | async-start | bytes 3670016 | tf_op jit(solution)/shard_map/all_to_all | solution.py:391
  37.7 19.2 %batch_part.1 = (bf16[2048,2048]{1,0:T(8,128)(2,1)}, f32[2048,128]{1,0:T(8,128)}, f32[2048,512]{1,0:T(8,128)}) custom-call(s32[8,2048]{1,0:T(8,128)} %bitcast.19, s32[1,2048]{1,0:T(1,128)} %bitcast.15, bf16[2048,128]{1,0:T(8,128)(2,1)} %f_ref.1, bf16[2048,512]{1,0:T(8,128)(2,1)} %get-tuple-element.22.gs_ref.gs_hbm), custom_call_target="tpu_custom_call" | custom-call | tf_op jit(solution)/shard_map/batch_part/pallas_call | solution.py:214
  57.0 7.7 %all-to-all-done.1 = bf16[128,8,896]{2,1,0:T(8,128)(2,1)S(1)} async-done(((bf16[128,8,896]{2,1,0:T(8,128)(2,1)}), bf16[128,8,896]{2,1,0:T(8,128)(2,1)S(1)}, u32[]{:S(2)}, u32[]{:S(2)}) %all-to-all-start.1) | async-done | bytes 1835040 | tf_op jit(solution)/shard_map/all_to_all | solution.py:391
  64.7 0.0 copy-start
  64.7 1.3 copy-done
  65.9 17.9 %main_part.1 = (bf16[2048,512]{1,0:T(8,128)(2,1)}, bf16[512,512]{1,0:T(8,128)(2,1)}, bf16[1024,384]{1,0:T(8,128)(2,1)}) custom-call(bf16[1024,896]{1,0:T(8,128)(2,1)} %bitcast.10, bf16[512,2048]{1,0:T(8,128)(2,1)} %get-tuple-element.21.h_hbm, f32[2048,128]{1,0:T(8,128)} %get-tuple-element.23.cf_hbm, bf16[2048,2048]{1,0:T(8,128)(2,1)} %get-tuple-element.24.c_hbm, ...), custom_call_target="tpu_custom_call" | custom-call | tf_op jit(solution)/shard_map/main_part/pallas_call | solution.py:294
  83.8 21.8 %all_to_all.20.x_ref = bf16[128,8,384]{2,1,0:T(8,128)(2,1)} all-to-all(bf16[128,8,384]{2,1,0:T(8,128)(2,1)} %bitcast.13), channel_id=1, replica_groups=mesh['dp'=8,'mp'=16] {'dp','mp'}, dimensions={0} | all-to-all | bytes 1572864 | tf_op jit(solution)/shard_map/all_to_all | solution.py:391
  105.6 2.2 %sum_part.1 = bf16[128,8,384]{2,1,0:T(8,128)(2,1)} custom-call(bf16[128,8,384]{2,1,0:T(8,128)(2,1)} %all_to_all.20.x_ref), custom_call_target="tpu_custom_call" | custom-call | tf_op jit(solution)/shard_map/sum_part/pallas_call | solution.py:363
  107.8 4.8 %all-to-all-start.3 = ((bf16[128,8,384]{2,1,0:T(8,128)(2,1)}), bf16[128,8,384]{2,1,0:T(8,128)(2,1)S(1)}, u32[]{:S(2)}, u32[]{:S(2)}) async-start(bf16[128,8,384]{2,1,0:T(8,128)(2,1)} %sum_part.1), calls=%async_computation.3 | async-start | bytes 1572864 | tf_op jit(solution)/shard_map/all_to_all | solution.py:391
  112.6 6.0 %tail_part.1 = (bf16[2048,512]{1,0:T(8,128)(2,1)}, bf16[2048,512]{1,0:T(8,128)(2,1)}) custom-call(bf16[2048,512]{1,0:T(8,128)(2,1)} %get-tuple-element.26.u_ref, bf16[512,512]{1,0:T(8,128)(2,1)} %w2_ref.3, s32[1,2048]{1,0:T(1,128)} %bitcast.17, bf16[512,2048]{1,0:T(8,128)(2,1)} %get-tuple-element.27.s_ref, bf16[512,512]{1,0:T(8,128)(2,1)} %get-tuple-element.28.pa_ref), custom_call_target="tpu_custom_call" | custom-call | tf_op jit(solution)/shard_map/tail_part/pallas_call | solution.py:334
  118.7 10.1 %all-to-all-done.3 = bf16[128,8,384]{2,1,0:T(8,128)(2,1)S(1)} async-done(((bf16[128,8,384]{2,1,0:T(8,128)(2,1)}), bf16[128,8,384]{2,1,0:T(8,128)(2,1)S(1)}, u32[]{:S(2)}, u32[]{:S(2)}) %all-to-all-start.3) | async-done | bytes 786464 | tf_op jit(solution)/shard_map/all_to_all | solution.py:391
  128.8 0.0 copy-start.1
  128.8 0.9 copy-done.1
  129.7 2.3 %final_part.1 = (f32[128,512]{1,0:T(8,128)}, f32[512,512]{1,0:T(8,128)}) custom-call(bf16[1024,384]{1,0:T(8,128)(2,1)} %bitcast.11), custom_call_target="tpu_custom_call" | custom-call | tf_op jit(solution)/shard_map/final_part/pallas_call | solution.py:380
Async XLA Ops:
  2.0 21.0 %all-to-all-start = ((s32[128,1,4]{2,1,0:T(1,128)}), s32[128,1,4]{2,1,0:T(1,128)S(1)}, u32[]{:S(2)}, u32[]{:S(2)}) async-start(s32[128,1,4]{2,1,0:T(1,128)} %bitcast), calls=%async_computation | async-start | bytes 131072 | tf_op jit(solution)/shard_map/all_to_all | solution.py:391
  23.1 0.6 copy-start.2
  32.0 32.7 %all-to-all-start.1 = ((bf16[128,8,896]{2,1,0:T(8,128)(2,1)}), bf16[128,8,896]{2,1,0:T(8,128)(2,1)S(1)}, u32[]{:S(2)}, u32[]{:S(2)}) async-start(bf16[128,8,896]{2,1,0:T(8,128)(2,1)} %bitcast.12), calls=%async_computation.1 | async-start | bytes 3670016 | tf_op jit(solution)/shard_map/all_to_all | solution.py:391
  64.7 1.3 copy-start
  107.8 20.9 %all-to-all-start.3 = ((bf16[128,8,384]{2,1,0:T(8,128)(2,1)}), bf16[128,8,384]{2,1,0:T(8,128)(2,1)S(1)}, u32[]{:S(2)}, u32[]{:S(2)}) async-start(bf16[128,8,384]{2,1,0:T(8,128)(2,1)} %sum_part.1), calls=%async_computation.3 | async-start | bytes 1572864 | tf_op jit(solution)/shard_map/all_to_all | solution.py:391
  128.8 0.9 copy-start.1

commit v2 on v1

v2 whole, which is shorter than its diff:
```python
import jax
import jax.numpy as jnp
from jax import lax
from jax.experimental import pallas as pl
from jax.experimental.pallas import tpu as pltpu
from jax.sharding import PartitionSpec as P

BF = jnp.bfloat16
F32 = jnp.float32
AXES = ("dp", "mp")
NB = 2048
NH = 512
HID = 512
FEAT = 128
STEP = 512


def hbm_spec():
    return pl.BlockSpec(memory_space=pltpu.HBM)


def vmem_spec():
    return pl.BlockSpec(memory_space=pltpu.VMEM)


def held(*shape, dtype=BF):
    return pltpu.VMEM(shape, dtype)


def keep(x):
    return pltpu.with_memory_space_constraint(x, pltpu.VMEM)


def leave(x):
    return pltpu.with_memory_space_constraint(x, pltpu.HBM)


def limit(mib):
    return pltpu.CompilerParams(vmem_limit_bytes=mib * 1024 * 1024)


def dot(left, right):
    return jnp.dot(left, right, preferred_element_type=F32)


def dot_t(left, right):
    return lax.dot_general(left, right, (((1,), (1,)), ((), ())), preferred_element_type=F32)


def dot_tl(left, right):
    return lax.dot_general(left, right, (((0,), (0,)), ((), ())), preferred_element_type=F32)


def columns(row):
    n = row.shape[1]
    return jnp.concatenate(
        [jnp.broadcast_to(row[:, s : s + 128], (128, 128)).T for s in range(0, n, 128)], axis=0
    )


def scale_rows(x, col):
    reps = x.shape[1] // 128
    return x * (jnp.tile(col, (1, reps)) if reps > 1 else col)


def count_tiles(dst_ref, nbrs, rows0, n_rows):
    times = jnp.ones(nbrs.shape, jnp.int32)
    for k in range(1, 8):
        times = times + (nbrs == pltpu.roll(nbrs, k, 0)).astype(jnp.int32)
    times = times.astype(F32)
    zero = jnp.zeros((16, 128), BF)
    sub = lax.broadcasted_iota(jnp.int32, (16, 128), 0)
    for c in range(0, nbrs.shape[1], 128):
        idx = [
            jnp.broadcast_to(nbrs[k : k + 1, c : c + 128], (16, 128)).astype(jnp.int16)
            for k in range(8)
        ]
        val = [jnp.broadcast_to(times[k : k + 1, c : c + 128], (16, 128)).astype(BF) for k in range(8)]

        def group(t, _):
            base = pl.multiple_of(t * 128, 128)
            first = (sub + (base + rows0)).astype(jnp.int16)
            for r in range(0, 128, 16):
                here = first + jnp.int16(r)
                acc = zero
                for k in range(8):
                    acc = jnp.where(idx[k] == here, val[k], acc)
                dst_ref[pl.ds(base + r, 16), c : c + 128] = acc
            return 0

        lax.fori_loop(0, n_rows // 128, group, 0)


def halo_kernel(
    hn_ref, hl_ref, bdeg_ref, hdeg_ref, g_hbm, h_hbm, gs_hbm, p_ref, g_ref, h_ref, gs_ref, sems
):
    copy_in = pltpu.make_async_copy(g_hbm, g_ref, sems.at[0])
    copy_in.start()
    nbrs = hn_ref[...]
    slot = lax.broadcasted_iota(jnp.int32, nbrs.shape, 0)
    nbrs = jnp.where(slot < hl_ref[...], nbrs, -1)
    count_tiles(h_ref, nbrs, 0, NH)
    copy_h = pltpu.make_async_copy(h_ref, h_hbm, sems.at[1])
    copy_h.start()
    inv = columns(lax.rsqrt(bdeg_ref[...].astype(F32)))
    inv_h = columns(lax.rsqrt(hdeg_ref[...].astype(F32)))
    copy_in.wait()
    for s in range(0, NB, STEP):
        gs = scale_rows(g_ref[s : s + STEP, :].astype(F32), inv[s : s + STEP])
        gs_ref[s : s + STEP, :] = gs.astype(BF)
    copy_gs = pltpu.make_async_copy(gs_ref, gs_hbm, sems.at[2])
    copy_gs.start()
    p_ref[...] = scale_rows(dot(h_ref[...], gs_ref[...]), inv_h).astype(BF)
    copy_h.wait()
    copy_gs.wait()


def halo_call(hn, hl, bdeg, hdeg, g):
    return pl.pallas_call(
        halo_kernel,
        in_specs=[vmem_spec()] * 4 + [hbm_spec()],
        out_specs=[hbm_spec(), hbm_spec(), vmem_spec()],
        out_shape=(
            pltpu.HBM((NH, NB), BF),
            pltpu.HBM((NB, HID), BF),
            held(NH, HID),
        ),
        scratch_shapes=[
            pltpu.VMEM((NB, HID), BF),
            pltpu.VMEM((NH, NB), BF),
            pltpu.VMEM((NB, HID), BF),
            pltpu.SemaphoreType.DMA((3,)),
        ],
        compiler_params=limit(58),
        name="halo_part",
    )(hn, hl, bdeg, hdeg, leave(g))


def pair_up(top, bottom):
    w = top.shape[1]
    t = top.reshape(64, 8, w)
    b = bottom.reshape(64, 8, w)
    low = lax.broadcasted_iota(jnp.int32, (64, 8, w), 1) < 4
    even = jnp.where(low, t, pltpu.roll(b, 4, 1))
    odd = jnp.where(low, pltpu.roll(t, 4, 1), b)
    return jnp.concatenate([even, odd], axis=1).astype(BF).reshape(1024, w)


def part_up(both):
    w = both.shape[1]
    x = both.reshape(64, 16, w).astype(F32)
    even, odd = x[:, 0:8], x[:, 8:16]
    low = lax.broadcasted_iota(jnp.int32, (64, 8, w), 1) < 4
    top = jnp.where(low, even, pltpu.roll(odd, 4, 1))
    bottom = jnp.where(low, pltpu.roll(even, 4, 1), odd)
    return top.reshape(512, w), bottom.reshape(512, w)


def selector(ask_ref, s_ref):
    a = ask_ref[...].reshape(64, 2, 1, 4)
    sub = lax.broadcasted_iota(jnp.int32, (64, 8, 4), 1)
    lane = lax.broadcasted_iota(jnp.int32, (64, 8, 4), 2)
    mine = jnp.where(
        sub < 4, jnp.broadcast_to(a[:, 0], (64, 8, 4)), jnp.broadcast_to(a[:, 1], (64, 8, 4))
    )
    mine = jnp.where(lane == (sub & 3), mine & (NB - 1), 0)
    col = jnp.sum(mine.astype(F32), axis=2, keepdims=True).reshape(512, 1).astype(jnp.int32)
    colb = jnp.broadcast_to(col, (512, 128))
    lanes = lax.broadcasted_iota(jnp.int32, (512, 128), 1)
    for c in range(0, NB, 128):
        s_ref[:, c : c + 128] = jnp.where(colb == lanes + c, 1.0, 0.0).astype(BF)


def pick_kernel(
    ask_ref, x_hbm, e_hbm, v_hbm, p_ref, out_hbm, s_ref, x_ref, e_ref, v_ref, out_ref, sems
):
    copies = [
        pltpu.make_async_copy(src, dst, sems.at[n])
        for n, (src, dst) in enumerate(((e_hbm, e_ref), (v_hbm, v_ref), (x_hbm, x_ref)))
    ]
    for copy in copies:
        copy.start()
    selector(ask_ref, s_ref)
    s = s_ref[...]
    copies[0].wait()
    picked = dot(s, e_ref[...])
    copies[1].wait()
    out_ref[:, 0:512] = pair_up(picked, dot(s, v_ref[...]))
    left = pltpu.make_async_copy(out_ref.at[:, 0:512], out_hbm.at[:, 0:512], sems.at[3])
    left.start()
    copies[2].wait()
    p = p_ref[...].astype(F32)
    out_ref[:, 512:640] = pair_up(dot(s, x_ref[...]), p[:, 0:128])
    out_ref[:, 640:768] = pair_up(p[:, 128:256], p[:, 256:384])
    out_ref[:, 768:896] = pair_up(p[:, 384:512], p[:, 384:512])
    right = pltpu.make_async_copy(out_ref.at[:, 512:896], out_hbm.at[:, 512:896], sems.at[4])
    right.start()
    left.wait()
    right.wait()


def pick_call(asked, x, e, v, p):
    return pl.pallas_call(
        pick_kernel,
        in_specs=[vmem_spec(), hbm_spec(), hbm_spec(), hbm_spec(), vmem_spec()],
        out_specs=hbm_spec(),
        out_shape=pltpu.HBM((1024, 896), BF),
        scratch_shapes=[
            pltpu.VMEM((NH, NB), BF),
            pltpu.VMEM((NB, FEAT), BF),
            pltpu.VMEM((NB, HID), BF),
            pltpu.VMEM((NB, HID), BF),
            pltpu.VMEM((1024, 896), BF),
            pltpu.SemaphoreType.DMA((5,)),
        ],
        compiler_params=limit(58),
        name="pick_rows",
    )(keep(asked), leave(x), leave(e), leave(v), keep(p))


def batch_kernel(
    nb_ref, bdeg_ref, f_ref, gs_ref, c_hbm, cf_ref, sp_hbm, fs_ref, c_ref, sp_ref, sems
):
    col = columns(lax.rsqrt(bdeg_ref[...].astype(F32)))
    fs_ref[...] = (f_ref[...].astype(F32) * col).astype(BF)
    eye = (
        lax.broadcasted_iota(jnp.int32, (128, 128), 0)
        == lax.broadcasted_iota(jnp.int32, (128, 128), 1)
    ).astype(F32).astype(BF)
    count_tiles(c_ref, nb_ref[...], 0, NB)
    for r in range(0, NB, 128):
        c_ref[r : r + 128, r : r + 128] = c_ref[r : r + 128, r : r + 128] + eye
    copies = [pltpu.make_async_copy(c_ref, c_hbm, sems.at[0])]
    copies[0].start()
    for n, r in enumerate(range(0, NB, STEP)):
        at = slice(r, r + STEP)
        sp_ref[at, :] = dot(c_ref[at, :], gs_ref[...])
        copies.append(pltpu.make_async_copy(sp_ref.at[at], sp_hbm.at[at], sems.at[1 + n]))
        copies[-1].start()
        cf_ref[at, :] = dot_tl(c_ref[:, at], fs_ref[...])
    for copy in copies:
        copy.wait()


def batch_call(nb, bdeg, f, gs):
    return pl.pallas_call(
        batch_kernel,
        in_specs=[vmem_spec()] * 4,
        out_specs=[hbm_spec(), vmem_spec(), hbm_spec()],
        out_shape=(
            pltpu.HBM((NB, NB), BF),
            pltpu.HBM((NB, FEAT), F32),
            pltpu.HBM((NB, HID), F32),
        ),
        scratch_shapes=[
            pltpu.VMEM((NB, FEAT), BF),
            pltpu.VMEM((NB, NB), BF),
            pltpu.VMEM((NB, HID), F32),
            pltpu.SemaphoreType.DMA((5,)),
        ],
        compiler_params=limit(58),
        name="batch_part",
    )(nb, bdeg, f, gs)


def main_kernel(
    r_ref, h_hbm, cf_hbm, c_hbm, sp_hbm, gs_hbm, w1_ref, w2_ref, bdeg_ref, hdeg_ref,
    u_hbm, pa_ref, grads_ref,
    h_ref, cf_ref, c_ref, sp_ref, gs_ref, u_ref,
    hid_ref, der_ref, u1_ref, he_ref, hv_ref, g1_ref, g2_ref, sems,
):
    pairs = (
        (h_hbm, h_ref), (cf_hbm, cf_ref), (c_hbm, c_ref), (gs_hbm, gs_ref), (sp_hbm, sp_ref),
    )
    copies = [pltpu.make_async_copy(src, dst, sems.at[n]) for n, (src, dst) in enumerate(pairs)]
    for copy in copies[:2]:
        copy.start()
    inv = columns(lax.rsqrt(bdeg_ref[...].astype(F32)))
    col_h = columns(lax.rsqrt(hdeg_ref[...].astype(F32)))
    for copy in copies[:2]:
        copy.wait()
    for copy in copies[2:]:
        copy.start()
    hx, p0 = part_up(r_ref[:, 512:640])
    hx = (hx * col_h).astype(BF)
    for s in range(0, NB, STEP):
        col = inv[s : s + STEP]
        u1 = (cf_ref[s : s + STEP, :] + dot_tl(h_ref[:, s : s + STEP], hx)).astype(BF)
        u1_ref[s : s + STEP, :] = u1
        pre = scale_rows(dot(u1, w1_ref[...]), col)
        sig = 0.5 + 0.5 * jnp.tanh(0.5 * pre)
        hid_ref[s : s + STEP, :] = scale_rows(pre * sig, col).astype(BF)
        der_ref[s : s + STEP, :] = scale_rows(sig * (1.0 + pre * (1.0 - sig)), col * col)
    he, hv = part_up(r_ref[:, 0:512])
    he_ref[...] = scale_rows(he, col_h).astype(BF)
    hv_ref[...] = scale_rows(hv, col_h).astype(BF)
    p1, p2 = part_up(r_ref[:, 640:768])
    p3, _ = part_up(r_ref[:, 768:896])
    pa_ref[:, 0:128] = p0.astype(BF)
    pa_ref[:, 128:256] = p1.astype(BF)
    pa_ref[:, 256:384] = p2.astype(BF)
    pa_ref[:, 384:512] = p3.astype(BF)
    for copy in copies[2:]:
        copy.wait()
    outs = []
    for s in range(0, NB, STEP):
        h = h_ref[:, s : s + STEP]
        u = (dot_tl(c_ref[:, s : s + STEP], hid_ref[...]) + dot_tl(h, he_ref[...])).astype(BF)
        at = slice(s, s + STEP)
        u_ref[at, :] = u
        outs.append(pltpu.make_async_copy(u_ref.at[at], u_hbm.at[at], sems.at[5 + s // STEP]))
        outs[-1].start()
        spread = (sp_ref[s : s + STEP, :] + dot_tl(h, hv_ref[...])).astype(BF)
        d_pre = (dot_t(spread, w2_ref[...]) * der_ref[s : s + STEP, :]).astype(BF)
        g2 = dot_tl(u, gs_ref[s : s + STEP, :])
        g1 = dot_tl(u1_ref[s : s + STEP, :], d_pre)
        if s == 0:
            g1_ref[...] = g1
            g2_ref[...] = g2
        else:
            g1_ref[...] += g1
            g2_ref[...] += g2
    grads_ref[0:512, 0:256] = g2_ref[:, 0:256].astype(BF)
    grads_ref[512:1024, 0:256] = g2_ref[:, 256:512].astype(BF)
    for q in range(4):
        grads_ref[128 * q : 128 * q + 128, 256:384] = g1_ref[:, 128 * q : 128 * q + 128].astype(BF)
    grads_ref[512:1024, 256:384] = jnp.zeros((512, 128), BF)
    for copy in outs:
        copy.wait()


def main_call(recv, c, h, cf, sp, gs, w1, w2, bdeg, hdeg):
    return pl.pallas_call(
        main_kernel,
        in_specs=[vmem_spec()] + [hbm_spec()] * 5 + [vmem_spec()] * 4,
        out_specs=[hbm_spec(), vmem_spec(), vmem_spec()],
        out_shape=(
            pltpu.HBM((NB, HID), BF),
            pltpu.HBM((NH, HID), BF),
            jax.ShapeDtypeStruct((1024, 384), BF),
        ),
        scratch_shapes=[
            pltpu.VMEM((NH, NB), BF),
            pltpu.VMEM((NB, FEAT), F32),
            pltpu.VMEM((NB, NB), BF),
            pltpu.VMEM((NB, HID), F32),
            pltpu.VMEM((NB, HID), BF),
            pltpu.VMEM((NB, HID), BF),
            pltpu.VMEM((NB, HID), BF),
            pltpu.VMEM((NB, HID), F32),
            pltpu.VMEM((NB, FEAT), BF),
            pltpu.VMEM((NH, HID), BF),
            pltpu.VMEM((NH, HID), BF),
            pltpu.VMEM((FEAT, HID), F32),
            pltpu.VMEM((HID, HID), F32),
            pltpu.SemaphoreType.DMA((10,)),
        ],
        compiler_params=limit(58),
        name="main_part",
    )(keep(recv), leave(h), leave(cf), leave(c), leave(sp), leave(gs), w1, w2, bdeg, hdeg)


def tail_kernel(
    u_ref, w2_ref, bdeg_ref, ask_ref, pa_ref, out_hbm, hg_hbm, s_ref, out_ref, hg_ref, sems
):
    selector(ask_ref, s_ref)
    col = columns(lax.rsqrt(bdeg_ref[...].astype(F32)))
    copies = []
    for n, r in enumerate(range(0, NB, STEP)):
        at = slice(r, r + STEP)
        out_ref[at] = scale_rows(dot(u_ref[at], w2_ref[...]), col[at]).astype(BF)
        hg_ref[at] = dot_tl(s_ref[:, at], pa_ref[...]).astype(BF)
        for m, (src, dst) in enumerate(((out_ref, out_hbm), (hg_ref, hg_hbm))):
            copies.append(pltpu.make_async_copy(src.at[at], dst.at[at], sems.at[2 * n + m]))
            copies[-1].start()
    for copy in copies:
        copy.wait()


def tail_call(u, w2, bdeg, asked, pa):
    return pl.pallas_call(
        tail_kernel,
        in_specs=[vmem_spec()] * 5,
        out_specs=[hbm_spec()] * 2,
        out_shape=(
            jax.ShapeDtypeStruct((NB, HID), BF),
            jax.ShapeDtypeStruct((NB, HID), BF),
        ),
        scratch_shapes=[
            pltpu.VMEM((NH, NB), BF),
            pltpu.VMEM((NB, HID), BF),
            pltpu.VMEM((NB, HID), BF),
            pltpu.SemaphoreType.DMA((8,)),
        ],
        compiler_params=limit(58),
        name="tail_part",
    )(u, w2, bdeg, keep(asked), pa)


def sum_kernel(x_ref, o_ref):
    total = jnp.sum(x_ref[...].astype(F32), axis=0)
    o_ref[...] = jnp.broadcast_to(total.astype(BF)[None], (128, 8, 384))


def sum_call(x):
    return pl.pallas_call(
        sum_kernel,
        in_specs=[vmem_spec()],
        out_specs=vmem_spec(),
        out_shape=jax.ShapeDtypeStruct((128, 8, 384), BF),
        name="sum_part",
    )(keep(x))


def final_kernel(x_ref, g1_ref, g2_ref):
    factor = 1.0 / 512.0
    g2_ref[:, 0:256] = x_ref[0:512, 0:256].astype(F32) * factor
    g2_ref[:, 256:512] = x_ref[512:1024, 0:256].astype(F32) * factor
    for q in range(4):
        part = x_ref[128 * q : 128 * q + 128, 256:384].astype(F32)
        g1_ref[:, 128 * q : 128 * q + 128] = part * factor


def final_call(x):
    return pl.pallas_call(
        final_kernel,
        in_specs=[vmem_spec()],
        out_specs=[vmem_spec()] * 2,
        out_shape=(
            jax.ShapeDtypeStruct((FEAT, HID), F32),
            jax.ShapeDtypeStruct((HID, HID), F32),
        ),
        name="final_part",
    )(keep(x))


def exchange(x):
    return lax.all_to_all(x, AXES, split_axis=0, concat_axis=0, tiled=True)


def local(
    node_feats, batch_deg, batch_nbrs, halo_nbrs, halo_len, halo_rows, halo_deg,
    feat_table, emb_table, grad_table, weight_one, weight_two, grad_out,
):
    bdeg = batch_deg.reshape(1, NB)
    hdeg = halo_deg.reshape(1, NH)
    asked = exchange(halo_rows.reshape(128, 1, 4))
    h, gs, p = halo_call(halo_nbrs.T, halo_len.reshape(1, NB), bdeg, hdeg, grad_out)
    send = pick_call(asked, feat_table, emb_table, grad_table, p)
    recv = exchange(send.reshape(128, 8, 896)).reshape(1024, 896)
    c, cf, sp = batch_call(batch_nbrs.T, bdeg, node_feats, gs)
    u, pa, grads = main_call(recv, c, h, cf, sp, gs, weight_one, weight_two, bdeg, hdeg)
    shares = exchange(grads.reshape(128, 8, 384))
    out_embed, halo_grad = tail_call(u, weight_two, bdeg, asked, pa)
    sums = exchange(sum_call(shares)).reshape(1024, 384)
    grad_one, grad_two = final_call(sums)
    return out_embed, halo_grad, grad_one, grad_two


def solution(mesh):
    rows = P(AXES, None)
    flat = P(AXES)
    return jax.shard_map(
        local,
        mesh=mesh,
        in_specs=(
            rows, flat, rows, rows, flat, flat, flat, rows, rows, rows, P(), P(), rows,
        ),
        out_specs=(rows, rows, P(), P()),
        check_vma=False,
    )
```

time: 133 us -> 127 us (0.955)
  Pallas kernels: 61.4 us -> 57.2 us
  local copies, waits for them, and re-layouts: 4.23 us -> 1.42 us
  waiting for transfers between devices: 21.8 us -> 24.1 us
    pallas_call x7, Pallas kernels: 61.4 us -> 57.2 us  [the longest x1 19.6 us: main_call(): pl.pallas_call(main_kernel, in_specs=[vmem_spec()] + [hbm_spec()] * 5 + [...]
    unnamed x6 -> x0, local copies, waits for them, and re-layouts: 2.82 us -> none
    all_to_all x3, waiting for transfers between devices: 21.8 us -> 24.1 us  [exchange(): return lax.all_to_all(x, AXES, split_axis=0, concat_axis=0, tiled=True)]
where the time goes in v2:
time: 127 us; the launch traced here: 126 us
  Pallas kernels  57.2 us (45%)
  waiting for transfers between devices  24.1 us (19%)
  starting transfers between devices  21.9 us (17%)
  blocking collectives  21.1 us (17%)
  local copies, waits for them, and re-layouts  1.42 us (1%)
    all_to_all x3, waiting for transfers between devices, exchange(): return lax.all_to_all(x, AXES, split_axis=0, concat_axis=0, tiled=True)  24.1 us
    all_to_all x3, starting transfers between devices, exchange(): return lax.all_to_all(x, AXES, split_axis=0, concat_axis=0, tiled=True)  21.9 us
    all_to_all x1, blocking collectives, exchange(): return lax.all_to_all(x, AXES, split_axis=0, concat_axis=0, tiled=True)  21.1 us
    pallas_call x1, Pallas kernels, main_call(): pl.pallas_call(main_kernel, in_specs=[vmem_spec()] + [hbm_spec()] * 5 + [...  19.6 us
    pallas_call x1, Pallas kernels, batch_call(): pl.pallas_call(batch_kernel, in_specs=[vmem_spec()] * 4, out_specs=[hbm_s...  17.8 us
    pallas_call x1, Pallas kernels, pick_call(): pl.pallas_call(pick_kernel, in_specs=[vmem_spec(), hbm_spec(), hbm_spec()...  6.9 us
    pallas_call x1, Pallas kernels, halo_call(): pl.pallas_call(halo_kernel, in_specs=[vmem_spec()] * 4 + [hbm_spec()], ou...  5.35 us
    pallas_call x1, Pallas kernels, tail_call(): pl.pallas_call(tail_kernel, in_specs=[vmem_spec()] * 5, out_specs=[hbm_sp...  5.34 us
  transfers between devices with their start and end apart: 3, of which 3 were waited for; matrix products, arithmetic and copies ran while one was open for 0% of the time, Pallas kernels for 23%

profile of v2, /device:TPU:1, one launch (start us, length us, event | category | flops | bytes accessed | tf_op | source)
XLA Modules:
  0.0 126.4 jit_solution(3039909747889797657)
XLA Ops:
  0.6 1.4 %reshape.32 = s32[128,1,4]{2,0,1:T(8,128)} reshape(s32[512]{0:T(512)} %param.18) | data formatting | bytes 4096 | tf_op jit(solution)/shard_map/reshape | solution.py:447
  2.0 11.5 %all-to-all-start = ((s32[128,1,4]{2,1,0:T(1,128)}), s32[128,1,4]{2,1,0:T(1,128)S(1)}, u32[]{:S(2)}, u32[]{:S(2)}) async-start(s32[128,1,4]{2,1,0:T(1,128)} %bitcast), calls=%async_computation | async-start | bytes 131072 | tf_op jit(solution)/shard_map/all_to_all | solution.py:438
  13.5 5.4 %halo_part.1 = (bf16[512,2048]{1,0:T(8,128)(2,1)}, bf16[2048,512]{1,0:T(8,128)(2,1)}, bf16[512,512]{1,0:T(8,128)(2,1)S(1)}) custom-call(s32[8,2048]{1,0:T(8,128)} %bitcast.18, s32[1,2048]{1,0:T(1,128)} %bitcast.20, s32[1,2048]{1,0:T(1,128)} %bitcast.14, s32[1,512]{1,0:T(1,128)} %bitcast.21, bf16[2048,512]{1,0:T(8,128)(2,1)} %g_hbm.1), custom_call_target="tpu_custom_call" | custom-call | tf_op jit(solution)/shard_map/halo_part/pallas_call | solution.py:119
  18.9 4.2 %all-to-all-done.ask_ref = s32[128,1,4]{2,1,0:T(1,128)S(1)} async-done(((s32[128,1,4]{2,1,0:T(1,128)}), s32[128,1,4]{2,1,0:T(1,128)S(1)}, u32[]{:S(2)}, u32[]{:S(2)}) %all-to-all-start) | async-done | bytes 2080 | tf_op jit(solution)/shard_map/all_to_all | solution.py:438
  23.1 6.9 %pick_rows.1 = bf16[1024,896]{1,0:T(8,128)(2,1)} custom-call(s32[128,1,4]{2,1,0:T(1,128)S(1)} %all-to-all-done.ask_ref, bf16[2048,128]{1,0:T(8,128)(2,1)} %x_hbm.1, bf16[2048,512]{1,0:T(8,128)(2,1)} %e_hbm.1, bf16[2048,512]{1,0:T(8,128)(2,1)} %v_hbm.1, bf16[512,512]{1,0:T(8,128)(2,1)S(1)} %get-tuple-element.17.p_ref), custom_call_target="tpu_custom_call" | custom-call | tf_op jit(solution)/shard_map/pick_rows/pallas_call | solution.py:203
  30.0 5.6 %all-to-all-start.1 = ((bf16[128,8,896]{2,1,0:T(8,128)(2,1)}), bf16[128,8,896]{2,1,0:T(8,128)(2,1)S(1)}, u32[]{:S(2)}, u32[]{:S(2)}) async-start(bf16[128,8,896]{2,1,0:T(8,128)(2,1)} %bitcast.12), calls=%async_computation.1 | async-start | bytes 3670016 | tf_op jit(solution)/shard_map/all_to_all | solution.py:438
  35.6 17.8 %batch_part.1 = (bf16[2048,2048]{1,0:T(8,128)(2,1)}, f32[2048,128]{1,0:T(8,128)}, f32[2048,512]{1,0:T(8,128)}) custom-call(s32[8,2048]{1,0:T(8,128)} %bitcast.19, s32[1,2048]{1,0:T(1,128)} %bitcast.15, bf16[2048,128]{1,0:T(8,128)(2,1)} %f_ref.1, bf16[2048,512]{1,0:T(8,128)(2,1)} %get-tuple-element.19.gs_ref.gs_hbm), custom_call_target="tpu_custom_call" | custom-call | tf_op jit(solution)/shard_map/batch_part/pallas_call | solution.py:246
  53.4 9.1 %all-to-all-done.1 = bf16[128,8,896]{2,1,0:T(8,128)(2,1)S(1)} async-done(((bf16[128,8,896]{2,1,0:T(8,128)(2,1)}), bf16[128,8,896]{2,1,0:T(8,128)(2,1)S(1)}, u32[]{:S(2)}, u32[]{:S(2)}) %all-to-all-start.1) | async-done | bytes 1835040 | tf_op jit(solution)/shard_map/all_to_all | solution.py:438
  62.5 19.6 %main_part.1 = (bf16[2048,512]{1,0:T(8,128)(2,1)}, bf16[512,512]{1,0:T(8,128)(2,1)}, bf16[1024,384]{1,0:T(8,128)(2,1)}) custom-call(bf16[1024,896]{1,0:T(8,128)(2,1)S(1)} %bitcast.10, bf16[512,2048]{1,0:T(8,128)(2,1)} %get-tuple-element.18.h_hbm, f32[2048,128]{1,0:T(8,128)} %get-tuple-element.20.cf_hbm, bf16[2048,2048]{1,0:T(8,128)(2,1)} %get-tuple-element.21.c_hbm, ...), custom_call_target="tpu_custom_call" | custom-call | tf_op jit(solution)/shard_map/main_part/pallas_call | solution.py:333
  82.1 21.1 %all_to_all.20.x_ref = bf16[128,8,384]{2,1,0:T(8,128)(2,1)S(1)} all-to-all(bf16[128,8,384]{2,1,0:T(8,128)(2,1)} %bitcast.13), channel_id=1, replica_groups=mesh['dp'=8,'mp'=16] {'dp','mp'}, dimensions={0} | all-to-all | bytes 1572864 | tf_op jit(solution)/shard_map/all_to_all | solution.py:438
  103.2 1.1 sum_part.1
  104.3 4.8 %all-to-all-start.3 = ((bf16[128,8,384]{2,1,0:T(8,128)(2,1)}), bf16[128,8,384]{2,1,0:T(8,128)(2,1)S(1)}, u32[]{:S(2)}, u32[]{:S(2)}) async-start(bf16[128,8,384]{2,1,0:T(8,128)(2,1)} %sum_part.1), calls=%async_computation.3 | async-start | bytes 1572864 | tf_op jit(solution)/shard_map/all_to_all | solution.py:438
  109.1 5.3 %tail_part.1 = (bf16[2048,512]{1,0:T(8,128)(2,1)}, bf16[2048,512]{1,0:T(8,128)(2,1)}) custom-call(bf16[2048,512]{1,0:T(8,128)(2,1)} %get-tuple-element.23.u_ref, bf16[512,512]{1,0:T(8,128)(2,1)} %w2_ref.3, s32[1,2048]{1,0:T(1,128)} %bitcast.17, s32[128,1,4]{2,1,0:T(1,128)S(1)} %all-to-all-done.ask_ref, bf16[512,512]{1,0:T(8,128)(2,1)} %get-tuple-element.24.pa_ref), custom_call_target="tpu_custom_call" | custom-call | tf_op jit(solution)/shard_map/tail_part/pallas_call | solution.py:381
  114.4 10.8 %all-to-all-done.3 = bf16[128,8,384]{2,1,0:T(8,128)(2,1)S(1)} async-done(((bf16[128,8,384]{2,1,0:T(8,128)(2,1)}), bf16[128,8,384]{2,1,0:T(8,128)(2,1)S(1)}, u32[]{:S(2)}, u32[]{:S(2)}) %all-to-all-start.3) | async-done | bytes 786464 | tf_op jit(solution)/shard_map/all_to_all | solution.py:438
  125.2 1.1 final_part.1
Async XLA Ops:
  2.0 21.0 %all-to-all-start = ((s32[128,1,4]{2,1,0:T(1,128)}), s32[128,1,4]{2,1,0:T(1,128)S(1)}, u32[]{:S(2)}, u32[]{:S(2)}) async-start(s32[128,1,4]{2,1,0:T(1,128)} %bitcast), calls=%async_computation | async-start | bytes 131072 | tf_op jit(solution)/shard_map/all_to_all | solution.py:438
  30.0 32.5 %all-to-all-start.1 = ((bf16[128,8,896]{2,1,0:T(8,128)(2,1)}), bf16[128,8,896]{2,1,0:T(8,128)(2,1)S(1)}, u32[]{:S(2)}, u32[]{:S(2)}) async-start(bf16[128,8,896]{2,1,0:T(8,128)(2,1)} %bitcast.12), calls=%async_computation.1 | async-start | bytes 3670016 | tf_op jit(solution)/shard_map/all_to_all | solution.py:438
  104.3 20.9 %all-to-all-start.3 = ((bf16[128,8,384]{2,1,0:T(8,128)(2,1)}), bf16[128,8,384]{2,1,0:T(8,128)(2,1)S(1)}, u32[]{:S(2)}, u32[]{:S(2)}) async-start(bf16[128,8,384]{2,1,0:T(8,128)(2,1)} %sum_part.1), calls=%async_computation.3 | async-start | bytes 1572864 | tf_op jit(solution)/shard_map/all_to_all | solution.py:438

commit v3 on v2

--- a/solution.py
+++ b/solution.py
@@ -219,7 +219,8 @@
 
 
 def batch_kernel(
-    nb_ref, bdeg_ref, f_ref, gs_ref, c_hbm, cf_ref, sp_hbm, fs_ref, c_ref, sp_ref, sems
+    nb_ref, bdeg_ref, f_ref, gs_ref, w2_ref, c_hbm, cf_ref, sp_hbm, bp_hbm,
+    fs_ref, c_ref, sp_ref, bp_ref, sems,
 ):
     col = columns(lax.rsqrt(bdeg_ref[...].astype(F32)))
     fs_ref[...] = (f_ref[...].astype(F32) * col).astype(BF)
@@ -234,92 +235,82 @@
     copies[0].start()
     for n, r in enumerate(range(0, NB, STEP)):
         at = slice(r, r + STEP)
-        sp_ref[at, :] = dot(c_ref[at, :], gs_ref[...])
-        copies.append(pltpu.make_async_copy(sp_ref.at[at], sp_hbm.at[at], sems.at[1 + n]))
-        copies[-1].start()
+        spread = dot(c_ref[at, :], gs_ref[...]).astype(BF)
+        sp_ref[at, :] = spread
+        bp_ref[at, :] = dot_t(spread, w2_ref[...])
+        for m, (src, dst) in enumerate(((sp_ref, sp_hbm), (bp_ref, bp_hbm))):
+            copies.append(pltpu.make_async_copy(src.at[at], dst.at[at], sems.at[1 + 2 * n + m]))
+            copies[-1].start()
         cf_ref[at, :] = dot_tl(c_ref[:, at], fs_ref[...])
     for copy in copies:
         copy.wait()
 
 
-def batch_call(nb, bdeg, f, gs):
+def batch_call(nb, bdeg, f, gs, w2):
     return pl.pallas_call(
         batch_kernel,
-        in_specs=[vmem_spec()] * 4,
-        out_specs=[hbm_spec(), vmem_spec(), hbm_spec()],
+        in_specs=[vmem_spec()] * 5,
+        out_specs=[hbm_spec(), vmem_spec(), hbm_spec(), hbm_spec()],
         out_shape=(
             pltpu.HBM((NB, NB), BF),
             pltpu.HBM((NB, FEAT), F32),
+            pltpu.HBM((NB, HID), BF),
             pltpu.HBM((NB, HID), F32),
         ),
         scratch_shapes=[
             pltpu.VMEM((NB, FEAT), BF),
             pltpu.VMEM((NB, NB), BF),
+            pltpu.VMEM((NB, HID), BF),
             pltpu.VMEM((NB, HID), F32),
-            pltpu.SemaphoreType.DMA((5,)),
+            pltpu.SemaphoreType.DMA((9,)),
         ],
         compiler_params=limit(58),
         name="batch_part",
-    )(nb, bdeg, f, gs)
+    )(nb, bdeg, f, gs, w2)
 
 
 def main_kernel(
-    r_ref, h_hbm, cf_hbm, c_hbm, sp_hbm, gs_hbm, w1_ref, w2_ref, bdeg_ref, hdeg_ref,
-    u_hbm, pa_ref, grads_ref,
-    h_ref, cf_ref, c_ref, sp_ref, gs_ref, u_ref,
-    hid_ref, der_ref, u1_ref, he_ref, hv_ref, g1_ref, g2_ref, sems,
-):
-    pairs = (
-        (h_hbm, h_ref), (cf_hbm, cf_ref), (c_hbm, c_ref), (gs_hbm, gs_ref), (sp_hbm, sp_ref),
-    )
+    r_ref, h_hbm, cf_hbm, sp_hbm, bp_hbm, p_ref, w1_ref, w2_ref, bdeg_ref, hdeg_ref,
+    hid_hbm, grads_ref,
+    h_ref, cf_ref, sp_ref, bp_ref, hid_ref, g1_ref, g2_ref, sems,
+):
+    pairs = ((h_hbm, h_ref), (cf_hbm, cf_ref), (bp_hbm, bp_ref), (sp_hbm, sp_ref))
     copies = [pltpu.make_async_copy(src, dst, sems.at[n]) for n, (src, dst) in enumerate(pairs)]
     for copy in copies[:2]:
         copy.start()
     inv = columns(lax.rsqrt(bdeg_ref[...].astype(F32)))
     col_h = columns(lax.rsqrt(hdeg_ref[...].astype(F32)))
+    hx, _ = part_up(r_ref[:, 512:640])
+    hx = (hx * col_h).astype(BF)
+    he, hv = part_up(r_ref[:, 0:512])
+    hvw = scale_rows(dot_t(hv.astype(BF), w2_ref[...]), col_h).astype(BF)
+    g2_ref[...] = dot_tl(he.astype(BF), p_ref[...])
     for copy in copies[:2]:
         copy.wait()
     for copy in copies[2:]:
         copy.start()
-    hx, p0 = part_up(r_ref[:, 512:640])
-    hx = (hx * col_h).astype(BF)
-    for s in range(0, NB, STEP):
-        col = inv[s : s + STEP]
-        u1 = (cf_ref[s : s + STEP, :] + dot_tl(h_ref[:, s : s + STEP], hx)).astype(BF)
-        u1_ref[s : s + STEP, :] = u1
+    outs = []
+    for n, s in enumerate(range(0, NB, STEP)):
+        at = slice(s, s + STEP)
+        col = inv[at]
+        h = h_ref[:, at]
+        u1 = (cf_ref[at, :] + dot_tl(h, hx)).astype(BF)
         pre = scale_rows(dot(u1, w1_ref[...]), col)
         sig = 0.5 + 0.5 * jnp.tanh(0.5 * pre)
-        hid_ref[s : s + STEP, :] = scale_rows(pre * sig, col).astype(BF)
-        der_ref[s : s + STEP, :] = scale_rows(sig * (1.0 + pre * (1.0 - sig)), col * col)
-    he, hv = part_up(r_ref[:, 0:512])
-    he_ref[...] = scale_rows(he, col_h).astype(BF)
-    hv_ref[...] = scale_rows(hv, col_h).astype(BF)
-    p1, p2 = part_up(r_ref[:, 640:768])
-    p3, _ = part_up(r_ref[:, 768:896])
-    pa_ref[:, 0:128] = p0.astype(BF)
-    pa_ref[:, 128:256] = p1.astype(BF)
-    pa_ref[:, 256:384] = p2.astype(BF)
-    pa_ref[:, 384:512] = p3.astype(BF)
-    for copy in copies[2:]:
-        copy.wait()
-    outs = []
-    for s in range(0, NB, STEP):
-        h = h_ref[:, s : s + STEP]
-        u = (dot_tl(c_ref[:, s : s + STEP], hid_ref[...]) + dot_tl(h, he_ref[...])).astype(BF)
-        at = slice(s, s + STEP)
-        u_ref[at, :] = u
-        outs.append(pltpu.make_async_copy(u_ref.at[at], u_hbm.at[at], sems.at[5 + s // STEP]))
+        hid_ref[at, :] = scale_rows(pre * sig, col).astype(BF)
+        outs.append(pltpu.make_async_copy(hid_ref.at[at], hid_hbm.at[at], sems.at[4 + n]))
         outs[-1].start()
-        spread = (sp_ref[s : s + STEP, :] + dot_tl(h, hv_ref[...])).astype(BF)
-        d_pre = (dot_t(spread, w2_ref[...]) * der_ref[s : s + STEP, :]).astype(BF)
-        g2 = dot_tl(u, gs_ref[s : s + STEP, :])
-        g1 = dot_tl(u1_ref[s : s + STEP, :], d_pre)
-        if s == 0:
+        der = scale_rows(sig * (1.0 + pre * (1.0 - sig)), col * col)
+        if n == 0:
+            copies[2].wait()
+        d_pre = ((bp_ref[at, :] + dot_tl(h, hvw)) * der).astype(BF)
+        g1 = dot_tl(u1, d_pre)
+        if n == 0:
+            copies[3].wait()
             g1_ref[...] = g1
-            g2_ref[...] = g2
         else:
             g1_ref[...] += g1
-            g2_ref[...] += g2
+    g2_ref[...] += dot_tl(hid_ref[...], sp_ref[...])
     grads_ref[0:512, 0:256] = g2_ref[:, 0:256].astype(BF)
     grads_ref[512:1024, 0:256] = g2_ref[:, 256:512].astype(BF)
     for q in range(4):
@@ -329,72 +320,104 @@
         copy.wait()
 
 
-def main_call(recv, c, h, cf, sp, gs, w1, w2, bdeg, hdeg):
+def main_call(recv, h, cf, sp, bp, p, w1, w2, bdeg, hdeg):
     return pl.pallas_call(
         main_kernel,
-        in_specs=[vmem_spec()] + [hbm_spec()] * 5 + [vmem_spec()] * 4,
-        out_specs=[hbm_spec(), vmem_spec(), vmem_spec()],
-        out_shape=(
-            pltpu.HBM((NB, HID), BF),
-            pltpu.HBM((NH, HID), BF),
-            jax.ShapeDtypeStruct((1024, 384), BF),
-        ),
+        in_specs=[vmem_spec()] + [hbm_spec()] * 4 + [vmem_spec()] * 5,
+        out_specs=[hbm_spec(), vmem_spec()],
+        out_shape=(pltpu.HBM((NB, HID), BF), jax.ShapeDtypeStruct((1024, 384), BF)),
         scratch_shapes=[
             pltpu.VMEM((NH, NB), BF),
             pltpu.VMEM((NB, FEAT), F32),
-            pltpu.VMEM((NB, NB), BF),
+            pltpu.VMEM((NB, HID), BF),
             pltpu.VMEM((NB, HID), F32),
             pltpu.VMEM((NB, HID), BF),
-            pltpu.VMEM((NB, HID), BF),
-            pltpu.VMEM((NB, HID), BF),
-            pltpu.VMEM((NB, HID), F32),
-            pltpu.VMEM((NB, FEAT), BF),
-            pltpu.VMEM((NH, HID), BF),
-            pltpu.VMEM((NH, HID), BF),
             pltpu.VMEM((FEAT, HID), F32),
             pltpu.VMEM((HID, HID), F32),
-            pltpu.SemaphoreType.DMA((10,)),
+            pltpu.SemaphoreType.DMA((8,)),
         ],
         compiler_params=limit(58),
         name="main_part",
-    )(keep(recv), leave(h), leave(cf), leave(c), leave(sp), leave(gs), w1, w2, bdeg, hdeg)
-
-
-def tail_kernel(
-    u_ref, w2_ref, bdeg_ref, ask_ref, pa_ref, out_hbm, hg_hbm, s_ref, out_ref, hg_ref, sems
-):
+    )(keep(recv), leave(h), leave(cf), leave(sp), leave(bp), keep(p), w1, w2, bdeg, hdeg)
+
+
+def out_kernel(
+    r_ref, c_hbm, h_hbm, hid_ref, w2_ref, bdeg_ref, hdeg_ref, out_hbm,
+    c_ref, h_ref, he_ref, out_ref, sems,
+):
+    ins = [
+        pltpu.make_async_copy(c_hbm, c_ref, sems.at[0]),
+        pltpu.make_async_copy(h_hbm, h_ref, sems.at[1]),
+    ]
+    for copy in ins:
+        copy.start()
+    inv = columns(lax.rsqrt(bdeg_ref[...].astype(F32)))
+    col_h = columns(lax.rsqrt(hdeg_ref[...].astype(F32)))
+    he, _ = part_up(r_ref[:, 0:512])
+    he_ref[...] = scale_rows(he, col_h).astype(BF)
+    for copy in ins:
+        copy.wait()
+    outs = []
+    for n, s in enumerate(range(0, NB, STEP)):
+        at = slice(s, s + STEP)
+        u = dot_tl(c_ref[:, at], hid_ref[...]) + dot_tl(h_ref[:, at], he_ref[...])
+        out_ref[at] = scale_rows(dot(u.astype(BF), w2_ref[...]), inv[at]).astype(BF)
+        outs.append(pltpu.make_async_copy(out_ref.at[at], out_hbm.at[at], sems.at[2 + n]))
+        outs[-1].start()
+    for copy in outs:
+        copy.wait()
+
+
+def out_call(recv, c, h, hid, w2, bdeg, hdeg):
+    return pl.pallas_call(
+        out_kernel,
+        in_specs=[vmem_spec(), hbm_spec(), hbm_spec()] + [vmem_spec()] * 4,
+        out_specs=hbm_spec(),
+        out_shape=jax.ShapeDtypeStruct((NB, HID), BF),
+        scratch_shapes=[
+            pltpu.VMEM((NB, NB), BF),
+            pltpu.VMEM((NH, NB), BF),
+            pltpu.VMEM((NH, HID), BF),
+            pltpu.VMEM((NB, HID), BF),
+            pltpu.SemaphoreType.DMA((6,)),
+        ],
+        compiler_params=limit(58),
+        name="out_part",
+    )(keep(recv), leave(c), leave(h), hid, w2, bdeg, hdeg)
+
+
+def tail_kernel(ask_ref, r_ref, hg_hbm, s_ref, pa_ref, hg_ref, sems):
     selector(ask_ref, s_ref)
-    col = columns(lax.rsqrt(bdeg_ref[...].astype(F32)))
+    _, p0 = part_up(r_ref[:, 512:640])
+    p1, p2 = part_up(r_ref[:, 640:768])
+    p3, _ = part_up(r_ref[:, 768:896])
+    for q, part in enumerate((p0, p1, p2, p3)):
+        pa_ref[:, 128 * q : 128 * q + 128] = part.astype(BF)
     copies = []
     for n, r in enumerate(range(0, NB, STEP)):
         at = slice(r, r + STEP)
-        out_ref[at] = scale_rows(dot(u_ref[at], w2_ref[...]), col[at]).astype(BF)
         hg_ref[at] = dot_tl(s_ref[:, at], pa_ref[...]).astype(BF)
-        for m, (src, dst) in enumerate(((out_ref, out_hbm), (hg_ref, hg_hbm))):
-            copies.append(pltpu.make_async_copy(src.at[at], dst.at[at], sems.at[2 * n + m]))
-            copies[-1].start()
+        copies.append(pltpu.make_async_copy(hg_ref.at[at], hg_hbm.at[at], sems.at[n]))
+        copies[-1].start()
     for copy in copies:
         copy.wait()
 
 
-def tail_call(u, w2, bdeg, asked, pa):
+def tail_call(asked, recv):
     return pl.pallas_call(
         tail_kernel,
-        in_specs=[vmem_spec()] * 5,
-        out_specs=[hbm_spec()] * 2,
-        out_shape=(
-            jax.ShapeDtypeStruct((NB, HID), BF),
-            jax.ShapeDtypeStruct((NB, HID), BF),
-        ),
+        in_specs=[vmem_spec()] * 2,
+        out_specs=hbm_spec(),
+        out_shape=jax.ShapeDtypeStruct((NB, HID), BF),
         scratch_shapes=[
             pltpu.VMEM((NH, NB), BF),
-            pltpu.VMEM((NB, HID), BF),
-            pltpu.VMEM((NB, HID), BF),
-            pltpu.SemaphoreType.DMA((8,)),
+            pltpu.VMEM((NH, HID), BF),
+            pltpu.VMEM((NB, HID), BF),
+            pltpu.SemaphoreType.DMA((4,)),
         ],
         compiler_params=limit(58),
         name="tail_part",
-    )(u, w2, bdeg, keep(asked), pa)
+    )(keep(asked), keep(recv))
 
 
 def sum_kernel(x_ref, o_ref):
@@ -448,11 +471,13 @@
     h, gs, p = halo_call(halo_nbrs.T, halo_len.reshape(1, NB), bdeg, hdeg, grad_out)
     send = pick_call(asked, feat_table, emb_table, grad_table, p)
     recv = exchange(send.reshape(128, 8, 896)).reshape(1024, 896)
-    c, cf, sp = batch_call(batch_nbrs.T, bdeg, node_feats, gs)
-    u, pa, grads = main_call(recv, c, h, cf, sp, gs, weight_one, weight_two, bdeg, hdeg)
+    c, cf, sp, bp = batch_call(batch_nbrs.T, bdeg, node_feats, gs, weight_two)
+    hid, grads = main_call(recv, h, cf, sp, bp, p, weight_one, weight_two, bdeg, hdeg)
     shares = exchange(grads.reshape(128, 8, 384))
-    out_embed, halo_grad = tail_call(u, weight_two, bdeg, asked, pa)
+    out_embed = out_call(recv, c, h, hid, weight_two, bdeg, hdeg)
+    shares, out_embed = lax.optimization_barrier((shares, out_embed))
     sums = exchange(sum_call(shares)).reshape(1024, 384)
+    halo_grad = tail_call(asked, recv)
     grad_one, grad_two = final_call(sums)
     return out_embed, halo_grad, grad_one, grad_two
 

time: 127 us -> 121 us (0.953)
  blocking collectives: 21.1 us -> 0 us
  starting transfers between devices: 21.9 us -> 28.9 us
  Pallas kernels: 57.2 us -> 63.3 us
  waiting for transfers between devices: 24.1 us -> 26.4 us
    all_to_all x1 -> x0, blocking collectives: 21.1 us -> none  [exchange(): return lax.all_to_all(x, AXES, split_axis=0, concat_axis=0, tiled=True)]
    all_to_all x3 -> x4, starting transfers between devices: 21.9 us -> 28.9 us  [exchange(): return lax.all_to_all(x, AXES, split_axis=0, concat_axis=0, tiled=True)]
    pallas_call x3 -> x4, Pallas kernels: 42.8 us -> 48.9 us  [the longest x1 20.9 us: batch_call(): pl.pallas_call(batch_kernel, in_specs=[vmem_spec()] * 5, out_specs=[hbm_s...]
    all_to_all x3 -> x4, waiting for transfers between devices: 24.1 us -> 26.4 us  [exchange(): return lax.all_to_all(x, AXES, split_axis=0, concat_axis=0, tiled=True)]
  transfers between devices with their start and end apart: 3 -> 4, of which waited for: 3 -> 4; matrix products, arithmetic and copies ran while one was open for 0% -> 0% of each run, Pallas kernels for 23% -> 35%
where the time goes in v3:
time: 121 us
  Pallas kernels  63.3 us (52%)
  starting transfers between devices  28.9 us (24%)
  waiting for transfers between devices  26.4 us (22%)
  local copies, waits for them, and re-layouts  1.42 us (1%)
    all_to_all x4, starting transfers between devices, exchange(): return lax.all_to_all(x, AXES, split_axis=0, concat_axis=0, tiled=True)  28.9 us
    all_to_all x4, waiting for transfers between devices, exchange(): return lax.all_to_all(x, AXES, split_axis=0, concat_axis=0, tiled=True)  26.4 us
    pallas_call x1, Pallas kernels, batch_call(): pl.pallas_call(batch_kernel, in_specs=[vmem_spec()] * 5, out_specs=[hbm_s...  20.9 us
    pallas_call x1, Pallas kernels, out_call(): pl.pallas_call(out_kernel, in_specs=[vmem_spec(), hbm_spec(), hbm_spec()]...  13.3 us
    pallas_call x1, Pallas kernels, main_call(): pl.pallas_call(main_kernel, in_specs=[vmem_spec()] + [hbm_spec()] * 4 + [...  12.1 us
    pallas_call x1, Pallas kernels, pick_call(): pl.pallas_call(pick_kernel, in_specs=[vmem_spec(), hbm_spec(), hbm_spec()...  6.88 us
    pallas_call x1, Pallas kernels, halo_call(): pl.pallas_call(halo_kernel, in_specs=[vmem_spec()] * 4 + [hbm_spec()], ou...  5.35 us
    pallas_call x1, Pallas kernels, tail_call(): pl.pallas_call(tail_kernel, in_specs=[vmem_spec()] * 2, out_specs=hbm_spe...  2.63 us
  transfers between devices with their start and end apart: 4, of which 4 were waited for; matrix products, arithmetic and copies ran while one was open for 0% of the time, Pallas kernels for 35%

profile of v3, /device:TPU:1, one launch (start us, length us, event | category | flops | bytes accessed | tf_op | source)
XLA Modules:
  0.0 120.8 jit_solution(5567294309593591259)
XLA Ops:
  0.6 1.4 %reshape.32 = s32[128,1,4]{2,0,1:T(8,128)} reshape(s32[512]{0:T(512)} %param.18) | data formatting | bytes 4096 | tf_op jit(solution)/shard_map/reshape | solution.py:470
  2.0 11.5 %all-to-all-start = ((s32[128,1,4]{2,1,0:T(1,128)}), s32[128,1,4]{2,1,0:T(1,128)S(1)}, u32[]{:S(2)}, u32[]{:S(2)}) async-start(s32[128,1,4]{2,1,0:T(1,128)} %bitcast), calls=%async_computation | async-start | bytes 131072 | tf_op jit(solution)/shard_map/all_to_all | solution.py:461
  13.5 5.4 %halo_part.1 = (bf16[512,2048]{1,0:T(8,128)(2,1)}, bf16[2048,512]{1,0:T(8,128)(2,1)}, bf16[512,512]{1,0:T(8,128)(2,1)S(1)}) custom-call(s32[8,2048]{1,0:T(8,128)} %bitcast.20, s32[1,2048]{1,0:T(1,128)} %bitcast.25, s32[1,2048]{1,0:T(1,128)} %bitcast.16, s32[1,512]{1,0:T(1,128)} %bitcast.22, bf16[2048,512]{1,0:T(8,128)(2,1)} %g_hbm.1), custom_call_target="tpu_custom_call" | custom-call | tf_op jit(solution)/shard_map/halo_part/pallas_call | solution.py:119
  18.9 4.2 %all-to-all-done.ask_ref = s32[128,1,4]{2,1,0:T(1,128)S(1)} async-done(((s32[128,1,4]{2,1,0:T(1,128)}), s32[128,1,4]{2,1,0:T(1,128)S(1)}, u32[]{:S(2)}, u32[]{:S(2)}) %all-to-all-start) | async-done | bytes 2080 | tf_op jit(solution)/shard_map/all_to_all | solution.py:461
  23.1 6.9 %pick_rows.1 = bf16[1024,896]{1,0:T(8,128)(2,1)} custom-call(s32[128,1,4]{2,1,0:T(1,128)S(1)} %all-to-all-done.ask_ref, bf16[2048,128]{1,0:T(8,128)(2,1)} %x_hbm.1, bf16[2048,512]{1,0:T(8,128)(2,1)} %e_hbm.1, bf16[2048,512]{1,0:T(8,128)(2,1)} %v_hbm.1, bf16[512,512]{1,0:T(8,128)(2,1)S(1)} %get-tuple-element.17.p_ref), custom_call_target="tpu_custom_call" | custom-call | tf_op jit(solution)/shard_map/pick_rows/pallas_call | solution.py:203
  30.0 5.6 %all-to-all-start.1 = ((bf16[128,8,896]{2,1,0:T(8,128)(2,1)}), bf16[128,8,896]{2,1,0:T(8,128)(2,1)S(1)}, u32[]{:S(2)}, u32[]{:S(2)}) async-start(bf16[128,8,896]{2,1,0:T(8,128)(2,1)} %bitcast.14), calls=%async_computation.1 | async-start | bytes 3670016 | tf_op jit(solution)/shard_map/all_to_all | solution.py:461
  35.6 20.9 %batch_part.1 = (bf16[2048,2048]{1,0:T(8,128)(2,1)}, f32[2048,128]{1,0:T(8,128)}, bf16[2048,512]{1,0:T(8,128)(2,1)}, f32[2048,512]{1,0:T(8,128)}) custom-call(s32[8,2048]{1,0:T(8,128)} %bitcast.21, s32[1,2048]{1,0:T(1,128)} %bitcast.17, bf16[2048,128]{1,0:T(8,128)(2,1)} %f_ref.1, bf16[2048,512]{1,0:T(8,128)(2,1)} %get-tuple-element.19.gs_ref, ...), custom_call_target="tpu_custom_call" | custom-call | tf_op jit(solution)/shard_map/batch_part/pallas_call | solution.py:250
  56.5 6.0 %all-to-all-done.1 = bf16[128,8,896]{2,1,0:T(8,128)(2,1)S(1)} async-done(((bf16[128,8,896]{2,1,0:T(8,128)(2,1)}), bf16[128,8,896]{2,1,0:T(8,128)(2,1)S(1)}, u32[]{:S(2)}, u32[]{:S(2)}) %all-to-all-start.1) | async-done | bytes 1835040 | tf_op jit(solution)/shard_map/all_to_all | solution.py:461
  62.5 12.1 %main_part.1 = (bf16[2048,512]{1,0:T(8,128)(2,1)}, bf16[1024,384]{1,0:T(8,128)(2,1)}) custom-call(bf16[1024,896]{1,0:T(8,128)(2,1)S(1)} %bitcast.10, bf16[512,2048]{1,0:T(8,128)(2,1)} %get-tuple-element.18.h_hbm, f32[2048,128]{1,0:T(8,128)} %get-tuple-element.20.cf_hbm, bf16[2048,512]{1,0:T(8,128)(2,1)} %get-tuple-element.21.sp_hbm, ...), custom_call_target="tpu_custom_call" | custom-call | tf_op jit(solution)/shard_map/main_part/pallas_call | solution.py:324
  74.6 4.7 %all-to-all-start.2 = ((bf16[128,8,384]{2,1,0:T(8,128)(2,1)}), bf16[128,8,384]{2,1,0:T(8,128)(2,1)S(1)}, u32[]{:S(2)}, u32[]{:S(2)}) async-start(bf16[128,8,384]{2,1,0:T(8,128)(2,1)} %bitcast.15), calls=%async_computation.2 | async-start | bytes 1572864 | tf_op jit(solution)/shard_map/all_to_all | solution.py:461
  79.3 13.3 %out_part.1 = bf16[2048,512]{1,0:T(8,128)(2,1)} custom-call(bf16[1024,896]{1,0:T(8,128)(2,1)S(1)} %bitcast.11, bf16[2048,2048]{1,0:T(8,128)(2,1)} %get-tuple-element.24.c_hbm, bf16[512,2048]{1,0:T(8,128)(2,1)} %get-tuple-element.18.h_hbm, bf16[2048,512]{1,0:T(8,128)(2,1)} %get-tuple-element.25.hid_ref, bf16[512,512]{1,0:T(8,128)(2,1)} %w2_ref.5, ...), custom_call_target="tpu_custom_call" | custom-call | tf_op jit(solution)/shard_map/out_part/pallas_call | solution.py:372
  92.6 2.8 %all-to-all-done.2.x_ref = bf16[128,8,384]{2,1,0:T(8,128)(2,1)S(1)} async-done(((bf16[128,8,384]{2,1,0:T(8,128)(2,1)}), bf16[128,8,384]{2,1,0:T(8,128)(2,1)S(1)}, u32[]{:S(2)}, u32[]{:S(2)}) %all-to-all-start.2) | async-done | bytes 786464 | tf_op jit(solution)/shard_map/all_to_all | solution.py:461
  95.4 1.1 sum_part.1
  96.5 7.1 %all-to-all-start.3 = ((bf16[128,8,384]{2,1,0:T(8,128)(2,1)}), bf16[128,8,384]{2,1,0:T(8,128)(2,1)S(1)}, u32[]{:S(2)}, u32[]{:S(2)}) async-start(bf16[128,8,384]{2,1,0:T(8,128)(2,1)} %sum_part.1), calls=%async_computation.3 | async-start | bytes 1572864 | tf_op jit(solution)/shard_map/all_to_all | solution.py:461
  103.6 2.6 %tail_part.1 = bf16[2048,512]{1,0:T(8,128)(2,1)} custom-call(s32[128,1,4]{2,1,0:T(1,128)S(1)} %all-to-all-done.ask_ref, bf16[1024,896]{1,0:T(8,128)(2,1)S(1)} %bitcast.12), custom_call_target="tpu_custom_call" | custom-call | tf_op jit(solution)/shard_map/tail_part/pallas_call | solution.py:407
  106.3 13.4 %all-to-all-done.3 = bf16[128,8,384]{2,1,0:T(8,128)(2,1)S(1)} async-done(((bf16[128,8,384]{2,1,0:T(8,128)(2,1)}), bf16[128,8,384]{2,1,0:T(8,128)(2,1)S(1)}, u32[]{:S(2)}, u32[]{:S(2)}) %all-to-all-start.3) | async-done | bytes 786464 | tf_op jit(solution)/shard_map/all_to_all | solution.py:461
  119.6 1.1 final_part.1
Async XLA Ops:
  2.0 21.0 %all-to-all-start = ((s32[128,1,4]{2,1,0:T(1,128)}), s32[128,1,4]{2,1,0:T(1,128)S(1)}, u32[]{:S(2)}, u32[]{:S(2)}) async-start(s32[128,1,4]{2,1,0:T(1,128)} %bitcast), calls=%async_computation | async-start | bytes 131072 | tf_op jit(solution)/shard_map/all_to_all | solution.py:461
  30.0 32.5 %all-to-all-start.1 = ((bf16[128,8,896]{2,1,0:T(8,128)(2,1)}), bf16[128,8,896]{2,1,0:T(8,128)(2,1)S(1)}, u32[]{:S(2)}, u32[]{:S(2)}) async-start(bf16[128,8,896]{2,1,0:T(8,128)(2,1)} %bitcast.14), calls=%async_computation.1 | async-start | bytes 3670016 | tf_op jit(solution)/shard_map/all_to_all | solution.py:461
  74.6 20.9 %all-to-all-start.2 = ((bf16[128,8,384]{2,1,0:T(8,128)(2,1)}), bf16[128,8,384]{2,1,0:T(8,128)(2,1)S(1)}, u32[]{:S(2)}, u32[]{:S(2)}) async-start(bf16[128,8,384]{2,1,0:T(8,128)(2,1)} %bitcast.15), calls=%async_computation.2 | async-start | bytes 1572864 | tf_op jit(solution)/shard_map/all_to_all | solution.py:461
  96.5 23.1 %all-to-all-start.3 = ((bf16[128,8,384]{2,1,0:T(8,128)(2,1)}), bf16[128,8,384]{2,1,0:T(8,128)(2,1)S(1)}, u32[]{:S(2)}, u32[]{:S(2)}) async-start(bf16[128,8,384]{2,1,0:T(8,128)(2,1)} %sum_part.1), calls=%async_computation.3 | async-start | bytes 1572864 | tf_op jit(solution)/shard_map/all_to_all | solution.py:461

commit v4 on v3

--- a/solution.py
+++ b/solution.py
@@ -136,24 +136,12 @@
     )(hn, hl, bdeg, hdeg, leave(g))
 
 
-def pair_up(top, bottom):
-    w = top.shape[1]
-    t = top.reshape(64, 8, w)
-    b = bottom.reshape(64, 8, w)
-    low = lax.broadcasted_iota(jnp.int32, (64, 8, w), 1) < 4
-    even = jnp.where(low, t, pltpu.roll(b, 4, 1))
-    odd = jnp.where(low, pltpu.roll(t, 4, 1), b)
-    return jnp.concatenate([even, odd], axis=1).astype(BF).reshape(1024, w)
-
-
-def part_up(both):
-    w = both.shape[1]
-    x = both.reshape(64, 16, w).astype(F32)
-    even, odd = x[:, 0:8], x[:, 8:16]
-    low = lax.broadcasted_iota(jnp.int32, (64, 8, w), 1) < 4
-    top = jnp.where(low, even, pltpu.roll(odd, 4, 1))
-    bottom = jnp.where(low, pltpu.roll(even, 4, 1), odd)
-    return top.reshape(512, w), bottom.reshape(512, w)
+def rows_of(ref, lo, hi):
+    return ref[:, :, lo:hi].reshape(NH, hi - lo)
+
+
+def chunks_of(x):
+    return x.astype(BF).reshape(x.shape[0] // 4, 4, x.shape[1])
 
 
 def selector(ask_ref, s_ref):
@@ -180,23 +168,20 @@
     ]
     for copy in copies:
         copy.start()
+    out_ref[:, :, 1152:1664] = chunks_of(p_ref[...])
     selector(ask_ref, s_ref)
     s = s_ref[...]
-    copies[0].wait()
-    picked = dot(s, e_ref[...])
-    copies[1].wait()
-    out_ref[:, 0:512] = pair_up(picked, dot(s, v_ref[...]))
-    left = pltpu.make_async_copy(out_ref.at[:, 0:512], out_hbm.at[:, 0:512], sems.at[3])
-    left.start()
-    copies[2].wait()
-    p = p_ref[...].astype(F32)
-    out_ref[:, 512:640] = pair_up(dot(s, x_ref[...]), p[:, 0:128])
-    out_ref[:, 640:768] = pair_up(p[:, 128:256], p[:, 256:384])
-    out_ref[:, 768:896] = pair_up(p[:, 384:512], p[:, 384:512])
-    right = pltpu.make_async_copy(out_ref.at[:, 512:896], out_hbm.at[:, 512:896], sems.at[4])
-    right.start()
-    left.wait()
-    right.wait()
+    sends = []
+    for n, (lo, hi, src) in enumerate(((128, 640, e_ref), (640, 1152, v_ref), (0, 128, x_ref))):
+        copies[n].wait()
+        out_ref[:, :, lo:hi] = chunks_of(dot(s, src[...]))
+        if n == 1:
+            hi = 1664
+        at = (slice(None), slice(None), slice(lo, hi))
+        sends.append(pltpu.make_async_copy(out_ref.at[at], out_hbm.at[at], sems.at[3 + n]))
+        sends[-1].start()
+    for copy in sends:
+        copy.wait()
 
 
 def pick_call(asked, x, e, v, p):
@@ -204,14 +189,14 @@
         pick_kernel,
         in_specs=[vmem_spec(), hbm_spec(), hbm_spec(), hbm_spec(), vmem_spec()],
         out_specs=hbm_spec(),
-        out_shape=pltpu.HBM((1024, 896), BF),
+        out_shape=pltpu.HBM((128, 4, 1664), BF),
         scratch_shapes=[
             pltpu.VMEM((NH, NB), BF),
             pltpu.VMEM((NB, FEAT), BF),
             pltpu.VMEM((NB, HID), BF),
             pltpu.VMEM((NB, HID), BF),
-            pltpu.VMEM((1024, 896), BF),
-            pltpu.SemaphoreType.DMA((5,)),
+            pltpu.VMEM((128, 4, 1664), BF),
+            pltpu.SemaphoreType.DMA((6,)),
         ],
         compiler_params=limit(58),
         name="pick_rows",
@@ -280,11 +265,9 @@
         copy.start()
     inv = columns(lax.rsqrt(bdeg_ref[...].astype(F32)))
     col_h = columns(lax.rsqrt(hdeg_ref[...].astype(F32)))
-    hx, _ = part_up(r_ref[:, 512:640])
-    hx = (hx * col_h).astype(BF)
-    he, hv = part_up(r_ref[:, 0:512])
-    hvw = scale_rows(dot_t(hv.astype(BF), w2_ref[...]), col_h).astype(BF)
-    g2_ref[...] = dot_tl(he.astype(BF), p_ref[...])
+    hx = (rows_of(r_ref, 0, 128).astype(F32) * col_h).astype(BF)
+    hvw = scale_rows(dot_t(rows_of(r_ref, 640, 1152), w2_ref[...]), col_h).astype(BF)
+    g2_ref[...] = dot_tl(rows_of(r_ref, 128, 640), p_ref[...])
     for copy in copies[:2]:
         copy.wait()
     for copy in copies[2:]:
@@ -311,11 +294,10 @@
         else:
             g1_ref[...] += g1
     g2_ref[...] += dot_tl(hid_ref[...], sp_ref[...])
-    grads_ref[0:512, 0:256] = g2_ref[:, 0:256].astype(BF)
-    grads_ref[512:1024, 0:256] = g2_ref[:, 256:512].astype(BF)
+    grads_ref[:, :, 0:512] = chunks_of(g2_ref[...])
     for q in range(4):
-        grads_ref[128 * q : 128 * q + 128, 256:384] = g1_ref[:, 128 * q : 128 * q + 128].astype(BF)
-    grads_ref[512:1024, 256:384] = jnp.zeros((512, 128), BF)
+        part = g1_ref[:, 128 * q : 128 * q + 128]
+        grads_ref[32 * q : 32 * q + 32, :, 512:640] = chunks_of(part)
     for copy in outs:
         copy.wait()
 
@@ -325,7 +307,7 @@
         main_kernel,
         in_specs=[vmem_spec()] + [hbm_spec()] * 4 + [vmem_spec()] * 5,
         out_specs=[hbm_spec(), vmem_spec()],
-        out_shape=(pltpu.HBM((NB, HID), BF), jax.ShapeDtypeStruct((1024, 384), BF)),
+        out_shape=(pltpu.HBM((NB, HID), BF), jax.ShapeDtypeStruct((128, 4, 640), BF)),
         scratch_shapes=[
             pltpu.VMEM((NH, NB), BF),
             pltpu.VMEM((NB, FEAT), F32),
@@ -341,58 +323,55 @@
     )(keep(recv), leave(h), leave(cf), leave(sp), leave(bp), keep(p), w1, w2, bdeg, hdeg)
 
 
-def out_kernel(
-    r_ref, c_hbm, h_hbm, hid_ref, w2_ref, bdeg_ref, hdeg_ref, out_hbm,
-    c_ref, h_ref, he_ref, out_ref, sems,
-):
+def out_kernel(half, refs):
+    r_ref, c_hbm, h_hbm, hid_ref, w2_ref, bdeg_ref, hdeg_ref = refs[:7]
+    out_hbm, c_ref, h_ref, he_ref, out_ref, sems = refs[-6:]
+    at = slice(half * NB // 2, (half + 1) * NB // 2)
     ins = [
-        pltpu.make_async_copy(c_hbm, c_ref, sems.at[0]),
-        pltpu.make_async_copy(h_hbm, h_ref, sems.at[1]),
+        pltpu.make_async_copy(c_hbm.at[:, at], c_ref, sems.at[0]),
+        pltpu.make_async_copy(h_hbm.at[:, at], h_ref, sems.at[1]),
     ]
     for copy in ins:
         copy.start()
-    inv = columns(lax.rsqrt(bdeg_ref[...].astype(F32)))
+    inv = columns(lax.rsqrt(bdeg_ref[:, at].astype(F32)))
     col_h = columns(lax.rsqrt(hdeg_ref[...].astype(F32)))
-    he, _ = part_up(r_ref[:, 0:512])
-    he_ref[...] = scale_rows(he, col_h).astype(BF)
+    he_ref[...] = scale_rows(rows_of(r_ref, 128, 640).astype(F32), col_h).astype(BF)
     for copy in ins:
         copy.wait()
     outs = []
-    for n, s in enumerate(range(0, NB, STEP)):
-        at = slice(s, s + STEP)
-        u = dot_tl(c_ref[:, at], hid_ref[...]) + dot_tl(h_ref[:, at], he_ref[...])
-        out_ref[at] = scale_rows(dot(u.astype(BF), w2_ref[...]), inv[at]).astype(BF)
-        outs.append(pltpu.make_async_copy(out_ref.at[at], out_hbm.at[at], sems.at[2 + n]))
+    for n, s in enumerate(range(0, NB // 2, STEP)):
+        here = slice(s, s + STEP)
+        there = slice(at.start + s, at.start + s + STEP)
+        u = dot_tl(c_ref[:, here], hid_ref[...]) + dot_tl(h_ref[:, here], he_ref[...])
+        out_ref[here] = scale_rows(dot(u.astype(BF), w2_ref[...]), inv[here]).astype(BF)
+        outs.append(pltpu.make_async_copy(out_ref.at[here], out_hbm.at[there], sems.at[2 + n]))
         outs[-1].start()
     for copy in outs:
         copy.wait()
 
 
-def out_call(recv, c, h, hid, w2, bdeg, hdeg):
-    return pl.pallas_call(
-        out_kernel,
-        in_specs=[vmem_spec(), hbm_spec(), hbm_spec()] + [vmem_spec()] * 4,
+def out_call(half, recv, c, h, hid, w2, bdeg, hdeg, *first):
+    return pl.pallas_call(
+        lambda *refs: out_kernel(half, refs),
+        in_specs=[vmem_spec(), hbm_spec(), hbm_spec()] + [vmem_spec()] * 4 + [hbm_spec()] * len(first),
         out_specs=hbm_spec(),
-        out_shape=jax.ShapeDtypeStruct((NB, HID), BF),
-        scratch_shapes=[
-            pltpu.VMEM((NB, NB), BF),
-            pltpu.VMEM((NH, NB), BF),
+        out_shape=pltpu.HBM((NB, HID), BF),
+        input_output_aliases={7: 0} if first else {},
+        scratch_shapes=[
+            pltpu.VMEM((NB, NB // 2), BF),
+            pltpu.VMEM((NH, NB // 2), BF),
             pltpu.VMEM((NH, HID), BF),
-            pltpu.VMEM((NB, HID), BF),
-            pltpu.SemaphoreType.DMA((6,)),
-        ],
-        compiler_params=limit(58),
-        name="out_part",
-    )(keep(recv), leave(c), leave(h), hid, w2, bdeg, hdeg)
+            pltpu.VMEM((NB // 2, HID), BF),
+            pltpu.SemaphoreType.DMA((4,)),
+        ],
+        compiler_params=limit(58),
+        name=f"out_part_{half}",
+    )(keep(recv), leave(c), leave(h), hid, w2, bdeg, hdeg, *first)
 
 
 def tail_kernel(ask_ref, r_ref, hg_hbm, s_ref, pa_ref, hg_ref, sems):
     selector(ask_ref, s_ref)
-    _, p0 = part_up(r_ref[:, 512:640])
-    p1, p2 = part_up(r_ref[:, 640:768])
-    p3, _ = part_up(r_ref[:, 768:896])
-    for q, part in enumerate((p0, p1, p2, p3)):
-        pa_ref[:, 128 * q : 128 * q + 128] = part.astype(BF)
+    pa_ref[...] = rows_of(r_ref, 1152, 1664)
     copies = []
     for n, r in enumerate(range(0, NB, STEP)):
         at = slice(r, r + STEP)
@@ -422,7 +401,7 @@
 
 def sum_kernel(x_ref, o_ref):
     total = jnp.sum(x_ref[...].astype(F32), axis=0)
-    o_ref[...] = jnp.broadcast_to(total.astype(BF)[None], (128, 8, 384))
+    o_ref[...] = jnp.broadcast_to(total.astype(BF)[None], (128, 4, 640))
 
 
 def sum_call(x):
@@ -430,18 +409,17 @@
         sum_kernel,
         in_specs=[vmem_spec()],
         out_specs=vmem_spec(),
-        out_shape=jax.ShapeDtypeStruct((128, 8, 384), BF),
+        out_shape=jax.ShapeDtypeStruct((128, 4, 640), BF),
         name="sum_part",
     )(keep(x))
 
 
 def final_kernel(x_ref, g1_ref, g2_ref):
     factor = 1.0 / 512.0
-    g2_ref[:, 0:256] = x_ref[0:512, 0:256].astype(F32) * factor
-    g2_ref[:, 256:512] = x_ref[512:1024, 0:256].astype(F32) * factor
+    g2_ref[...] = rows_of(x_ref, 0, 512).astype(F32) * factor
     for q in range(4):
-        part = x_ref[128 * q : 128 * q + 128, 256:384].astype(F32)
-        g1_ref[:, 128 * q : 128 * q + 128] = part * factor
+        part = x_ref[32 * q : 32 * q + 32, :, 512:640].reshape(128, 128)
+        g1_ref[:, 128 * q : 128 * q + 128] = part.astype(F32) * factor
 
 
 def final_call(x):
@@ -470,13 +448,14 @@
     asked = exchange(halo_rows.reshape(128, 1, 4))
     h, gs, p = halo_call(halo_nbrs.T, halo_len.reshape(1, NB), bdeg, hdeg, grad_out)
     send = pick_call(asked, feat_table, emb_table, grad_table, p)
-    recv = exchange(send.reshape(128, 8, 896)).reshape(1024, 896)
+    recv = exchange(send)
     c, cf, sp, bp = batch_call(batch_nbrs.T, bdeg, node_feats, gs, weight_two)
     hid, grads = main_call(recv, h, cf, sp, bp, p, weight_one, weight_two, bdeg, hdeg)
-    shares = exchange(grads.reshape(128, 8, 384))
-    out_embed = out_call(recv, c, h, hid, weight_two, bdeg, hdeg)
-    shares, out_embed = lax.optimization_barrier((shares, out_embed))
-    sums = exchange(sum_call(shares)).reshape(1024, 384)
+    shares = exchange(grads)
+    half = out_call(0, recv, c, h, hid, weight_two, bdeg, hdeg)
+    shares, half = lax.optimization_barrier((shares, half))
+    sums = exchange(sum_call(shares))
+    out_embed = out_call(1, recv, c, h, hid, weight_two, bdeg, hdeg, half)
     halo_grad = tail_call(asked, recv)
     grad_one, grad_two = final_call(sums)
     return out_embed, halo_grad, grad_one, grad_two

time: 121 us -> 115 us (0.950)
  waiting for transfers between devices: 26.4 us -> 18.7 us
  Pallas kernels: 63.3 us -> 66.9 us
  starting transfers between devices: 28.9 us -> 27 us
    all_to_all x4, waiting for transfers between devices: 26.4 us -> 18.7 us  [exchange(): return lax.all_to_all(x, AXES, split_axis=0, concat_axis=0, tiled=True)]
    pallas_call x1 -> x2, Pallas kernels: 13.3 us -> 17.1 us  [out_call(): pl.pallas_call(lambda *refs: out_kernel(half, refs), in_specs=[vmem_spec(...]
    all_to_all x4, starting transfers between devices: 28.9 us -> 27 us  [exchange(): return lax.all_to_all(x, AXES, split_axis=0, concat_axis=0, tiled=True)]
  transfers between devices with their start and end apart: 4 -> 4, of which waited for: 4 -> 4; matrix products, arithmetic and copies ran while one was open for 0% -> 0% of each run, Pallas kernels for 35% -> 40%
where the time goes in v4:
time: 115 us
  Pallas kernels  66.9 us (58%)
  starting transfers between devices  27 us (23%)
  waiting for transfers between devices  18.7 us (16%)
  local copies, waits for them, and re-layouts  1.42 us (1%)
    all_to_all x4, starting transfers between devices, exchange(): return lax.all_to_all(x, AXES, split_axis=0, concat_axis=0, tiled=True)  27 us
    pallas_call x1, Pallas kernels, batch_call(): pl.pallas_call(batch_kernel, in_specs=[vmem_spec()] * 5, out_specs=[hbm_s...  20.9 us
    all_to_all x4, waiting for transfers between devices, exchange(): return lax.all_to_all(x, AXES, split_axis=0, concat_axis=0, tiled=True)  18.7 us
    pallas_call x2, Pallas kernels, out_call(): pl.pallas_call(lambda *refs: out_kernel(half, refs), in_specs=[vmem_spec(...  17.1 us
    pallas_call x1, Pallas kernels, main_call(): pl.pallas_call(main_kernel, in_specs=[vmem_spec()] + [hbm_spec()] * 4 + [...  12 us
    pallas_call x1, Pallas kernels, pick_call(): pl.pallas_call(pick_kernel, in_specs=[vmem_spec(), hbm_spec(), hbm_spec()...  6.67 us
    pallas_call x1, Pallas kernels, halo_call(): pl.pallas_call(halo_kernel, in_specs=[vmem_spec()] * 4 + [hbm_spec()], ou...  5.35 us
    pallas_call x1, Pallas kernels, tail_call(): pl.pallas_call(tail_kernel, in_specs=[vmem_spec()] * 2, out_specs=hbm_spe...  2.48 us
  transfers between devices with their start and end apart: 4, of which 4 were waited for; matrix products, arithmetic and copies ran while one was open for 0% of the time, Pallas kernels for 40%

profile of v4, /device:TPU:1, one launch (start us, length us, event | category | flops | bytes accessed | tf_op | source)
XLA Modules:
  0.0 114.7 jit_solution(16804764409103070918)
XLA Ops:
  0.6 1.4 %reshape.20 = s32[128,1,4]{2,0,1:T(8,128)} reshape(s32[512]{0:T(512)} %param.18) | data formatting | bytes 4096 | tf_op jit(solution)/shard_map/reshape | solution.py:448
  2.0 11.5 %all-to-all-start = ((s32[128,1,4]{2,1,0:T(1,128)}), s32[128,1,4]{2,1,0:T(1,128)S(1)}, u32[]{:S(2)}, u32[]{:S(2)}) async-start(s32[128,1,4]{2,1,0:T(1,128)} %bitcast), calls=%async_computation | async-start | bytes 131072 | tf_op jit(solution)/shard_map/all_to_all | solution.py:439
  13.5 5.4 %halo_part.1 = (bf16[512,2048]{1,0:T(8,128)(2,1)}, bf16[2048,512]{1,0:T(8,128)(2,1)}, bf16[512,512]{1,0:T(8,128)(2,1)S(1)}) custom-call(s32[8,2048]{1,0:T(8,128)} %bitcast.11, s32[1,2048]{1,0:T(1,128)} %bitcast.17, s32[1,2048]{1,0:T(1,128)} %bitcast.6, s32[1,512]{1,0:T(1,128)} %bitcast.13, bf16[2048,512]{1,0:T(8,128)(2,1)} %g_hbm.1), custom_call_target="tpu_custom_call" | custom-call | tf_op jit(solution)/shard_map/halo_part/pallas_call | solution.py:119
  18.9 4.2 %all-to-all-done.ask_ref = s32[128,1,4]{2,1,0:T(1,128)S(1)} async-done(((s32[128,1,4]{2,1,0:T(1,128)}), s32[128,1,4]{2,1,0:T(1,128)S(1)}, u32[]{:S(2)}, u32[]{:S(2)}) %all-to-all-start) | async-done | bytes 2080 | tf_op jit(solution)/shard_map/all_to_all | solution.py:439
  23.1 6.7 %pick_rows.1 = bf16[128,4,1664]{2,1,0:T(4,128)(2,1)} custom-call(s32[128,1,4]{2,1,0:T(1,128)S(1)} %all-to-all-done.ask_ref, bf16[2048,128]{1,0:T(8,128)(2,1)} %x_hbm.1, bf16[2048,512]{1,0:T(8,128)(2,1)} %e_hbm.1, bf16[2048,512]{1,0:T(8,128)(2,1)} %v_hbm.1, bf16[512,512]{1,0:T(8,128)(2,1)S(1)} %get-tuple-element.17.p_ref), custom_call_target="tpu_custom_call" | custom-call | tf_op jit(solution)/shard_map/pick_rows/pallas_call | solution.py:188
  29.7 5.6 %all-to-all-start.1 = ((bf16[128,4,1664]{2,1,0:T(4,128)(2,1)}), bf16[128,4,1664]{2,1,0:T(4,128)(2,1)S(1)}, u32[]{:S(2)}, u32[]{:S(2)}) async-start(bf16[128,4,1664]{2,1,0:T(4,128)(2,1)} %pick_rows.1), calls=%async_computation.1 | async-start | bytes 3407872 | tf_op jit(solution)/shard_map/all_to_all | solution.py:439
  35.4 20.9 %batch_part.1 = (bf16[2048,2048]{1,0:T(8,128)(2,1)}, f32[2048,128]{1,0:T(8,128)}, bf16[2048,512]{1,0:T(8,128)(2,1)}, f32[2048,512]{1,0:T(8,128)}) custom-call(s32[8,2048]{1,0:T(8,128)} %bitcast.12, s32[1,2048]{1,0:T(1,128)} %bitcast.7, bf16[2048,128]{1,0:T(8,128)(2,1)} %f_ref.1, bf16[2048,512]{1,0:T(8,128)(2,1)} %get-tuple-element.18.gs_ref, ...), custom_call_target="tpu_custom_call" | custom-call | tf_op jit(solution)/shard_map/batch_part/pallas_call | solution.py:235
  56.2 4.6 %all-to-all-done.1.r_ref.refs_0_ = bf16[128,4,1664]{2,1,0:T(4,128)(2,1)S(1)} async-done(((bf16[128,4,1664]{2,1,0:T(4,128)(2,1)}), bf16[128,4,1664]{2,1,0:T(4,128)(2,1)S(1)}, u32[]{:S(2)}, u32[]{:S(2)}) %all-to-all-start.1) | async-done | bytes 1703968 | tf_op jit(solution)/shard_map/all_to_all | solution.py:439
  60.9 12.0 %main_part.1 = (bf16[2048,512]{1,0:T(8,128)(2,1)}, bf16[128,4,640]{2,1,0:T(4,128)(2,1)}) custom-call(bf16[128,4,1664]{2,1,0:T(4,128)(2,1)S(1)} %all-to-all-done.1.r_ref.refs_0_, bf16[512,2048]{1,0:T(8,128)(2,1)} %get-tuple-element.20.h_hbm.refs_2_, f32[2048,128]{1,0:T(8,128)} %get-tuple-element.21.cf_hbm, bf16[2048,512]{1,0:T(8,128)(2,1)} %get-tuple-element.22.sp_hbm, ...), custom_call_target="tpu_custom_call" | custom-call | tf_op jit(solution)/shard_map/main_part/pallas_call | solution.py:306
  72.9 5.1 %all-to-all-start.2 = ((bf16[128,4,640]{2,1,0:T(4,128)(2,1)}), bf16[128,4,640]{2,1,0:T(4,128)(2,1)S(1)}, u32[]{:S(2)}, u32[]{:S(2)}) async-start(bf16[128,4,640]{2,1,0:T(4,128)(2,1)} %get-tuple-element.25), calls=%async_computation.2 | async-start | bytes 1310720 | tf_op jit(solution)/shard_map/all_to_all | solution.py:439
  78.0 8.5 %out_part_0.1.refs_7_ = bf16[2048,512]{1,0:T(8,128)(2,1)} custom-call(bf16[128,4,1664]{2,1,0:T(4,128)(2,1)S(1)} %all-to-all-done.1.r_ref.refs_0_, bf16[2048,2048]{1,0:T(8,128)(2,1)} %get-tuple-element.19.refs_1_, bf16[512,2048]{1,0:T(8,128)(2,1)} %get-tuple-element.20.h_hbm.refs_2_, bf16[2048,512]{1,0:T(8,128)(2,1)} %get-tuple-element.24.refs_3_, ...), custom_call_target="tpu_custom_call" | custom-call | tf_op jit(solution)/shard_map/out_part_0/pallas_call | solution.py:354
  86.6 6.1 %all-to-all-done.2.x_ref = bf16[128,4,640]{2,1,0:T(4,128)(2,1)S(1)} async-done(((bf16[128,4,640]{2,1,0:T(4,128)(2,1)}), bf16[128,4,640]{2,1,0:T(4,128)(2,1)S(1)}, u32[]{:S(2)}, u32[]{:S(2)}) %all-to-all-start.2) | async-done | bytes 655392 | tf_op jit(solution)/shard_map/all_to_all | solution.py:439
  92.7 1.3 %sum_part.1 = bf16[128,4,640]{2,1,0:T(4,128)(2,1)} custom-call(bf16[128,4,640]{2,1,0:T(4,128)(2,1)S(1)} %all-to-all-done.2.x_ref), custom_call_target="tpu_custom_call" | custom-call | tf_op jit(solution)/shard_map/sum_part/pallas_call | solution.py:408
  93.9 4.8 %all-to-all-start.3 = ((bf16[128,4,640]{2,1,0:T(4,128)(2,1)}), bf16[128,4,640]{2,1,0:T(4,128)(2,1)S(1)}, u32[]{:S(2)}, u32[]{:S(2)}) async-start(bf16[128,4,640]{2,1,0:T(4,128)(2,1)} %sum_part.1), calls=%async_computation.3 | async-start | bytes 1310720 | tf_op jit(solution)/shard_map/all_to_all | solution.py:439
  98.7 2.5 %tail_part.1 = bf16[2048,512]{1,0:T(8,128)(2,1)} custom-call(s32[128,1,4]{2,1,0:T(1,128)S(1)} %all-to-all-done.ask_ref, bf16[128,4,1664]{2,1,0:T(4,128)(2,1)S(1)} %all-to-all-done.1.r_ref.refs_0_), custom_call_target="tpu_custom_call" | custom-call | tf_op jit(solution)/shard_map/tail_part/pallas_call | solution.py:386
  101.2 8.5 %out_part_1.1 = bf16[2048,512]{1,0:T(8,128)(2,1)} custom-call(bf16[128,4,1664]{2,1,0:T(4,128)(2,1)S(1)} %all-to-all-done.1.r_ref.refs_0_, bf16[2048,2048]{1,0:T(8,128)(2,1)} %get-tuple-element.19.refs_1_, bf16[512,2048]{1,0:T(8,128)(2,1)} %get-tuple-element.20.h_hbm.refs_2_, ...), custom_call_target="tpu_custom_call", output_to_operand_aliasing={{}: (7, {})} | custom-call | tf_op jit(solution)/shard_map/out_part_1/pallas_call | solution.py:354
  109.7 3.8 %all-to-all-done.3.x_ref = bf16[128,4,640]{2,1,0:T(4,128)(2,1)S(1)} async-done(((bf16[128,4,640]{2,1,0:T(4,128)(2,1)}), bf16[128,4,640]{2,1,0:T(4,128)(2,1)S(1)}, u32[]{:S(2)}, u32[]{:S(2)}) %all-to-all-start.3) | async-done | bytes 655392 | tf_op jit(solution)/shard_map/all_to_all | solution.py:439
  113.5 1.2 %final_part.1 = (f32[128,512]{1,0:T(8,128)}, f32[512,512]{1,0:T(8,128)}) custom-call(bf16[128,4,640]{2,1,0:T(4,128)(2,1)S(1)} %all-to-all-done.3.x_ref), custom_call_target="tpu_custom_call" | custom-call | tf_op jit(solution)/shard_map/final_part/pallas_call | solution.py:426
Async XLA Ops:
  2.0 21.0 %all-to-all-start = ((s32[128,1,4]{2,1,0:T(1,128)}), s32[128,1,4]{2,1,0:T(1,128)S(1)}, u32[]{:S(2)}, u32[]{:S(2)}) async-start(s32[128,1,4]{2,1,0:T(1,128)} %bitcast), calls=%async_computation | async-start | bytes 131072 | tf_op jit(solution)/shard_map/all_to_all | solution.py:439
  29.7 31.1 %all-to-all-start.1 = ((bf16[128,4,1664]{2,1,0:T(4,128)(2,1)}), bf16[128,4,1664]{2,1,0:T(4,128)(2,1)S(1)}, u32[]{:S(2)}, u32[]{:S(2)}) async-start(bf16[128,4,1664]{2,1,0:T(4,128)(2,1)} %pick_rows.1), calls=%async_computation.1 | async-start | bytes 3407872 | tf_op jit(solution)/shard_map/all_to_all | solution.py:439
  72.9 19.8 %all-to-all-start.2 = ((bf16[128,4,640]{2,1,0:T(4,128)(2,1)}), bf16[128,4,640]{2,1,0:T(4,128)(2,1)S(1)}, u32[]{:S(2)}, u32[]{:S(2)}) async-start(bf16[128,4,640]{2,1,0:T(4,128)(2,1)} %get-tuple-element.25), calls=%async_computation.2 | async-start | bytes 1310720 | tf_op jit(solution)/shard_map/all_to_all | solution.py:439
  93.9 19.6 %all-to-all-start.3 = ((bf16[128,4,640]{2,1,0:T(4,128)(2,1)}), bf16[128,4,640]{2,1,0:T(4,128)(2,1)S(1)}, u32[]{:S(2)}, u32[]{:S(2)}) async-start(bf16[128,4,640]{2,1,0:T(4,128)(2,1)} %sum_part.1), calls=%async_computation.3 | async-start | bytes 1310720 | tf_op jit(solution)/shard_map/all_to_all | solution.py:439

commit v5 on v4

--- a/solution.py
+++ b/solution.py
@@ -153,33 +153,36 @@
     )
     mine = jnp.where(lane == (sub & 3), mine & (NB - 1), 0)
     col = jnp.sum(mine.astype(F32), axis=2, keepdims=True).reshape(512, 1).astype(jnp.int32)
-    colb = jnp.broadcast_to(col, (512, 128))
-    lanes = lax.broadcasted_iota(jnp.int32, (512, 128), 1)
+    colb = jnp.broadcast_to(col, (512, 128)).reshape(64, 8, 128)
+    lanes = lax.broadcasted_iota(jnp.int32, (1, 8, 128), 2)
     for c in range(0, NB, 128):
-        s_ref[:, c : c + 128] = jnp.where(colb == lanes + c, 1.0, 0.0).astype(BF)
+        s_ref[:, c : c + 128] = jnp.where(colb == lanes + c, 1.0, 0.0).reshape(512, 128).astype(BF)
 
 
 def pick_kernel(
-    ask_ref, x_hbm, e_hbm, v_hbm, p_ref, out_hbm, s_ref, x_ref, e_ref, v_ref, out_ref, sems
+    ask_ref, x_hbm, e_ref, v_hbm, p_ref, out_hbm, s_ref, x_ref, v_ref, out_ref, sems
 ):
     copies = [
         pltpu.make_async_copy(src, dst, sems.at[n])
-        for n, (src, dst) in enumerate(((e_hbm, e_ref), (v_hbm, v_ref), (x_hbm, x_ref)))
+        for n, (src, dst) in enumerate(((v_hbm, v_ref), (x_hbm, x_ref)))
     ]
     for copy in copies:
         copy.start()
+    def send(lo, hi, n):
+        at = (slice(None), slice(None), slice(lo, hi))
+        sends.append(pltpu.make_async_copy(out_ref.at[at], out_hbm.at[at], sems.at[n]))
+        sends[-1].start()
+
+    sends = []
     out_ref[:, :, 1152:1664] = chunks_of(p_ref[...])
+    send(1152, 1664, 3)
     selector(ask_ref, s_ref)
     s = s_ref[...]
-    sends = []
     for n, (lo, hi, src) in enumerate(((128, 640, e_ref), (640, 1152, v_ref), (0, 128, x_ref))):
-        copies[n].wait()
+        if n:
+            copies[n - 1].wait()
         out_ref[:, :, lo:hi] = chunks_of(dot(s, src[...]))
-        if n == 1:
-            hi = 1664
-        at = (slice(None), slice(None), slice(lo, hi))
-        sends.append(pltpu.make_async_copy(out_ref.at[at], out_hbm.at[at], sems.at[3 + n]))
-        sends[-1].start()
+        send(lo, hi, 4 + n)
     for copy in sends:
         copy.wait()
 
@@ -187,20 +190,19 @@
 def pick_call(asked, x, e, v, p):
     return pl.pallas_call(
         pick_kernel,
-        in_specs=[vmem_spec(), hbm_spec(), hbm_spec(), hbm_spec(), vmem_spec()],
+        in_specs=[vmem_spec(), hbm_spec(), vmem_spec(), hbm_spec(), vmem_spec()],
         out_specs=hbm_spec(),
         out_shape=pltpu.HBM((128, 4, 1664), BF),
         scratch_shapes=[
             pltpu.VMEM((NH, NB), BF),
             pltpu.VMEM((NB, FEAT), BF),
             pltpu.VMEM((NB, HID), BF),
-            pltpu.VMEM((NB, HID), BF),
             pltpu.VMEM((128, 4, 1664), BF),
-            pltpu.SemaphoreType.DMA((6,)),
+            pltpu.SemaphoreType.DMA((7,)),
         ],
         compiler_params=limit(58),
         name="pick_rows",
-    )(keep(asked), leave(x), leave(e), leave(v), keep(p))
+    )(keep(asked), leave(x), keep(e), leave(v), keep(p))
 
 
 def batch_kernel(
@@ -255,44 +257,58 @@
 
 
 def main_kernel(
-    r_ref, h_hbm, cf_hbm, sp_hbm, bp_hbm, p_ref, w1_ref, w2_ref, bdeg_ref, hdeg_ref,
+    r_ref, h_hbm, cf_hbm, sp_hbm, bp_hbm, p_ref, w1_hbm, w2_hbm, bdeg_hbm, hdeg_hbm,
     hid_hbm, grads_ref,
-    h_ref, cf_ref, sp_ref, bp_ref, hid_ref, g1_ref, g2_ref, sems,
+    h_ref, cf_ref, sp_ref, bp_ref, w1_ref, w2_ref, bdeg_ref, hdeg_ref,
+    hid_ref, mix_ref, g1_ref, g2_ref, sems,
 ):
-    pairs = ((h_hbm, h_ref), (cf_hbm, cf_ref), (bp_hbm, bp_ref), (sp_hbm, sp_ref))
-    copies = [pltpu.make_async_copy(src, dst, sems.at[n]) for n, (src, dst) in enumerate(pairs)]
-    for copy in copies[:2]:
+    first = (
+        (hdeg_hbm, hdeg_ref), (w2_hbm, w2_ref), (bdeg_hbm, bdeg_ref),
+        (h_hbm, h_ref), (cf_hbm, cf_ref), (w1_hbm, w1_ref),
+    )
+    copies = [pltpu.make_async_copy(src, dst, sems.at[n]) for n, (src, dst) in enumerate(first)]
+    for copy in copies:
         copy.start()
+    bp_copies = [
+        pltpu.make_async_copy(bp_hbm.at[s : s + STEP], bp_ref.at[s : s + STEP], sems.at[6 + s // STEP])
+        for s in range(0, NB, STEP)
+    ]
+    sp_copy = pltpu.make_async_copy(sp_hbm, sp_ref, sems.at[10])
+    g2_ref[...] = dot_tl(rows_of(r_ref, 128, 640), p_ref[...])
+    copies[0].wait()
+    col_h = columns(lax.rsqrt(hdeg_ref[...].astype(F32)))
+    mix_ref[:, 512:640] = (rows_of(r_ref, 0, 128).astype(F32) * col_h).astype(BF)
+    copies[1].wait()
+    mix_ref[:, 0:512] = scale_rows(dot_t(rows_of(r_ref, 640, 1152), w2_ref[...]), col_h).astype(BF)
+    copies[2].wait()
     inv = columns(lax.rsqrt(bdeg_ref[...].astype(F32)))
-    col_h = columns(lax.rsqrt(hdeg_ref[...].astype(F32)))
-    hx = (rows_of(r_ref, 0, 128).astype(F32) * col_h).astype(BF)
-    hvw = scale_rows(dot_t(rows_of(r_ref, 640, 1152), w2_ref[...]), col_h).astype(BF)
-    g2_ref[...] = dot_tl(rows_of(r_ref, 128, 640), p_ref[...])
-    for copy in copies[:2]:
-        copy.wait()
-    for copy in copies[2:]:
+    for copy in copies[3:]:
+        copy.wait()
+    for copy in bp_copies:
         copy.start()
+    sp_copy.start()
     outs = []
     for n, s in enumerate(range(0, NB, STEP)):
         at = slice(s, s + STEP)
-        col = inv[at]
+        half = 0.5 * inv[at]
+        half_sq = half * inv[at]
         h = h_ref[:, at]
-        u1 = (cf_ref[at, :] + dot_tl(h, hx)).astype(BF)
-        pre = scale_rows(dot(u1, w1_ref[...]), col)
-        sig = 0.5 + 0.5 * jnp.tanh(0.5 * pre)
-        hid_ref[at, :] = scale_rows(pre * sig, col).astype(BF)
-        outs.append(pltpu.make_async_copy(hid_ref.at[at], hid_hbm.at[at], sems.at[4 + n]))
+        u1 = (cf_ref[at, :] + dot_tl(h, mix_ref[:, 512:640])).astype(BF)
+        z = dot(u1, w1_ref[...])
+        zh = scale_rows(z, half)
+        t = jnp.tanh(zh)
+        w = scale_rows(1.0 + t, half_sq)
+        hid_ref[at, :] = (z * w).astype(BF)
+        outs.append(pltpu.make_async_copy(hid_ref.at[at], hid_hbm.at[at], sems.at[11 + n]))
         outs[-1].start()
-        der = scale_rows(sig * (1.0 + pre * (1.0 - sig)), col * col)
-        if n == 0:
-            copies[2].wait()
-        d_pre = ((bp_ref[at, :] + dot_tl(h, hvw)) * der).astype(BF)
+        bp_copies[n].wait()
+        d_pre = ((bp_ref[at, :] + dot_tl(h, mix_ref[:, 0:512])) * (w * (1.0 + zh * (1.0 - t)))).astype(BF)
         g1 = dot_tl(u1, d_pre)
         if n == 0:
-            copies[3].wait()
             g1_ref[...] = g1
         else:
             g1_ref[...] += g1
+    sp_copy.wait()
     g2_ref[...] += dot_tl(hid_ref[...], sp_ref[...])
     grads_ref[:, :, 0:512] = chunks_of(g2_ref[...])
     for q in range(4):
@@ -305,7 +321,7 @@
 def main_call(recv, h, cf, sp, bp, p, w1, w2, bdeg, hdeg):
     return pl.pallas_call(
         main_kernel,
-        in_specs=[vmem_spec()] + [hbm_spec()] * 4 + [vmem_spec()] * 5,
+        in_specs=[vmem_spec()] + [hbm_spec()] * 4 + [vmem_spec()] + [hbm_spec()] * 4,
         out_specs=[hbm_spec(), vmem_spec()],
         out_shape=(pltpu.HBM((NB, HID), BF), jax.ShapeDtypeStruct((128, 4, 640), BF)),
         scratch_shapes=[
@@ -313,14 +329,19 @@
             pltpu.VMEM((NB, FEAT), F32),
             pltpu.VMEM((NB, HID), BF),
             pltpu.VMEM((NB, HID), F32),
-            pltpu.VMEM((NB, HID), BF),
+            pltpu.VMEM((FEAT, HID), BF),
+            pltpu.VMEM((HID, HID), BF),
+            pltpu.VMEM((1, NB), jnp.int32),
+            pltpu.VMEM((1, NH), jnp.int32),
+            pltpu.VMEM((NB, HID), BF),
+            pltpu.VMEM((NH, HID + FEAT), BF),
             pltpu.VMEM((FEAT, HID), F32),
             pltpu.VMEM((HID, HID), F32),
-            pltpu.SemaphoreType.DMA((8,)),
+            pltpu.SemaphoreType.DMA((15,)),
         ],
         compiler_params=limit(58),
         name="main_part",
-    )(keep(recv), leave(h), leave(cf), leave(sp), leave(bp), keep(p), w1, w2, bdeg, hdeg)
+    )(keep(recv), leave(h), leave(cf), leave(sp), leave(bp), keep(p), leave(w1), leave(w2), leave(bdeg), leave(hdeg))
 
 
 def out_kernel(half, refs):

time: 115 us -> 113 us (0.983)
  Pallas kernels: 66.9 us -> 65 us
    pallas_call x1, Pallas kernels: 12 us -> 9.87 us  [main_call(): pl.pallas_call(main_kernel, in_specs=[vmem_spec()] + [hbm_spec()] * 4 + [...]
  transfers between devices with their start and end apart: 4 -> 4, of which waited for: 4 -> 4; matrix products, arithmetic and copies ran while one was open for 0% -> 0% of each run, Pallas kernels for 40% -> 41%
where the time goes in v5:
time: 113 us
  Pallas kernels  65 us (58%)
  starting transfers between devices  27 us (24%)
  waiting for transfers between devices  18.7 us (17%)
  local copies, waits for them, and re-layouts  1.57 us (1%)
    all_to_all x4, starting transfers between devices, exchange(): return lax.all_to_all(x, AXES, split_axis=0, concat_axis=0, tiled=True)  27 us
    pallas_call x1, Pallas kernels, batch_call(): pl.pallas_call(batch_kernel, in_specs=[vmem_spec()] * 5, out_specs=[hbm_s...  20.9 us
    all_to_all x4, waiting for transfers between devices, exchange(): return lax.all_to_all(x, AXES, split_axis=0, concat_axis=0, tiled=True)  18.7 us
    pallas_call x2, Pallas kernels, out_call(): pl.pallas_call(lambda *refs: out_kernel(half, refs), in_specs=[vmem_spec(...  17.1 us
    pallas_call x1, Pallas kernels, main_call(): pl.pallas_call(main_kernel, in_specs=[vmem_spec()] + [hbm_spec()] * 4 + [...  9.87 us
    pallas_call x1, Pallas kernels, pick_call(): pl.pallas_call(pick_kernel, in_specs=[vmem_spec(), hbm_spec(), vmem_spec(...  6.92 us
    pallas_call x1, Pallas kernels, halo_call(): pl.pallas_call(halo_kernel, in_specs=[vmem_spec()] * 4 + [hbm_spec()], ou...  5.35 us
    pallas_call x1, Pallas kernels, tail_call(): pl.pallas_call(tail_kernel, in_specs=[vmem_spec()] * 2, out_specs=hbm_spe...  2.48 us
  transfers between devices with their start and end apart: 4, of which 4 were waited for; matrix products, arithmetic and copies ran while one was open for 0% of the time, Pallas kernels for 41%

profile of v5, /device:TPU:1, one launch (start us, length us, event | category | flops | bytes accessed | tf_op | source)
XLA Modules:
  0.0 113.0 jit_solution(14709196842058817697)
XLA Ops:
  0.6 0.0 copy-start
  0.6 1.6 %reshape.20 = s32[128,1,4]{2,0,1:T(8,128)} reshape(s32[512]{0:T(512)} %param.18) | data formatting | bytes 4096 | tf_op jit(solution)/shard_map/reshape | solution.py:469
  2.2 11.5 %all-to-all-start = ((s32[128,1,4]{2,1,0:T(1,128)}), s32[128,1,4]{2,1,0:T(1,128)S(1)}, u32[]{:S(2)}, u32[]{:S(2)}) async-start(s32[128,1,4]{2,1,0:T(1,128)} %bitcast), calls=%async_computation | async-start | bytes 131072 | tf_op jit(solution)/shard_map/all_to_all | solution.py:460
  13.7 5.4 %halo_part.1 = (bf16[512,2048]{1,0:T(8,128)(2,1)}, bf16[2048,512]{1,0:T(8,128)(2,1)}, bf16[512,512]{1,0:T(8,128)(2,1)S(1)}) custom-call(s32[8,2048]{1,0:T(8,128)} %bitcast.11, s32[1,2048]{1,0:T(1,128)} %bitcast.17, s32[1,2048]{1,0:T(1,128)} %bitcast.6, s32[1,512]{1,0:T(1,128)} %bitcast.13, bf16[2048,512]{1,0:T(8,128)(2,1)} %g_hbm.1), custom_call_target="tpu_custom_call" | custom-call | tf_op jit(solution)/shard_map/halo_part/pallas_call | solution.py:119
  19.1 4.2 %all-to-all-done.ask_ref = s32[128,1,4]{2,1,0:T(1,128)S(1)} async-done(((s32[128,1,4]{2,1,0:T(1,128)}), s32[128,1,4]{2,1,0:T(1,128)S(1)}, u32[]{:S(2)}, u32[]{:S(2)}) %all-to-all-start) | async-done | bytes 2080 | tf_op jit(solution)/shard_map/all_to_all | solution.py:460
  23.2 0.0 copy-done
  23.2 6.9 %pick_rows.1 = bf16[128,4,1664]{2,1,0:T(4,128)(2,1)} custom-call(s32[128,1,4]{2,1,0:T(1,128)S(1)} %all-to-all-done.ask_ref, bf16[2048,128]{1,0:T(8,128)(2,1)} %x_hbm.1, bf16[2048,512]{1,0:T(8,128)(2,1)S(1)} %copy-done, bf16[2048,512]{1,0:T(8,128)(2,1)} %v_hbm.1, bf16[512,512]{1,0:T(8,128)(2,1)S(1)} %get-tuple-element.17.p_ref), custom_call_target="tpu_custom_call" | custom-call | tf_op jit(solution)/shard_map/pick_rows/pallas_call | solution.py:191
  30.2 5.6 %all-to-all-start.1 = ((bf16[128,4,1664]{2,1,0:T(4,128)(2,1)}), bf16[128,4,1664]{2,1,0:T(4,128)(2,1)S(1)}, u32[]{:S(2)}, u32[]{:S(2)}) async-start(bf16[128,4,1664]{2,1,0:T(4,128)(2,1)} %pick_rows.1), calls=%async_computation.1 | async-start | bytes 3407872 | tf_op jit(solution)/shard_map/all_to_all | solution.py:460
  35.8 20.9 %batch_part.1 = (bf16[2048,2048]{1,0:T(8,128)(2,1)}, f32[2048,128]{1,0:T(8,128)}, bf16[2048,512]{1,0:T(8,128)(2,1)}, f32[2048,512]{1,0:T(8,128)}) custom-call(s32[8,2048]{1,0:T(8,128)} %bitcast.12, s32[1,2048]{1,0:T(1,128)} %bitcast.7, bf16[2048,128]{1,0:T(8,128)(2,1)} %f_ref.1, bf16[2048,512]{1,0:T(8,128)(2,1)} %get-tuple-element.18.gs_ref, ...), custom_call_target="tpu_custom_call" | custom-call | tf_op jit(solution)/shard_map/batch_part/pallas_call | solution.py:237
  56.7 4.6 %all-to-all-done.1.r_ref.refs_0_ = bf16[128,4,1664]{2,1,0:T(4,128)(2,1)S(1)} async-done(((bf16[128,4,1664]{2,1,0:T(4,128)(2,1)}), bf16[128,4,1664]{2,1,0:T(4,128)(2,1)S(1)}, u32[]{:S(2)}, u32[]{:S(2)}) %all-to-all-start.1) | async-done | bytes 1703968 | tf_op jit(solution)/shard_map/all_to_all | solution.py:460
  61.3 9.9 %main_part.1 = (bf16[2048,512]{1,0:T(8,128)(2,1)}, bf16[128,4,640]{2,1,0:T(4,128)(2,1)}) custom-call(bf16[128,4,1664]{2,1,0:T(4,128)(2,1)S(1)} %all-to-all-done.1.r_ref.refs_0_, bf16[512,2048]{1,0:T(8,128)(2,1)} %get-tuple-element.20.h_hbm.refs_2_, f32[2048,128]{1,0:T(8,128)} %get-tuple-element.21.cf_hbm, bf16[2048,512]{1,0:T(8,128)(2,1)} %get-tuple-element.22.sp_hbm, ...), custom_call_target="tpu_custom_call" | custom-call | tf_op jit(solution)/shard_map/main_part/pallas_call | solution.py:322
  71.2 5.1 %all-to-all-start.2 = ((bf16[128,4,640]{2,1,0:T(4,128)(2,1)}), bf16[128,4,640]{2,1,0:T(4,128)(2,1)S(1)}, u32[]{:S(2)}, u32[]{:S(2)}) async-start(bf16[128,4,640]{2,1,0:T(4,128)(2,1)} %get-tuple-element.25), calls=%async_computation.2 | async-start | bytes 1310720 | tf_op jit(solution)/shard_map/all_to_all | solution.py:460
  76.3 8.5 %out_part_0.1.refs_7_ = bf16[2048,512]{1,0:T(8,128)(2,1)} custom-call(bf16[128,4,1664]{2,1,0:T(4,128)(2,1)S(1)} %all-to-all-done.1.r_ref.refs_0_, bf16[2048,2048]{1,0:T(8,128)(2,1)} %get-tuple-element.19.refs_1_, bf16[512,2048]{1,0:T(8,128)(2,1)} %get-tuple-element.20.h_hbm.refs_2_, bf16[2048,512]{1,0:T(8,128)(2,1)} %get-tuple-element.24.refs_3_, ...), custom_call_target="tpu_custom_call" | custom-call | tf_op jit(solution)/shard_map/out_part_0/pallas_call | solution.py:375
  84.9 6.1 %all-to-all-done.2.x_ref = bf16[128,4,640]{2,1,0:T(4,128)(2,1)S(1)} async-done(((bf16[128,4,640]{2,1,0:T(4,128)(2,1)}), bf16[128,4,640]{2,1,0:T(4,128)(2,1)S(1)}, u32[]{:S(2)}, u32[]{:S(2)}) %all-to-all-start.2) | async-done | bytes 655392 | tf_op jit(solution)/shard_map/all_to_all | solution.py:460
  91.0 1.3 %sum_part.1 = bf16[128,4,640]{2,1,0:T(4,128)(2,1)} custom-call(bf16[128,4,640]{2,1,0:T(4,128)(2,1)S(1)} %all-to-all-done.2.x_ref), custom_call_target="tpu_custom_call" | custom-call | tf_op jit(solution)/shard_map/sum_part/pallas_call | solution.py:429
  92.3 4.8 %all-to-all-start.3 = ((bf16[128,4,640]{2,1,0:T(4,128)(2,1)}), bf16[128,4,640]{2,1,0:T(4,128)(2,1)S(1)}, u32[]{:S(2)}, u32[]{:S(2)}) async-start(bf16[128,4,640]{2,1,0:T(4,128)(2,1)} %sum_part.1), calls=%async_computation.3 | async-start | bytes 1310720 | tf_op jit(solution)/shard_map/all_to_all | solution.py:460
  97.0 2.5 %tail_part.1 = bf16[2048,512]{1,0:T(8,128)(2,1)} custom-call(s32[128,1,4]{2,1,0:T(1,128)S(1)} %all-to-all-done.ask_ref, bf16[128,4,1664]{2,1,0:T(4,128)(2,1)S(1)} %all-to-all-done.1.r_ref.refs_0_), custom_call_target="tpu_custom_call" | custom-call | tf_op jit(solution)/shard_map/tail_part/pallas_call | solution.py:407
  99.5 8.6 %out_part_1.1 = bf16[2048,512]{1,0:T(8,128)(2,1)} custom-call(bf16[128,4,1664]{2,1,0:T(4,128)(2,1)S(1)} %all-to-all-done.1.r_ref.refs_0_, bf16[2048,2048]{1,0:T(8,128)(2,1)} %get-tuple-element.19.refs_1_, bf16[512,2048]{1,0:T(8,128)(2,1)} %get-tuple-element.20.h_hbm.refs_2_, ...), custom_call_target="tpu_custom_call", output_to_operand_aliasing={{}: (7, {})} | custom-call | tf_op jit(solution)/shard_map/out_part_1/pallas_call | solution.py:375
  108.1 3.8 %all-to-all-done.3.x_ref = bf16[128,4,640]{2,1,0:T(4,128)(2,1)S(1)} async-done(((bf16[128,4,640]{2,1,0:T(4,128)(2,1)}), bf16[128,4,640]{2,1,0:T(4,128)(2,1)S(1)}, u32[]{:S(2)}, u32[]{:S(2)}) %all-to-all-start.3) | async-done | bytes 655392 | tf_op jit(solution)/shard_map/all_to_all | solution.py:460
  111.8 1.2 %final_part.1 = (f32[128,512]{1,0:T(8,128)}, f32[512,512]{1,0:T(8,128)}) custom-call(bf16[128,4,640]{2,1,0:T(4,128)(2,1)S(1)} %all-to-all-done.3.x_ref), custom_call_target="tpu_custom_call" | custom-call | tf_op jit(solution)/shard_map/final_part/pallas_call | solution.py:447
Async XLA Ops:
  0.6 22.6 %copy-start = (bf16[2048,512]{1,0:T(8,128)(2,1)S(1)}, bf16[2048,512]{1,0:T(8,128)(2,1)}, u32[]{:S(2)}) copy-start(bf16[2048,512]{1,0:T(8,128)(2,1)} %e_ref.1) | copy-start | bytes 6291460
  2.2 21.0 %all-to-all-start = ((s32[128,1,4]{2,1,0:T(1,128)}), s32[128,1,4]{2,1,0:T(1,128)S(1)}, u32[]{:S(2)}, u32[]{:S(2)}) async-start(s32[128,1,4]{2,1,0:T(1,128)} %bitcast), calls=%async_computation | async-start | bytes 131072 | tf_op jit(solution)/shard_map/all_to_all | solution.py:460
  30.2 31.1 %all-to-all-start.1 = ((bf16[128,4,1664]{2,1,0:T(4,128)(2,1)}), bf16[128,4,1664]{2,1,0:T(4,128)(2,1)S(1)}, u32[]{:S(2)}, u32[]{:S(2)}) async-start(bf16[128,4,1664]{2,1,0:T(4,128)(2,1)} %pick_rows.1), calls=%async_computation.1 | async-start | bytes 3407872 | tf_op jit(solution)/shard_map/all_to_all | solution.py:460
  71.2 19.8 %all-to-all-start.2 = ((bf16[128,4,640]{2,1,0:T(4,128)(2,1)}), bf16[128,4,640]{2,1,0:T(4,128)(2,1)S(1)}, u32[]{:S(2)}, u32[]{:S(2)}) async-start(bf16[128,4,640]{2,1,0:T(4,128)(2,1)} %get-tuple-element.25), calls=%async_computation.2 | async-start | bytes 1310720 | tf_op jit(solution)/shard_map/all_to_all | solution.py:460
  92.3 19.6 %all-to-all-start.3 = ((bf16[128,4,640]{2,1,0:T(4,128)(2,1)}), bf16[128,4,640]{2,1,0:T(4,128)(2,1)S(1)}, u32[]{:S(2)}, u32[]{:S(2)}) async-start(bf16[128,4,640]{2,1,0:T(4,128)(2,1)} %sum_part.1), calls=%async_computation.3 | async-start | bytes 1310720 | tf_op jit(solution)/shard_map/all_to_all | solution.py:460

commit v6 on v5

--- a/solution.py
+++ b/solution.py
@@ -63,11 +63,11 @@
     return x * (jnp.tile(col, (1, reps)) if reps > 1 else col)
 
 
-def count_tiles(dst_ref, nbrs, rows0, n_rows):
+def count_tiles(dst_ref, nbrs, rows0, n_rows, weight=1.0):
     times = jnp.ones(nbrs.shape, jnp.int32)
     for k in range(1, 8):
         times = times + (nbrs == pltpu.roll(nbrs, k, 0)).astype(jnp.int32)
-    times = times.astype(F32)
+    times = times.astype(F32) * weight
     zero = jnp.zeros((16, 128), BF)
     sub = lax.broadcasted_iota(jnp.int32, (16, 128), 0)
     for c in range(0, nbrs.shape[1], 128):
@@ -91,45 +91,31 @@
         lax.fori_loop(0, n_rows // 128, group, 0)
 
 
-def halo_kernel(
-    hn_ref, hl_ref, bdeg_ref, hdeg_ref, g_hbm, h_hbm, gs_hbm, p_ref, g_ref, h_ref, gs_ref, sems
-):
+def halo_kernel(hn_ref, hl_ref, bdeg_ref, hdeg_ref, g_hbm, h_hbm, p_ref, g_ref, h_ref, sems):
     copy_in = pltpu.make_async_copy(g_hbm, g_ref, sems.at[0])
     copy_in.start()
     nbrs = hn_ref[...]
     slot = lax.broadcasted_iota(jnp.int32, nbrs.shape, 0)
     nbrs = jnp.where(slot < hl_ref[...], nbrs, -1)
-    count_tiles(h_ref, nbrs, 0, NH)
+    count_tiles(h_ref, nbrs, 0, NH, lax.rsqrt(bdeg_ref[...].astype(F32)))
     copy_h = pltpu.make_async_copy(h_ref, h_hbm, sems.at[1])
     copy_h.start()
-    inv = columns(lax.rsqrt(bdeg_ref[...].astype(F32)))
     inv_h = columns(lax.rsqrt(hdeg_ref[...].astype(F32)))
     copy_in.wait()
-    for s in range(0, NB, STEP):
-        gs = scale_rows(g_ref[s : s + STEP, :].astype(F32), inv[s : s + STEP])
-        gs_ref[s : s + STEP, :] = gs.astype(BF)
-    copy_gs = pltpu.make_async_copy(gs_ref, gs_hbm, sems.at[2])
-    copy_gs.start()
-    p_ref[...] = scale_rows(dot(h_ref[...], gs_ref[...]), inv_h).astype(BF)
+    p_ref[...] = scale_rows(dot(h_ref[...], g_ref[...]), inv_h).astype(BF)
     copy_h.wait()
-    copy_gs.wait()
 
 
 def halo_call(hn, hl, bdeg, hdeg, g):
     return pl.pallas_call(
         halo_kernel,
         in_specs=[vmem_spec()] * 4 + [hbm_spec()],
-        out_specs=[hbm_spec(), hbm_spec(), vmem_spec()],
-        out_shape=(
-            pltpu.HBM((NH, NB), BF),
-            pltpu.HBM((NB, HID), BF),
-            held(NH, HID),
-        ),
+        out_specs=[hbm_spec(), vmem_spec()],
+        out_shape=(pltpu.HBM((NH, NB), BF), held(NH, HID)),
         scratch_shapes=[
             pltpu.VMEM((NB, HID), BF),
             pltpu.VMEM((NH, NB), BF),
-            pltpu.VMEM((NB, HID), BF),
-            pltpu.SemaphoreType.DMA((3,)),
+            pltpu.SemaphoreType.DMA((2,)),
         ],
         compiler_params=limit(58),
         name="halo_part",
@@ -206,9 +192,11 @@
 
 
 def batch_kernel(
-    nb_ref, bdeg_ref, f_ref, gs_ref, w2_ref, c_hbm, cf_ref, sp_hbm, bp_hbm,
-    fs_ref, c_ref, sp_ref, bp_ref, sems,
+    nb_ref, bdeg_ref, f_ref, g_hbm, w2_ref, c_hbm, cf_ref, sp_hbm, bp_hbm,
+    fs_ref, g_ref, gs_ref, c_ref, sp_ref, bp_ref, sems,
 ):
+    copy_in = pltpu.make_async_copy(g_hbm, g_ref, sems.at[9])
+    copy_in.start()
     col = columns(lax.rsqrt(bdeg_ref[...].astype(F32)))
     fs_ref[...] = (f_ref[...].astype(F32) * col).astype(BF)
     eye = (
@@ -220,23 +208,27 @@
         c_ref[r : r + 128, r : r + 128] = c_ref[r : r + 128, r : r + 128] + eye
     copies = [pltpu.make_async_copy(c_ref, c_hbm, sems.at[0])]
     copies[0].start()
+    copy_in.wait()
+    for s in range(0, NB, STEP):
+        gs = scale_rows(g_ref[s : s + STEP, :].astype(F32), col[s : s + STEP])
+        gs_ref[s : s + STEP, :] = gs.astype(BF)
     for n, r in enumerate(range(0, NB, STEP)):
         at = slice(r, r + STEP)
         spread = dot(c_ref[at, :], gs_ref[...]).astype(BF)
         sp_ref[at, :] = spread
-        bp_ref[at, :] = dot_t(spread, w2_ref[...])
+        bp_ref[at, :] = scale_rows(dot_t(spread, w2_ref[...]), col[at])
         for m, (src, dst) in enumerate(((sp_ref, sp_hbm), (bp_ref, bp_hbm))):
             copies.append(pltpu.make_async_copy(src.at[at], dst.at[at], sems.at[1 + 2 * n + m]))
             copies[-1].start()
-        cf_ref[at, :] = dot_tl(c_ref[:, at], fs_ref[...])
+        cf_ref[at, :] = dot_tl(c_ref[:, at], fs_ref[...]) * col[at]
     for copy in copies:
         copy.wait()
 
 
-def batch_call(nb, bdeg, f, gs, w2):
+def batch_call(nb, bdeg, f, g, w2):
     return pl.pallas_call(
         batch_kernel,
-        in_specs=[vmem_spec()] * 5,
+        in_specs=[vmem_spec()] * 3 + [hbm_spec(), vmem_spec()],
         out_specs=[hbm_spec(), vmem_spec(), hbm_spec(), hbm_spec()],
         out_shape=(
             pltpu.HBM((NB, NB), BF),
@@ -246,14 +238,16 @@
         ),
         scratch_shapes=[
             pltpu.VMEM((NB, FEAT), BF),
+            pltpu.VMEM((NB, HID), BF),
+            pltpu.VMEM((NB, HID), BF),
             pltpu.VMEM((NB, NB), BF),
             pltpu.VMEM((NB, HID), BF),
             pltpu.VMEM((NB, HID), F32),
-            pltpu.SemaphoreType.DMA((9,)),
+            pltpu.SemaphoreType.DMA((10,)),
         ],
         compiler_params=limit(58),
         name="batch_part",
-    )(nb, bdeg, f, gs, w2)
+    )(nb, bdeg, f, leave(g), w2)
 
 
 def main_kernel(
@@ -262,47 +256,49 @@
     h_ref, cf_ref, sp_ref, bp_ref, w1_ref, w2_ref, bdeg_ref, hdeg_ref,
     hid_ref, mix_ref, g1_ref, g2_ref, sems,
 ):
-    first = (
-        (hdeg_hbm, hdeg_ref), (w2_hbm, w2_ref), (bdeg_hbm, bdeg_ref),
-        (h_hbm, h_ref), (cf_hbm, cf_ref), (w1_hbm, w1_ref),
-    )
+    first = ((hdeg_hbm, hdeg_ref), (w2_hbm, w2_ref), (bdeg_hbm, bdeg_ref), (w1_hbm, w1_ref))
     copies = [pltpu.make_async_copy(src, dst, sems.at[n]) for n, (src, dst) in enumerate(first)]
     for copy in copies:
         copy.start()
-    bp_copies = [
-        pltpu.make_async_copy(bp_hbm.at[s : s + STEP], bp_ref.at[s : s + STEP], sems.at[6 + s // STEP])
-        for s in range(0, NB, STEP)
-    ]
-    sp_copy = pltpu.make_async_copy(sp_hbm, sp_ref, sems.at[10])
+    blocks = []
+    for n, s in enumerate(range(0, NB, STEP)):
+        at = slice(s, s + STEP)
+        blocks.append([
+            pltpu.make_async_copy(h_hbm.at[:, at], h_ref.at[:, at], sems.at[4 + 3 * n]),
+            pltpu.make_async_copy(cf_hbm.at[at], cf_ref.at[at], sems.at[5 + 3 * n]),
+            pltpu.make_async_copy(bp_hbm.at[at], bp_ref.at[at], sems.at[6 + 3 * n]),
+        ])
+    sp_copy = pltpu.make_async_copy(sp_hbm, sp_ref, sems.at[16])
+    for copy in blocks[0]:
+        copy.start()
     g2_ref[...] = dot_tl(rows_of(r_ref, 128, 640), p_ref[...])
     copies[0].wait()
     col_h = columns(lax.rsqrt(hdeg_ref[...].astype(F32)))
     mix_ref[:, 512:640] = (rows_of(r_ref, 0, 128).astype(F32) * col_h).astype(BF)
     copies[1].wait()
     mix_ref[:, 0:512] = scale_rows(dot_t(rows_of(r_ref, 640, 1152), w2_ref[...]), col_h).astype(BF)
+    for block in blocks[1:]:
+        for copy in block:
+            copy.start()
+    sp_copy.start()
     copies[2].wait()
     inv = columns(lax.rsqrt(bdeg_ref[...].astype(F32)))
-    for copy in copies[3:]:
-        copy.wait()
-    for copy in bp_copies:
-        copy.start()
-    sp_copy.start()
+    copies[3].wait()
     outs = []
     for n, s in enumerate(range(0, NB, STEP)):
         at = slice(s, s + STEP)
-        half = 0.5 * inv[at]
-        half_sq = half * inv[at]
+        blocks[n][0].wait()
+        blocks[n][1].wait()
         h = h_ref[:, at]
         u1 = (cf_ref[at, :] + dot_tl(h, mix_ref[:, 512:640])).astype(BF)
-        z = dot(u1, w1_ref[...])
-        zh = scale_rows(z, half)
+        zh = 0.5 * dot(u1, w1_ref[...])
         t = jnp.tanh(zh)
-        w = scale_rows(1.0 + t, half_sq)
-        hid_ref[at, :] = (z * w).astype(BF)
-        outs.append(pltpu.make_async_copy(hid_ref.at[at], hid_hbm.at[at], sems.at[11 + n]))
+        hid_ref[at, :] = (zh * scale_rows(1.0 + t, inv[at])).astype(BF)
+        outs.append(pltpu.make_async_copy(hid_ref.at[at], hid_hbm.at[at], sems.at[17 + n]))
         outs[-1].start()
-        bp_copies[n].wait()
-        d_pre = ((bp_ref[at, :] + dot_tl(h, mix_ref[:, 0:512])) * (w * (1.0 + zh * (1.0 - t)))).astype(BF)
+        slope = (0.5 + 0.5 * t) * (1.0 + zh * (1.0 - t))
+        blocks[n][2].wait()
+        d_pre = ((bp_ref[at, :] + dot_tl(h, mix_ref[:, 0:512])) * slope).astype(BF)
         g1 = dot_tl(u1, d_pre)
         if n == 0:
             g1_ref[...] = g1
@@ -337,7 +333,7 @@
             pltpu.VMEM((NH, HID + FEAT), BF),
             pltpu.VMEM((FEAT, HID), F32),
             pltpu.VMEM((HID, HID), F32),
-            pltpu.SemaphoreType.DMA((15,)),
+            pltpu.SemaphoreType.DMA((21,)),
         ],
         compiler_params=limit(58),
         name="main_part",
@@ -363,8 +359,9 @@
     for n, s in enumerate(range(0, NB // 2, STEP)):
         here = slice(s, s + STEP)
         there = slice(at.start + s, at.start + s + STEP)
-        u = dot_tl(c_ref[:, here], hid_ref[...]) + dot_tl(h_ref[:, here], he_ref[...])
-        out_ref[here] = scale_rows(dot(u.astype(BF), w2_ref[...]), inv[here]).astype(BF)
+        own = scale_rows(dot_tl(c_ref[:, here], hid_ref[...]), inv[here])
+        u = (own + dot_tl(h_ref[:, here], he_ref[...])).astype(BF)
+        out_ref[here] = dot(u, w2_ref[...]).astype(BF)
         outs.append(pltpu.make_async_copy(out_ref.at[here], out_hbm.at[there], sems.at[2 + n]))
         outs[-1].start()
     for copy in outs:
@@ -467,10 +464,10 @@
     bdeg = batch_deg.reshape(1, NB)
     hdeg = halo_deg.reshape(1, NH)
     asked = exchange(halo_rows.reshape(128, 1, 4))
-    h, gs, p = halo_call(halo_nbrs.T, halo_len.reshape(1, NB), bdeg, hdeg, grad_out)
+    h, p = halo_call(halo_nbrs.T, halo_len.reshape(1, NB), bdeg, hdeg, grad_out)
     send = pick_call(asked, feat_table, emb_table, grad_table, p)
     recv = exchange(send)
-    c, cf, sp, bp = batch_call(batch_nbrs.T, bdeg, node_feats, gs, weight_two)
+    c, cf, sp, bp = batch_call(batch_nbrs.T, bdeg, node_feats, grad_out, weight_two)
     hid, grads = main_call(recv, h, cf, sp, bp, p, weight_one, weight_two, bdeg, hdeg)
     shares = exchange(grads)
     half = out_call(0, recv, c, h, hid, weight_two, bdeg, hdeg)

time: 113 us -> 113 us (level)
  waiting for transfers between devices: 18.7 us -> 20.7 us
  Pallas kernels: 65 us -> 63.4 us
  starting transfers between devices: 27 us -> 25.5 us
    all_to_all x4, waiting for transfers between devices: 18.7 us -> 20.7 us  [exchange(): return lax.all_to_all(x, AXES, split_axis=0, concat_axis=0, tiled=True)]
    all_to_all x4, starting transfers between devices: 27 us -> 25.5 us  [exchange(): return lax.all_to_all(x, AXES, split_axis=0, concat_axis=0, tiled=True)]
    pallas_call x1, Pallas kernels: 5.35 us -> 4.05 us  [halo_call(): pl.pallas_call(halo_kernel, in_specs=[vmem_spec()] * 4 + [hbm_spec()], ou...]
  transfers between devices with their start and end apart: 4 -> 4, of which waited for: 4 -> 4; matrix products, arithmetic and copies ran while one was open for 0% -> 0% of each run, Pallas kernels for 41% -> 39%
where the time goes in v6:
time: 113 us; the launch traced here: 112 us
  Pallas kernels  63.4 us (56%)
  starting transfers between devices  25.5 us (23%)
  waiting for transfers between devices  20.7 us (18%)
  local copies, waits for them, and re-layouts  1.57 us (1%)
    all_to_all x4, starting transfers between devices, exchange(): return lax.all_to_all(x, AXES, split_axis=0, concat_axis=0, tiled=True)  25.5 us
    all_to_all x4, waiting for transfers between devices, exchange(): return lax.all_to_all(x, AXES, split_axis=0, concat_axis=0, tiled=True)  20.7 us
    pallas_call x1, Pallas kernels, batch_call(): pl.pallas_call(batch_kernel, in_specs=[vmem_spec()] * 3 + [hbm_spec(), vm...  20.3 us
    pallas_call x2, Pallas kernels, out_call(): pl.pallas_call(lambda *refs: out_kernel(half, refs), in_specs=[vmem_spec(...  17.1 us
    pallas_call x1, Pallas kernels, main_call(): pl.pallas_call(main_kernel, in_specs=[vmem_spec()] + [hbm_spec()] * 4 + [...  10.2 us
    pallas_call x1, Pallas kernels, pick_call(): pl.pallas_call(pick_kernel, in_specs=[vmem_spec(), hbm_spec(), vmem_spec(...  6.89 us
    pallas_call x1, Pallas kernels, halo_call(): pl.pallas_call(halo_kernel, in_specs=[vmem_spec()] * 4 + [hbm_spec()], ou...  4.05 us
    pallas_call x1, Pallas kernels, tail_call(): pl.pallas_call(tail_kernel, in_specs=[vmem_spec()] * 2, out_specs=hbm_spe...  2.48 us
  transfers between devices with their start and end apart: 4, of which 4 were waited for; matrix products, arithmetic and copies ran while one was open for 0% of the time, Pallas kernels for 39%

profile of v6, /device:TPU:1, one launch (start us, length us, event | category | flops | bytes accessed | tf_op | source)
XLA Modules:
  0.0 112.0 jit_solution(16147866962385473028)
XLA Ops:
  0.6 0.0 copy-start
  0.6 1.6 %reshape.20 = s32[128,1,4]{2,0,1:T(8,128)} reshape(s32[512]{0:T(512)} %param.18) | data formatting | bytes 4096 | tf_op jit(solution)/shard_map/reshape | solution.py:466
  2.2 11.5 %all-to-all-start = ((s32[128,1,4]{2,1,0:T(1,128)}), s32[128,1,4]{2,1,0:T(1,128)S(1)}, u32[]{:S(2)}, u32[]{:S(2)}) async-start(s32[128,1,4]{2,1,0:T(1,128)} %bitcast), calls=%async_computation | async-start | bytes 131072 | tf_op jit(solution)/shard_map/all_to_all | solution.py:457
  13.7 4.1 %halo_part.1 = (bf16[512,2048]{1,0:T(8,128)(2,1)}, bf16[512,512]{1,0:T(8,128)(2,1)S(1)}) custom-call(s32[8,2048]{1,0:T(8,128)} %bitcast.11, s32[1,2048]{1,0:T(1,128)} %bitcast.17, s32[1,2048]{1,0:T(1,128)} %bitcast.6, s32[1,512]{1,0:T(1,128)} %bitcast.13, bf16[2048,512]{1,0:T(8,128)(2,1)} %g_hbm.3), custom_call_target="tpu_custom_call" | custom-call | tf_op jit(solution)/shard_map/halo_part/pallas_call | solution.py:110
  17.8 5.5 %all-to-all-done.ask_ref = s32[128,1,4]{2,1,0:T(1,128)S(1)} async-done(((s32[128,1,4]{2,1,0:T(1,128)}), s32[128,1,4]{2,1,0:T(1,128)S(1)}, u32[]{:S(2)}, u32[]{:S(2)}) %all-to-all-start) | async-done | bytes 2080 | tf_op jit(solution)/shard_map/all_to_all | solution.py:457
  23.2 0.0 copy-done
  23.2 6.9 %pick_rows.1 = bf16[128,4,1664]{2,1,0:T(4,128)(2,1)} custom-call(s32[128,1,4]{2,1,0:T(1,128)S(1)} %all-to-all-done.ask_ref, bf16[2048,128]{1,0:T(8,128)(2,1)} %x_hbm.1, bf16[2048,512]{1,0:T(8,128)(2,1)S(1)} %copy-done, bf16[2048,512]{1,0:T(8,128)(2,1)} %v_hbm.1, bf16[512,512]{1,0:T(8,128)(2,1)S(1)} %get-tuple-element.16.p_ref), custom_call_target="tpu_custom_call" | custom-call | tf_op jit(solution)/shard_map/pick_rows/pallas_call | solution.py:177
  30.1 4.5 %all-to-all-start.1 = ((bf16[128,4,1664]{2,1,0:T(4,128)(2,1)}), bf16[128,4,1664]{2,1,0:T(4,128)(2,1)S(1)}, u32[]{:S(2)}, u32[]{:S(2)}) async-start(bf16[128,4,1664]{2,1,0:T(4,128)(2,1)} %pick_rows.1), calls=%async_computation.1 | async-start | bytes 3407872 | tf_op jit(solution)/shard_map/all_to_all | solution.py:457
  34.6 20.3 %batch_part.1 = (bf16[2048,2048]{1,0:T(8,128)(2,1)}, f32[2048,128]{1,0:T(8,128)}, bf16[2048,512]{1,0:T(8,128)(2,1)}, f32[2048,512]{1,0:T(8,128)}) custom-call(s32[8,2048]{1,0:T(8,128)} %bitcast.12, s32[1,2048]{1,0:T(1,128)} %bitcast.7, bf16[2048,128]{1,0:T(8,128)(2,1)} %f_ref.1, bf16[2048,512]{1,0:T(8,128)(2,1)} %g_hbm.3, bf16[512,512]{1,0:T(8,128)(2,1)} %refs_4_.3), custom_call_target="tpu_custom_call" | custom-call | tf_op jit(solution)/shard_map/batch_part/pallas_call | solution.py:229
  55.0 5.3 %all-to-all-done.1.r_ref.refs_0_ = bf16[128,4,1664]{2,1,0:T(4,128)(2,1)S(1)} async-done(((bf16[128,4,1664]{2,1,0:T(4,128)(2,1)}), bf16[128,4,1664]{2,1,0:T(4,128)(2,1)S(1)}, u32[]{:S(2)}, u32[]{:S(2)}) %all-to-all-start.1) | async-done | bytes 1703968 | tf_op jit(solution)/shard_map/all_to_all | solution.py:457
  60.2 10.2 %main_part.1 = (bf16[2048,512]{1,0:T(8,128)(2,1)}, bf16[128,4,640]{2,1,0:T(4,128)(2,1)}) custom-call(bf16[128,4,1664]{2,1,0:T(4,128)(2,1)S(1)} %all-to-all-done.1.r_ref.refs_0_, bf16[512,2048]{1,0:T(8,128)(2,1)} %get-tuple-element.18.h_hbm.refs_2_, f32[2048,128]{1,0:T(8,128)} %get-tuple-element.19.cf_hbm, bf16[2048,512]{1,0:T(8,128)(2,1)} %get-tuple-element.20.sp_hbm, ...), custom_call_target="tpu_custom_call" | custom-call | tf_op jit(solution)/shard_map/main_part/pallas_call | solution.py:318
  70.4 4.8 %all-to-all-start.2 = ((bf16[128,4,640]{2,1,0:T(4,128)(2,1)}), bf16[128,4,640]{2,1,0:T(4,128)(2,1)S(1)}, u32[]{:S(2)}, u32[]{:S(2)}) async-start(bf16[128,4,640]{2,1,0:T(4,128)(2,1)} %get-tuple-element.23), calls=%async_computation.2 | async-start | bytes 1310720 | tf_op jit(solution)/shard_map/all_to_all | solution.py:457
  75.2 8.5 %out_part_0.1.refs_7_ = bf16[2048,512]{1,0:T(8,128)(2,1)} custom-call(bf16[128,4,1664]{2,1,0:T(4,128)(2,1)S(1)} %all-to-all-done.1.r_ref.refs_0_, bf16[2048,2048]{1,0:T(8,128)(2,1)} %get-tuple-element.17.refs_1_, bf16[512,2048]{1,0:T(8,128)(2,1)} %get-tuple-element.18.h_hbm.refs_2_, bf16[2048,512]{1,0:T(8,128)(2,1)} %get-tuple-element.22.refs_3_, ...), custom_call_target="tpu_custom_call" | custom-call | tf_op jit(solution)/shard_map/out_part_0/pallas_call | solution.py:372
  83.8 6.2 %all-to-all-done.2.x_ref = bf16[128,4,640]{2,1,0:T(4,128)(2,1)S(1)} async-done(((bf16[128,4,640]{2,1,0:T(4,128)(2,1)}), bf16[128,4,640]{2,1,0:T(4,128)(2,1)S(1)}, u32[]{:S(2)}, u32[]{:S(2)}) %all-to-all-start.2) | async-done | bytes 655392 | tf_op jit(solution)/shard_map/all_to_all | solution.py:457
  90.0 1.3 %sum_part.1 = bf16[128,4,640]{2,1,0:T(4,128)(2,1)} custom-call(bf16[128,4,640]{2,1,0:T(4,128)(2,1)S(1)} %all-to-all-done.2.x_ref), custom_call_target="tpu_custom_call" | custom-call | tf_op jit(solution)/shard_map/sum_part/pallas_call | solution.py:426
  91.3 4.8 %all-to-all-start.3 = ((bf16[128,4,640]{2,1,0:T(4,128)(2,1)}), bf16[128,4,640]{2,1,0:T(4,128)(2,1)S(1)}, u32[]{:S(2)}, u32[]{:S(2)}) async-start(bf16[128,4,640]{2,1,0:T(4,128)(2,1)} %sum_part.1), calls=%async_computation.3 | async-start | bytes 1310720 | tf_op jit(solution)/shard_map/all_to_all | solution.py:457
  96.0 2.5 %tail_part.1 = bf16[2048,512]{1,0:T(8,128)(2,1)} custom-call(s32[128,1,4]{2,1,0:T(1,128)S(1)} %all-to-all-done.ask_ref, bf16[128,4,1664]{2,1,0:T(4,128)(2,1)S(1)} %all-to-all-done.1.r_ref.refs_0_), custom_call_target="tpu_custom_call" | custom-call | tf_op jit(solution)/shard_map/tail_part/pallas_call | solution.py:404
  98.5 8.6 %out_part_1.1 = bf16[2048,512]{1,0:T(8,128)(2,1)} custom-call(bf16[128,4,1664]{2,1,0:T(4,128)(2,1)S(1)} %all-to-all-done.1.r_ref.refs_0_, bf16[2048,2048]{1,0:T(8,128)(2,1)} %get-tuple-element.17.refs_1_, bf16[512,2048]{1,0:T(8,128)(2,1)} %get-tuple-element.18.h_hbm.refs_2_, ...), custom_call_target="tpu_custom_call", output_to_operand_aliasing={{}: (7, {})} | custom-call | tf_op jit(solution)/shard_map/out_part_1/pallas_call | solution.py:372
  107.1 3.8 %all-to-all-done.3.x_ref = bf16[128,4,640]{2,1,0:T(4,128)(2,1)S(1)} async-done(((bf16[128,4,640]{2,1,0:T(4,128)(2,1)}), bf16[128,4,640]{2,1,0:T(4,128)(2,1)S(1)}, u32[]{:S(2)}, u32[]{:S(2)}) %all-to-all-start.3) | async-done | bytes 655392 | tf_op jit(solution)/shard_map/all_to_all | solution.py:457
  110.8 1.2 %final_part.1 = (f32[128,512]{1,0:T(8,128)}, f32[512,512]{1,0:T(8,128)}) custom-call(bf16[128,4,640]{2,1,0:T(4,128)(2,1)S(1)} %all-to-all-done.3.x_ref), custom_call_target="tpu_custom_call" | custom-call | tf_op jit(solution)/shard_map/final_part/pallas_call | solution.py:444
Async XLA Ops:
  0.6 22.6 %copy-start = (bf16[2048,512]{1,0:T(8,128)(2,1)S(1)}, bf16[2048,512]{1,0:T(8,128)(2,1)}, u32[]{:S(2)}) copy-start(bf16[2048,512]{1,0:T(8,128)(2,1)} %e_ref.1) | copy-start | bytes 6291460
  2.2 21.0 %all-to-all-start = ((s32[128,1,4]{2,1,0:T(1,128)}), s32[128,1,4]{2,1,0:T(1,128)S(1)}, u32[]{:S(2)}, u32[]{:S(2)}) async-start(s32[128,1,4]{2,1,0:T(1,128)} %bitcast), calls=%async_computation | async-start | bytes 131072 | tf_op jit(solution)/shard_map/all_to_all | solution.py:457
  30.1 30.1 %all-to-all-start.1 = ((bf16[128,4,1664]{2,1,0:T(4,128)(2,1)}), bf16[128,4,1664]{2,1,0:T(4,128)(2,1)S(1)}, u32[]{:S(2)}, u32[]{:S(2)}) async-start(bf16[128,4,1664]{2,1,0:T(4,128)(2,1)} %pick_rows.1), calls=%async_computation.1 | async-start | bytes 3407872 | tf_op jit(solution)/shard_map/all_to_all | solution.py:457
  70.4 19.6 %all-to-all-start.2 = ((bf16[128,4,640]{2,1,0:T(4,128)(2,1)}), bf16[128,4,640]{2,1,0:T(4,128)(2,1)S(1)}, u32[]{:S(2)}, u32[]{:S(2)}) async-start(bf16[128,4,640]{2,1,0:T(4,128)(2,1)} %get-tuple-element.23), calls=%async_computation.2 | async-start | bytes 1310720 | tf_op jit(solution)/shard_map/all_to_all | solution.py:457
  91.3 19.6 %all-to-all-start.3 = ((bf16[128,4,640]{2,1,0:T(4,128)(2,1)}), bf16[128,4,640]{2,1,0:T(4,128)(2,1)S(1)}, u32[]{:S(2)}, u32[]{:S(2)}) async-start(bf16[128,4,640]{2,1,0:T(4,128)(2,1)} %sum_part.1), calls=%async_computation.3 | async-start | bytes 1310720 | tf_op jit(solution)/shard_map/all_to_all | solution.py:457

commit v7 on v6

--- a/solution.py
+++ b/solution.py
@@ -154,23 +154,16 @@
     ]
     for copy in copies:
         copy.start()
-    def send(lo, hi, n):
-        at = (slice(None), slice(None), slice(lo, hi))
-        sends.append(pltpu.make_async_copy(out_ref.at[at], out_hbm.at[at], sems.at[n]))
-        sends[-1].start()
-
-    sends = []
     out_ref[:, :, 1152:1664] = chunks_of(p_ref[...])
-    send(1152, 1664, 3)
     selector(ask_ref, s_ref)
     s = s_ref[...]
     for n, (lo, hi, src) in enumerate(((128, 640, e_ref), (640, 1152, v_ref), (0, 128, x_ref))):
         if n:
             copies[n - 1].wait()
         out_ref[:, :, lo:hi] = chunks_of(dot(s, src[...]))
-        send(lo, hi, 4 + n)
-    for copy in sends:
-        copy.wait()
+    send = pltpu.make_async_copy(out_ref, out_hbm, sems.at[2])
+    send.start()
+    send.wait()
 
 
 def pick_call(asked, x, e, v, p):
@@ -184,7 +177,7 @@
             pltpu.VMEM((NB, FEAT), BF),
             pltpu.VMEM((NB, HID), BF),
             pltpu.VMEM((128, 4, 1664), BF),
-            pltpu.SemaphoreType.DMA((7,)),
+            pltpu.SemaphoreType.DMA((3,)),
         ],
         compiler_params=limit(58),
         name="pick_rows",

time: 113 us -> 113 us (level)
  no operation moved by 1% of the time
where the time goes in v7:
time: 113 us; the launch traced here: 112 us
  Pallas kernels  63.5 us (56%)
  starting transfers between devices  25.5 us (23%)
  waiting for transfers between devices  20.7 us (18%)
  local copies, waits for them, and re-layouts  1.57 us (1%)
    all_to_all x4, starting transfers between devices, exchange(): return lax.all_to_all(x, AXES, split_axis=0, concat_axis=0, tiled=True)  25.5 us
    all_to_all x4, waiting for transfers between devices, exchange(): return lax.all_to_all(x, AXES, split_axis=0, concat_axis=0, tiled=True)  20.7 us
    pallas_call x1, Pallas kernels, batch_call(): pl.pallas_call(batch_kernel, in_specs=[vmem_spec()] * 3 + [hbm_spec(), vm...  20.3 us
    pallas_call x2, Pallas kernels, out_call(): pl.pallas_call(lambda *refs: out_kernel(half, refs), in_specs=[vmem_spec(...  17.1 us
    pallas_call x1, Pallas kernels, main_call(): pl.pallas_call(main_kernel, in_specs=[vmem_spec()] + [hbm_spec()] * 4 + [...  10.2 us
    pallas_call x1, Pallas kernels, pick_call(): pl.pallas_call(pick_kernel, in_specs=[vmem_spec(), hbm_spec(), vmem_spec(...  7.01 us
    pallas_call x1, Pallas kernels, halo_call(): pl.pallas_call(halo_kernel, in_specs=[vmem_spec()] * 4 + [hbm_spec()], ou...  4.05 us
    pallas_call x1, Pallas kernels, tail_call(): pl.pallas_call(tail_kernel, in_specs=[vmem_spec()] * 2, out_specs=hbm_spe...  2.48 us
  transfers between devices with their start and end apart: 4, of which 4 were waited for; matrix products, arithmetic and copies ran while one was open for 0% of the time, Pallas kernels for 39%

profile of v7, /device:TPU:1, one launch (start us, length us, event | category | flops | bytes accessed | tf_op | source)
XLA Modules:
  0.0 112.1 jit_solution(4786355499696485311)
XLA Ops:
  0.6 0.0 copy-start
  0.6 1.6 %reshape.20 = s32[128,1,4]{2,0,1:T(8,128)} reshape(s32[512]{0:T(512)} %param.18) | data formatting | bytes 4096 | tf_op jit(solution)/shard_map/reshape | solution.py:459
  2.2 11.5 %all-to-all-start = ((s32[128,1,4]{2,1,0:T(1,128)}), s32[128,1,4]{2,1,0:T(1,128)S(1)}, u32[]{:S(2)}, u32[]{:S(2)}) async-start(s32[128,1,4]{2,1,0:T(1,128)} %bitcast), calls=%async_computation | async-start | bytes 131072 | tf_op jit(solution)/shard_map/all_to_all | solution.py:450
  13.7 4.1 %halo_part.1 = (bf16[512,2048]{1,0:T(8,128)(2,1)}, bf16[512,512]{1,0:T(8,128)(2,1)S(1)}) custom-call(s32[8,2048]{1,0:T(8,128)} %bitcast.11, s32[1,2048]{1,0:T(1,128)} %bitcast.17, s32[1,2048]{1,0:T(1,128)} %bitcast.6, s32[1,512]{1,0:T(1,128)} %bitcast.13, bf16[2048,512]{1,0:T(8,128)(2,1)} %g_hbm.3), custom_call_target="tpu_custom_call" | custom-call | tf_op jit(solution)/shard_map/halo_part/pallas_call | solution.py:110
  17.8 5.5 %all-to-all-done.ask_ref = s32[128,1,4]{2,1,0:T(1,128)S(1)} async-done(((s32[128,1,4]{2,1,0:T(1,128)}), s32[128,1,4]{2,1,0:T(1,128)S(1)}, u32[]{:S(2)}, u32[]{:S(2)}) %all-to-all-start) | async-done | bytes 2080 | tf_op jit(solution)/shard_map/all_to_all | solution.py:450
  23.2 0.0 copy-done
  23.2 7.0 %pick_rows.1 = bf16[128,4,1664]{2,1,0:T(4,128)(2,1)} custom-call(s32[128,1,4]{2,1,0:T(1,128)S(1)} %all-to-all-done.ask_ref, bf16[2048,128]{1,0:T(8,128)(2,1)} %x_hbm.1, bf16[2048,512]{1,0:T(8,128)(2,1)S(1)} %copy-done, bf16[2048,512]{1,0:T(8,128)(2,1)} %v_hbm.1, bf16[512,512]{1,0:T(8,128)(2,1)S(1)} %get-tuple-element.16.p_ref), custom_call_target="tpu_custom_call" | custom-call | tf_op jit(solution)/shard_map/pick_rows/pallas_call | solution.py:170
  30.2 4.5 %all-to-all-start.1 = ((bf16[128,4,1664]{2,1,0:T(4,128)(2,1)}), bf16[128,4,1664]{2,1,0:T(4,128)(2,1)S(1)}, u32[]{:S(2)}, u32[]{:S(2)}) async-start(bf16[128,4,1664]{2,1,0:T(4,128)(2,1)} %pick_rows.1), calls=%async_computation.1 | async-start | bytes 3407872 | tf_op jit(solution)/shard_map/all_to_all | solution.py:450
  34.7 20.3 %batch_part.1 = (bf16[2048,2048]{1,0:T(8,128)(2,1)}, f32[2048,128]{1,0:T(8,128)}, bf16[2048,512]{1,0:T(8,128)(2,1)}, f32[2048,512]{1,0:T(8,128)}) custom-call(s32[8,2048]{1,0:T(8,128)} %bitcast.12, s32[1,2048]{1,0:T(1,128)} %bitcast.7, bf16[2048,128]{1,0:T(8,128)(2,1)} %f_ref.1, bf16[2048,512]{1,0:T(8,128)(2,1)} %g_hbm.3, bf16[512,512]{1,0:T(8,128)(2,1)} %refs_4_.3), custom_call_target="tpu_custom_call" | custom-call | tf_op jit(solution)/shard_map/batch_part/pallas_call | solution.py:222
  55.1 5.3 %all-to-all-done.1.r_ref.refs_0_ = bf16[128,4,1664]{2,1,0:T(4,128)(2,1)S(1)} async-done(((bf16[128,4,1664]{2,1,0:T(4,128)(2,1)}), bf16[128,4,1664]{2,1,0:T(4,128)(2,1)S(1)}, u32[]{:S(2)}, u32[]{:S(2)}) %all-to-all-start.1) | async-done | bytes 1703968 | tf_op jit(solution)/shard_map/all_to_all | solution.py:450
  60.3 10.2 %main_part.1 = (bf16[2048,512]{1,0:T(8,128)(2,1)}, bf16[128,4,640]{2,1,0:T(4,128)(2,1)}) custom-call(bf16[128,4,1664]{2,1,0:T(4,128)(2,1)S(1)} %all-to-all-done.1.r_ref.refs_0_, bf16[512,2048]{1,0:T(8,128)(2,1)} %get-tuple-element.18.h_hbm.refs_2_, f32[2048,128]{1,0:T(8,128)} %get-tuple-element.19.cf_hbm, bf16[2048,512]{1,0:T(8,128)(2,1)} %get-tuple-element.20.sp_hbm, ...), custom_call_target="tpu_custom_call" | custom-call | tf_op jit(solution)/shard_map/main_part/pallas_call | solution.py:311
  70.5 4.8 %all-to-all-start.2 = ((bf16[128,4,640]{2,1,0:T(4,128)(2,1)}), bf16[128,4,640]{2,1,0:T(4,128)(2,1)S(1)}, u32[]{:S(2)}, u32[]{:S(2)}) async-start(bf16[128,4,640]{2,1,0:T(4,128)(2,1)} %get-tuple-element.23), calls=%async_computation.2 | async-start | bytes 1310720 | tf_op jit(solution)/shard_map/all_to_all | solution.py:450
  75.3 8.5 %out_part_0.1.refs_7_ = bf16[2048,512]{1,0:T(8,128)(2,1)} custom-call(bf16[128,4,1664]{2,1,0:T(4,128)(2,1)S(1)} %all-to-all-done.1.r_ref.refs_0_, bf16[2048,2048]{1,0:T(8,128)(2,1)} %get-tuple-element.17.refs_1_, bf16[512,2048]{1,0:T(8,128)(2,1)} %get-tuple-element.18.h_hbm.refs_2_, bf16[2048,512]{1,0:T(8,128)(2,1)} %get-tuple-element.22.refs_3_, ...), custom_call_target="tpu_custom_call" | custom-call | tf_op jit(solution)/shard_map/out_part_0/pallas_call | solution.py:365
  83.9 6.2 %all-to-all-done.2.x_ref = bf16[128,4,640]{2,1,0:T(4,128)(2,1)S(1)} async-done(((bf16[128,4,640]{2,1,0:T(4,128)(2,1)}), bf16[128,4,640]{2,1,0:T(4,128)(2,1)S(1)}, u32[]{:S(2)}, u32[]{:S(2)}) %all-to-all-start.2) | async-done | bytes 655392 | tf_op jit(solution)/shard_map/all_to_all | solution.py:450
  90.1 1.3 %sum_part.1 = bf16[128,4,640]{2,1,0:T(4,128)(2,1)} custom-call(bf16[128,4,640]{2,1,0:T(4,128)(2,1)S(1)} %all-to-all-done.2.x_ref), custom_call_target="tpu_custom_call" | custom-call | tf_op jit(solution)/shard_map/sum_part/pallas_call | solution.py:419
  91.4 4.8 %all-to-all-start.3 = ((bf16[128,4,640]{2,1,0:T(4,128)(2,1)}), bf16[128,4,640]{2,1,0:T(4,128)(2,1)S(1)}, u32[]{:S(2)}, u32[]{:S(2)}) async-start(bf16[128,4,640]{2,1,0:T(4,128)(2,1)} %sum_part.1), calls=%async_computation.3 | async-start | bytes 1310720 | tf_op jit(solution)/shard_map/all_to_all | solution.py:450
  96.2 2.5 %tail_part.1 = bf16[2048,512]{1,0:T(8,128)(2,1)} custom-call(s32[128,1,4]{2,1,0:T(1,128)S(1)} %all-to-all-done.ask_ref, bf16[128,4,1664]{2,1,0:T(4,128)(2,1)S(1)} %all-to-all-done.1.r_ref.refs_0_), custom_call_target="tpu_custom_call" | custom-call | tf_op jit(solution)/shard_map/tail_part/pallas_call | solution.py:397
  98.6 8.6 %out_part_1.1 = bf16[2048,512]{1,0:T(8,128)(2,1)} custom-call(bf16[128,4,1664]{2,1,0:T(4,128)(2,1)S(1)} %all-to-all-done.1.r_ref.refs_0_, bf16[2048,2048]{1,0:T(8,128)(2,1)} %get-tuple-element.17.refs_1_, bf16[512,2048]{1,0:T(8,128)(2,1)} %get-tuple-element.18.h_hbm.refs_2_, ...), custom_call_target="tpu_custom_call", output_to_operand_aliasing={{}: (7, {})} | custom-call | tf_op jit(solution)/shard_map/out_part_1/pallas_call | solution.py:365
  107.2 3.8 %all-to-all-done.3.x_ref = bf16[128,4,640]{2,1,0:T(4,128)(2,1)S(1)} async-done(((bf16[128,4,640]{2,1,0:T(4,128)(2,1)}), bf16[128,4,640]{2,1,0:T(4,128)(2,1)S(1)}, u32[]{:S(2)}, u32[]{:S(2)}) %all-to-all-start.3) | async-done | bytes 655392 | tf_op jit(solution)/shard_map/all_to_all | solution.py:450
  111.0 1.2 %final_part.1 = (f32[128,512]{1,0:T(8,128)}, f32[512,512]{1,0:T(8,128)}) custom-call(bf16[128,4,640]{2,1,0:T(4,128)(2,1)S(1)} %all-to-all-done.3.x_ref), custom_call_target="tpu_custom_call" | custom-call | tf_op jit(solution)/shard_map/final_part/pallas_call | solution.py:437
Async XLA Ops:
  0.6 22.6 %copy-start = (bf16[2048,512]{1,0:T(8,128)(2,1)S(1)}, bf16[2048,512]{1,0:T(8,128)(2,1)}, u32[]{:S(2)}) copy-start(bf16[2048,512]{1,0:T(8,128)(2,1)} %e_ref.1) | copy-start | bytes 6291460
  2.2 21.0 %all-to-all-start = ((s32[128,1,4]{2,1,0:T(1,128)}), s32[128,1,4]{2,1,0:T(1,128)S(1)}, u32[]{:S(2)}, u32[]{:S(2)}) async-start(s32[128,1,4]{2,1,0:T(1,128)} %bitcast), calls=%async_computation | async-start | bytes 131072 | tf_op jit(solution)/shard_map/all_to_all | solution.py:450
  30.2 30.1 %all-to-all-start.1 = ((bf16[128,4,1664]{2,1,0:T(4,128)(2,1)}), bf16[128,4,1664]{2,1,0:T(4,128)(2,1)S(1)}, u32[]{:S(2)}, u32[]{:S(2)}) async-start(bf16[128,4,1664]{2,1,0:T(4,128)(2,1)} %pick_rows.1), calls=%async_computation.1 | async-start | bytes 3407872 | tf_op jit(solution)/shard_map/all_to_all | solution.py:450
  70.5 19.6 %all-to-all-start.2 = ((bf16[128,4,640]{2,1,0:T(4,128)(2,1)}), bf16[128,4,640]{2,1,0:T(4,128)(2,1)S(1)}, u32[]{:S(2)}, u32[]{:S(2)}) async-start(bf16[128,4,640]{2,1,0:T(4,128)(2,1)} %get-tuple-element.23), calls=%async_computation.2 | async-start | bytes 1310720 | tf_op jit(solution)/shard_map/all_to_all | solution.py:450
  91.4 19.6 %all-to-all-start.3 = ((bf16[128,4,640]{2,1,0:T(4,128)(2,1)}), bf16[128,4,640]{2,1,0:T(4,128)(2,1)S(1)}, u32[]{:S(2)}, u32[]{:S(2)}) async-start(bf16[128,4,640]{2,1,0:T(4,128)(2,1)} %sum_part.1), calls=%async_computation.3 | async-start | bytes 1310720 | tf_op jit(solution)/shard_map/all_to_all | solution.py:450
